TPU v7x, 32 devices: a whole 2x2x4 slice. The times are simulated.
32 devices in a mesh: section: 8 (over z, y), tp: 4 (over x, core).
Axes of the slice: x: 2, y: 2, z: 4, core: 2. Of those that a mesh axis runs over, the one named last changes fastest.
Arguments:
- inputs: bfloat16 [8, 64, 4096], P('section', 'tp'), may hold values from -6 to 6
- hidden_grad: bfloat16 [8, 64, 14336], P('section', None, 'tp'), may hold values from -6 to 6
- top_grad: bfloat16 [64, 4096], P('tp'), may hold values from -6 to 6
- w_gate: bfloat16 [8, 96, 128, 128], P('section', 'tp'), may hold values from -0.5 to 0.5
- w_up: bfloat16 [8, 96, 128, 128], P('section', 'tp'), may hold values from -0.5 to 0.5
- block_pos: int32 [8, 96], P('section', 'tp'), may hold values from 0 to 895, as said below
- live_count: int32 [8, 4], P('section', 'tp'), may hold values from 6 to 24, as said below
Outputs:
- input_grad: bfloat16 [8, 64, 4096], P('section', 'tp')
- gate_wgrad: bfloat16 [8, 96, 128, 128], P('section', 'tp')
- up_wgrad: bfloat16 [8, 96, 128, 128], P('section', 'tp')
Inputs may be any that keep to these rules, and one draw needn't show every extreme that they name: `block_pos`: within one layer and shard the 24 positions are distinct; p // 28 is the row block and p % 28 the column block. `live_count`: the live slots of a shard are its first ones; in every layer one shard has all 24 slots live.
All inputs are finite; a program needn't handle non-finite values.
Results may differ from a plain program's by a relative error of at most 0.0085.
Values may be sent and summed in bfloat16 or wider, within the bound.
No kernel may reach another device: no remote copies, remote signals or barrier semaphores. Data moves between devices by JAX's collectives and lax.ppermute only.
A program may use at most 64 MiB of HBM per device.

v0:
```python
import jax
import jax.numpy as jnp
from jax import lax
from jax.sharding import PartitionSpec as P


def carried_in(array, axis, join, neutral):
    count = lax.axis_size(axis)
    place = lax.axis_index(axis)
    ahead = count - 1 - place
    gathered = lax.all_gather(array.astype(jnp.bfloat16), axis)
    state = jnp.zeros_like(array) + jnp.asarray(neutral, array.dtype)

    def one(hop, state):
        source = count - 1 - hop
        return join(state, lax.dynamic_index_in_dim(gathered, source, 0, False).astype(array.dtype))

    return lax.fori_loop(0, ahead, one, state)


def local(inputs, hidden_grad, top_grad, w_gate, w_up, block_pos, live_count):
    single_float = jnp.float32
    highest_precision = lax.Precision.HIGHEST
    own_rows = inputs[0]
    grad_hidden = hidden_grad[0]
    gate_weight_blocks = w_gate[0]
    up_weight_blocks = w_up[0]
    block_positions = gate_weight_blocks.shape[0]
    blk = gate_weight_blocks.shape[1]
    width = own_rows.shape[1]
    shard_cols = grad_hidden.shape[1]
    col_blocks = shard_cols // blk
    row_block_index = width // blk
    position = block_pos[0]
    block_count = live_count[0, 0]
    row_lookup = position // col_blocks
    column_lookup = position % col_blocks
    block_active_mask = (lax.iota(jnp.int32, block_positions) < block_count).astype(single_float)
    col_iota = lax.iota(jnp.int32, col_blocks)
    row_iota = lax.iota(jnp.int32, row_block_index)

    def over_slots(work, init):
        return jax.tree.map(jnp.add, init, work(0, block_positions))

    def slot_range():
        return (row_lookup, column_lookup, block_active_mask, gate_weight_blocks, up_weight_blocks)

    piece = lax.all_gather(own_rows, "tp", axis=0, tiled=True)
    gate_gradient = jnp.zeros((block_positions, blk, blk), single_float)
    up_gradient = jnp.zeros((block_positions, blk, blk), single_float)
    count_rows = piece.shape[0]
    split = piece.reshape(count_rows, row_block_index, blk)

    def project(first, number):
        rows_idx, cols_idx, live, gate_part, up_part = slot_range()
        picked = jnp.take(split, rows_idx, axis=1)
        select = (cols_idx[:, None] == col_iota[None, :]).astype(single_float) * live[:, None]
        pre_gate = jnp.einsum(
            "rkd,kdn->krn", picked, gate_part, preferred_element_type=single_float
        )
        pre_up = jnp.einsum("rkd,kdn->krn", picked, up_part, preferred_element_type=single_float)
        return (
            jnp.einsum("kc,krn->rcn", select, pre_gate, precision=highest_precision),
            jnp.einsum("kc,krn->rcn", select, pre_up, precision=highest_precision),
        )

    zero = jnp.zeros((count_rows, col_blocks, blk), single_float)
    gate, up = over_slots(project, (zero, zero))
    gate = gate.reshape(count_rows, shard_cols)
    up = up.reshape(count_rows, shard_cols)
    upstream = grad_hidden.astype(single_float)
    sig = jax.nn.sigmoid(gate)
    dgate = (upstream * up * sig * (1.0 + gate * (1.0 - sig))).astype(jnp.bfloat16)
    dup = (upstream * gate * sig).astype(jnp.bfloat16)
    dgate_split = dgate.reshape(count_rows, col_blocks, blk)
    dup_split = dup.reshape(count_rows, col_blocks, blk)

    def outer(first, number):
        rows_idx, cols_idx, live, gate_part, up_part = slot_range()
        picked = jnp.take(split, rows_idx, axis=1)
        gate_term = (
            jnp.einsum(
                "vof,vow->ofw",
                picked,
                jnp.take(dgate_split, cols_idx, axis=1),
                preferred_element_type=single_float,
            )
            * live[:, None, None]
        )
        up_term = (
            jnp.einsum(
                "vof,vow->ofw",
                picked,
                jnp.take(dup_split, cols_idx, axis=1),
                preferred_element_type=single_float,
            )
            * live[:, None, None]
        )
        return (gate_term, up_term)

    gate_gradient, up_gradient = over_slots(outer, (gate_gradient, up_gradient))
    dgate_all, dup_all, gate_gradient, up_gradient = (dgate, dup, gate_gradient, up_gradient)
    count_rows = own_rows.shape[0] * lax.axis_size("tp")
    dgate_rows = dgate_all.reshape(count_rows, col_blocks, blk)
    dup_rows = dup_all.reshape(count_rows, col_blocks, blk)

    def back(first, number):
        rows_idx, cols_idx, live, gate_part, up_part = slot_range()
        back_rows = jnp.einsum(
            "rkn,kdn->krd",
            jnp.take(dgate_rows, cols_idx, axis=1),
            gate_part,
            preferred_element_type=single_float,
        )
        back_rows = back_rows + jnp.einsum(
            "rkn,kdn->krd",
            jnp.take(dup_rows, cols_idx, axis=1),
            up_part,
            preferred_element_type=single_float,
        )
        select = (rows_idx[:, None] == row_iota[None, :]).astype(single_float) * live[:, None]
        return jnp.einsum("kb,krd->rbd", select, back_rows, precision=highest_precision)

    zero = jnp.zeros((count_rows, row_block_index, blk), single_float)
    own_term = lax.psum_scatter(
        over_slots(back, zero).reshape(count_rows, width).astype(jnp.bfloat16),
        "tp",
        scatter_dimension=0,
        tiled=True,
    ).astype(jnp.float32)
    top_rows = top_grad.astype(single_float)
    later = carried_in(
        own_term, "section", lambda earlier, after: earlier + after, jnp.zeros_like(own_term)
    )
    total = top_rows + own_term + later
    input_grad = total.astype(jnp.bfloat16)[None]
    return (
        input_grad,
        gate_gradient.astype(jnp.bfloat16)[None],
        up_gradient.astype(jnp.bfloat16)[None],
    )


def solution(mesh):
    in_specs = (
        P("section", "tp", None),
        P("section", None, "tp"),
        P("tp", None),
        P("section", "tp", None, None),
        P("section", "tp", None, None),
        P("section", "tp"),
        P("section", "tp"),
    )
    out_specs = (
        P("section", "tp", None),
        P("section", "tp", None, None),
        P("section", "tp", None, None),
    )
    return jax.shard_map(local, mesh=mesh, in_specs=in_specs, out_specs=out_specs, check_vma=False)
```

profile of v0, /device:TPU:0, one launch (start us, length us, event | category | flops | bytes accessed | tf_op | source)
XLA Modules:
  0.0 109.1 jit_solution(16907632383848354868)
XLA Ops:
  7.2 0.7 compare_and_fusion
  8.0 8.8 %all-gather = bf16[1,64,4096]{2,1,0:T(8,128)(2,1)S(1)} all-gather(bf16[1,16,4096]{2,1,0:T(8,128)(2,1)} %param.13), channel_id=2, replica_groups=mesh['section'=8,'tp'=4] {'tp'}, dimensions={1}, use_global_device_ids=true | all-gather | bytes 655360 | tf_op jit(solution)/shard_map/all_gather | solution.py:48
  18.1 0.6 gather_fusion
  19.1 0.7 copy-done.1
  20.2 1.7 %multiply_convert_fusion.2 = (bf16[64,28,128]{2,1,0:T(8,128)(2,1)S(1)}, f32[64,28,128]{2,1,0:T(8,128)S(1)}) fusion(f32[64,28,128]{2,1,0:T(8,128)S(1)} %reshape.77, f32[24]{0:T(128)S(1)} %compare_convert_fusion, s32[24]{0:T(128)S(1)} %get-tuple-element.71, f32[24,64,128]{2,1,0:T(8,128)S(1)} %fusion.8), kind=kOutput, calls=%fused_computation.16 | convolution fusion | flops 67437888 | bytes 3080384 | tf_op jit(solution)/shard_map/kc,krn->rcn/dot_general | solution.py:63
  21.9 1.9 %fusion.3 = bf16[64,28,128]{2,1,0:T(8,128)(2,1)S(1)} fusion(f32[64,28,128]{2,1,0:T(8,128)S(1)} %reshape.77, f32[64,28,128]{2,1,0:T(8,128)S(1)} %get-tuple-element.77, f32[24,64,128]{2,1,0:T(8,128)S(1)} %fusion.11, f32[24]{0:T(128)S(1)} %compare_convert_fusion, s32[24]{0:T(128)S(1)} %get-tuple-element.71), kind=kOutput, calls=%fused_computation.12 | convolution fusion | flops 68355392 | bytes 3080384 | tf_op jit(solution)/shard_map/kc,krn->rcn/dot_general | solution.py:64
  24.2 0.6 gather_fusion.1
  25.4 0.7 fusion.6
  26.1 0.7 convolution_add_fusion
  26.8 1.5 %convolution_convert_fusion = bf16[64,128,32]{1,2,0:T(8,128)(2,1)S(1)} fusion(f32[24,64,128]{2,1,0:T(8,128)S(1)} %convolution_add_fusion, f32[24]{0:T(128)S(1)} %compare_convert_fusion, s32[24]{0:T(128)S(1)} %get-tuple-element.75), kind=kOutput, calls=%fused_computation.11 | convolution fusion | flops 75761152 | bytes 1310912 | tf_op jit(solution)/shard_map/kb,krd->rbd/dot_general | solution.py:122
  28.3 1.0 copy.31
  29.4 22.6 %reduce-scatter.2.cloned.1.call-done = bf16[16,4096]{1,0:T(8,128)(2,1)} async-done(((bf16[64,4096]{1,0:T(8,128)(2,1)}), bf16[16,4096]{1,0:T(8,128)(2,1)}) %reduce-scatter.2.cloned.1.call-update) | async-done | bytes 131088 | tf_op jit(solution)/shard_map/reduce_scatter | solution.py:125
  52.1 1.4 %fusion.4 = bf16[1,24,128,128]{3,2,1,0:T(8,128)(2,1)} fusion(f32[24]{0:T(128)S(1)} %compare_convert_fusion, bf16[24,64,128]{2,1,0:T(8,128)(2,1)S(1)} %gather_fusion.1, pred[24]{0:T(512)(128)(4,1)S(1)} %get-tuple-element.70, bf16[24,64,128]{2,1,0:T(8,128)(2,1)S(1)} %gather_fusion, pred[24]{0:T(512)(128)(4,1)S(1)} %get-tuple-element.74), kind=kOutput, calls=%fused_computation.13 | convolution fusion | flops 51511296 | bytes 1573008 | tf_op jit(solution)/shard_map/vof,vow->ofw/dot_general | solution.py:82
  53.5 1.4 %fusion.5 = bf16[1,24,128,128]{3,2,1,0:T(8,128)(2,1)} fusion(f32[24]{0:T(128)S(1)} %compare_convert_fusion, bf16[24,64,128]{2,1,0:T(8,128)(2,1)S(1)} %gather_fusion.2, pred[24]{0:T(512)(128)(4,1)S(1)} %get-tuple-element.70, bf16[24,64,128]{2,1,0:T(8,128)(2,1)S(1)} %gather_fusion, pred[24]{0:T(512)(128)(4,1)S(1)} %get-tuple-element.74), kind=kOutput, calls=%fused_computation.14 | convolution fusion | flops 51511296 | bytes 1573008 | tf_op jit(solution)/shard_map/vof,vow->ofw/dot_general | solution.py:91
  54.8 39.7 %all-gather.4.cloned.1.call-done = bf16[128,4096]{1,0:T(8,128)(2,1)} async-done(((bf16[16,4096]{1,0:T(8,128)(2,1)}), bf16[128,4096]{1,0:T(8,128)(2,1)}) %all-gather.4.cloned.1.call-update) | async-done | bytes 1048592 | tf_op jit(solution)/shard_map/all_gather | solution.py:11
  94.6 6.9 %while.12 = (s32[]{:T(128)}, f32[16,4096]{1,0:T(8,128)S(1)}, s32[]{:T(128)}, bf16[8,16,4096]{2,1,0:T(8,128)(2,1)}, s32[]{:T(128)}, /*index=5*/s32[]{:T(128)}, s32[]{:T(128)}, s32[]{:T(128)}) while((s32[]{:T(128)}, f32[16,4096]{1,0:T(8,128)S(1)}, s32[]{:T(128)}, bf16[8,16,4096]{2,1,0:T(8,128)(2,1)}, s32[]{:T(128)}, /*index=5*/s32[]{:T(128)}, ...), condition=%wide.region_2.5_spmd, body=%wide.region_1.4_spmd.sunk | while | flops 131078 | bytes 655495 | solution.py:18
  94.7 1.0 convert_add_fusion.2
  95.7 0.9 convert_add_fusion.2
  96.7 0.9 convert_add_fusion.2
  97.6 0.9 convert_add_fusion.2
  98.6 0.9 convert_add_fusion.2
  99.6 0.9 convert_add_fusion.2
  100.6 0.9 convert_add_fusion.2
  101.5 0.7 fusion.24
  (26 shorter events, 2.5 us)
Async XLA Ops:
  7.2 11.6 %copy-start = (bf16[1,24,128,128]{3,2,1,0:T(8,128)(2,1)S(1)}, bf16[1,24,128,128]{3,2,1,0:T(8,128)(2,1)}, u32[]{:S(2)}) copy-start(bf16[1,24,128,128]{3,2,1,0:T(8,128)(2,1)} %param.16) | copy-start | bytes 2359300
  7.2 44.9 %reduce-scatter.2.cloned.1.call-start = ((), (), s32[]{:S(2)}) async-start(), calls=%async_computation.1 | async-start | bytes 655360 | tf_op jit(solution)/shard_map/reduce_scatter | solution.py:125
  16.8 1.0 copy-start.3
  18.7 1.1 %copy-start.1 = (bf16[1,24,128,128]{3,2,1,0:T(8,128)(2,1)S(1)}, bf16[1,24,128,128]{3,2,1,0:T(8,128)(2,1)}, u32[]{:S(2)}) copy-start(bf16[1,24,128,128]{3,2,1,0:T(8,128)(2,1)} %param.17) | copy-start | bytes 2359300
  29.4 65.2 %all-gather.4.cloned.1.call-start = ((), (), s32[]{:S(2)}) async-start(), calls=%async_computation.2 | async-start | bytes 1179648 | tf_op jit(solution)/shard_map/all_gather | solution.py:11
  94.6 6.9 %copy-start.2 = (bf16[16,4096]{1,0:T(8,128)(2,1)S(1)}, bf16[16,4096]{1,0:T(8,128)(2,1)}, u32[]{:S(2)}) copy-start(bf16[16,4096]{1,0:T(8,128)(2,1)} %reduce-scatter.2.cloned.1.call-done) | copy-start | bytes 393220
  94.6 6.9 %copy-start.4 = (bf16[16,4096]{1,0:T(8,128)(2,1)S(1)}, bf16[16,4096]{1,0:T(8,128)(2,1)}, u32[]{:S(2)}) copy-start(bf16[16,4096]{1,0:T(8,128)(2,1)} %param.15) | copy-start | bytes 393220
Sparse Core Ops, SparseCore 0:
  29.5 22.5 reduce-scatter.1
  54.4 40.1 all-gather.3
where the time goes:
time: 109 us
  waiting for transfers between devices  62.4 us (57%)
  between operations  14.9 us (14%)
  matrix products  9.97 us (9%)
  blocking collectives  8.83 us (8%)
  other arithmetic  8.16 us (7%)
  local copies, waits for them, and re-layouts  4.57 us (4%)
    all_gather x1, waiting for transfers between devices, carried_in(): gathered = lax.all_gather(array.astype(jnp.bfloat16), axis)  39.7 us
    reduce_scatter x1, waiting for transfers between devices, local(): lax.psum_scatter(over_slots(back, zero).reshape(count_rows, width).astype...  22.6 us
    all_gather x1, blocking collectives, local(): piece = lax.all_gather(own_rows, 'tp', axis=0, tiled=True)  8.83 us
    add x7, other arithmetic, local(): earlier + after  6.7 us
  transfers between devices with their start and end apart: 2, of which 2 were waited for; matrix products, arithmetic and copies ran while one was open for 3% of the time, Pallas kernels for 0%

commit v1 on v0

v1 whole, which is shorter than its diff:
```python
import functools

import jax
import jax.numpy as jnp
from jax import lax
from jax.experimental import pallas as pl
from jax.experimental.pallas import tpu as pltpu
from jax.sharding import PartitionSpec as P

F32 = jnp.float32
BF16 = jnp.bfloat16


def _forward_back(
    masks, blk, table_ref, place_ref, *refs
):
    pieces, refs = refs[: len(masks)], refs[len(masks) :]
    grad_ref, wg_ref, wu_ref, x_ref, cot_ref, *rest = refs
    outs, (act_ref, back_ref) = rest[:-2], rest[-2:]
    slots = wg_ref.shape[0]
    rows = x_ref.shape[0]
    row_blocks = x_ref.shape[1] // blk
    col_blocks = cot_ref.shape[0] - 1
    me = place_ref[0]
    for mask, piece in zip(masks, pieces, strict=True):
        count = piece.shape[0]
        if count == rows:
            x_ref[...] = piece[...]
        else:
            start = pl.multiple_of((me ^ mask) * count, count)
            x_ref[pl.ds(start, count), :] = piece[...]
    act_ref[...] = jnp.zeros_like(act_ref)
    back_ref[...] = jnp.zeros_like(back_ref)

    def weights(slot):
        return jnp.concatenate([wg_ref[slot], wu_ref[slot]], axis=1)

    for slot in range(slots):
        start = pl.multiple_of(table_ref[0, slot] * blk, blk)
        pre = jnp.dot(x_ref[:, pl.ds(start, blk)], weights(slot), preferred_element_type=F32)
        act_ref[table_ref[1, slot]] += pre
    for col in range(col_blocks):
        gate = act_ref[col, :, :blk]
        up = act_ref[col, :, blk:]
        upstream = grad_ref[:, col * blk : (col + 1) * blk].astype(F32)
        sig = jax.nn.sigmoid(gate)
        scaled = upstream * sig
        cot_ref[col, :, :blk] = (scaled * up * (1.0 + gate * (1.0 - sig))).astype(BF16)
        cot_ref[col, :, blk:] = (scaled * gate).astype(BF16)
    cot_ref[col_blocks] = jnp.zeros_like(cot_ref[col_blocks])
    for slot in range(slots):
        back = lax.dot_general(
            cot_ref[table_ref[1, slot]],
            weights(slot),
            (((1,), (1,)), ((), ())),
            preferred_element_type=F32,
        )
        back_ref[table_ref[0, slot]] += back
    if len(masks) == 1:
        for row in range(row_blocks):
            outs[0][:, row * blk : (row + 1) * blk] = back_ref[row].astype(BF16)
        return
    count = rows // len(masks)
    keep_ref, far_ref, send_ref = outs
    for target, mask in (
        (keep_ref, 0),
        (far_ref, 2),
        (send_ref.at[0], 1),
        (send_ref.at[1], 3),
    ):
        start = pl.multiple_of((me ^ mask) * count, count)
        for row in range(row_blocks):
            target[:, row * blk : (row + 1) * blk] = back_ref[row, pl.ds(start, count), :].astype(
                target.dtype
            )


def _weight_grads(blk, table_ref, x_ref, cot_ref, gate_ref, up_ref):
    slots = gate_ref.shape[0]
    for slot in range(slots):
        start = pl.multiple_of(table_ref[0, slot] * blk, blk)
        grads = lax.dot_general(
            x_ref[:, pl.ds(start, blk)],
            cot_ref[table_ref[1, slot]],
            (((0,), (0,)), ((), ())),
            preferred_element_type=F32,
        )
        gate_ref[slot] = grads[:, :blk].astype(BF16)
        up_ref[slot] = grads[:, blk:].astype(BF16)


def _swap(array, axis, distance):
    count = lax.axis_size(axis)
    return lax.ppermute(array, axis, [(i, i ^ distance) for i in range(count)])


def local(inputs, hidden_grad, top_grad, w_gate, w_up, block_pos, live_count):
    own_rows = inputs[0]
    count, width = own_rows.shape
    slots, blk = w_gate.shape[1], w_gate.shape[2]
    col_blocks = hidden_grad.shape[2] // blk
    tp = lax.axis_size("tp")
    sections = lax.axis_size("section")
    rows = count * tp
    me = lax.axis_index("tp")
    section = lax.axis_index("section")

    position = block_pos[0]
    live = lax.iota(jnp.int32, slots) < live_count[0, 0]
    table = jnp.stack(
        [position // col_blocks, jnp.where(live, position % col_blocks, col_blocks)]
    )
    place = jnp.reshape(me, (1,)).astype(jnp.int32)

    paired = tp == 4
    if paired:
        across = _swap(own_rows, "tp", 2)
        beside = _swap(own_rows, "tp", 1)
        beyond = _swap(across, "tp", 1)
        pieces, masks = (own_rows, beside, across, beyond), (0, 1, 2, 3)
        terms = (
            jax.ShapeDtypeStruct((count, width), F32),
            jax.ShapeDtypeStruct((count, width), F32),
            jax.ShapeDtypeStruct((2, count, width), BF16),
        )
    else:
        pieces, masks = (lax.all_gather(own_rows, "tp", axis=0, tiled=True),), (0,)
        terms = (jax.ShapeDtypeStruct((rows, width), BF16),)

    vmem = pl.BlockSpec(memory_space=pltpu.VMEM)
    smem = pl.BlockSpec(memory_space=pltpu.SMEM)
    x_all, cot, *terms = pl.pallas_call(
        functools.partial(_forward_back, masks, blk),
        out_shape=(
            jax.ShapeDtypeStruct((rows, width), BF16),
            jax.ShapeDtypeStruct((col_blocks + 1, rows, 2 * blk), BF16),
            *terms,
        ),
        in_specs=[smem, smem] + [vmem] * (len(pieces) + 3),
        out_specs=[vmem] * (2 + len(terms)),
        scratch_shapes=[
            pltpu.VMEM((col_blocks + 1, rows, 2 * blk), F32),
            pltpu.VMEM((width // blk, rows, blk), F32),
        ],
        compiler_params=pltpu.CompilerParams(vmem_limit_bytes=48 << 20),
        name="forward_back",
    )(table, place, *pieces, hidden_grad[0], w_gate[0], w_up[0])

    gate_gradient, up_gradient = pl.pallas_call(
        functools.partial(_weight_grads, blk),
        out_shape=(jax.ShapeDtypeStruct((slots, blk, blk), BF16),) * 2,
        in_specs=[smem, vmem, vmem],
        out_specs=[vmem, vmem],
        compiler_params=pltpu.CompilerParams(vmem_limit_bytes=48 << 20),
        name="weight_grads",
    )(table, x_all, cot)

    if paired:
        keep, far, send = terms
        came = _swap(send, "tp", 1)
        crossed = _swap((far + came[1].astype(F32)).astype(BF16), "tp", 2)
        own_term = keep + came[0].astype(F32) + crossed.astype(F32)
    else:
        own_term = lax.psum_scatter(terms[0], "tp", scatter_dimension=0, tiled=True).astype(F32)

    total = own_term
    result = top_grad.astype(F32) + own_term
    if sections & (sections - 1) == 0:
        distance = 1
        while distance < sections:
            other = _swap(total.astype(BF16), "section", distance).astype(F32)
            result = result + jnp.where(section & distance == 0, other, 0.0)
            total = total + other
            distance *= 2
    else:
        distance = 1
        while distance < sections:
            moves = [(i, i - distance) for i in range(distance, sections)]
            total = total + lax.ppermute(total.astype(BF16), "section", moves).astype(F32)
            distance *= 2
        result = top_grad.astype(F32) + total
    return (
        result.astype(BF16)[None],
        gate_gradient[None],
        up_gradient[None],
    )


def solution(mesh):
    in_specs = (
        P("section", "tp", None),
        P("section", None, "tp"),
        P("tp", None),
        P("section", "tp", None, None),
        P("section", "tp", None, None),
        P("section", "tp"),
        P("section", "tp"),
    )
    out_specs = (
        P("section", "tp", None),
        P("section", "tp", None, None),
        P("section", "tp", None, None),
    )
    return jax.shard_map(local, mesh=mesh, in_specs=in_specs, out_specs=out_specs, check_vma=False)
```

time: 109 us -> 41.3 us (0.38)
  waiting for transfers between devices: 62.4 us -> 17.9 us
  between operations: 14.9 us -> 1.35 us
  starting transfers between devices: 0.08 us -> 12 us
  matrix products: 9.97 us -> 0 us
  blocking collectives: 8.83 us -> 0 us
  other arithmetic: 8.16 us -> 0.93 us
  Pallas kernels: 0 us -> 4.6 us
    all_gather x1 -> x0, waiting for transfers between devices: 39.7 us -> none  [carried_in(): gathered = lax.all_gather(array.astype(jnp.bfloat16), axis)]
    reduce_scatter x1 -> x0, waiting for transfers between devices: 22.6 us -> none  [local(): lax.psum_scatter(over_slots(back, zero).reshape(count_rows, width).astype...]
    ppermute x0 -> x8, waiting for transfers between devices: none -> 17.9 us  [_swap(): return lax.ppermute(array, axis, [(i, i ^ distance) for i in range(count)])]
    ppermute x0 -> x8, starting transfers between devices: none -> 12 us  [_swap(): return lax.ppermute(array, axis, [(i, i ^ distance) for i in range(count)])]
    dot_general x9 -> x0, matrix products: 9.97 us -> none  [the longest x1 1.85 us: project(): jnp.einsum('kc,krn->rcn', select, pre_up, precision=highest_precision)]
    all_gather x1 -> x0, blocking collectives: 8.83 us -> none  [local(): piece = lax.all_gather(own_rows, 'tp', axis=0, tiled=True)]
    add x7 -> x0, other arithmetic: 6.7 us -> none  [local(): earlier + after]
    pallas_call x0 -> x2, Pallas kernels: none -> 4.6 us  [the longest x1 2.3 us: local(): pl.pallas_call(functools.partial(_weight_grads, blk), out_shape=(jax.Shap...]
  transfers between devices with their start and end apart: 2 -> 8, of which waited for: 2 -> 7; matrix products, arithmetic and copies ran while one was open for 3% -> 0% of each run, Pallas kernels for 0% -> 6%
where the time goes in v1:
time: 41.3 us; the launch traced here: 41 us
  waiting for transfers between devices  17.9 us (43%)
  starting transfers between devices  12 us (29%)
  Pallas kernels  4.6 us (11%)
  local copies, waits for them, and re-layouts  4.2 us (10%)
  between operations  1.35 us (3%)
  other arithmetic  0.93 us (2%)
    ppermute x8, waiting for transfers between devices, _swap(): return lax.ppermute(array, axis, [(i, i ^ distance) for i in range(count)])  17.9 us
    ppermute x8, starting transfers between devices, _swap(): return lax.ppermute(array, axis, [(i, i ^ distance) for i in range(count)])  12 us
    unnamed x12, local copies, waits for them, and re-layouts  4.2 us
    pallas_call x1, Pallas kernels, local(): pl.pallas_call(functools.partial(_weight_grads, blk), out_shape=(jax.Shap...  2.3 us
    pallas_call x1, Pallas kernels, local(): pl.pallas_call(functools.partial(_forward_back, masks, blk), out_shape=(j...  2.3 us
  transfers between devices with their start and end apart: 8, of which 7 were waited for; matrix products, arithmetic and copies ran while one was open for 0% of the time, Pallas kernels for 6%

profile of v1, /device:TPU:0, one launch (start us, length us, event | category | flops | bytes accessed | tf_op | source)
XLA Modules:
  0.0 41.0 jit_solution(16330447949810554546)
XLA Ops:
  0.6 3.0 %collective-permute-start.1 = (bf16[16,4096]{1,0:T(8,128)(2,1)}, bf16[16,4096]{1,0:T(8,128)(2,1)S(1)}, u32[]{:S(2)}, u32[]{:S(2)}) collective-permute-start(bf16[16,4096]{1,0:T(8,128)(2,1)} %bitcast.25), channel_id=1, source_target_pairs={{0,2},{1,3},{2,0},{3,1},{4,6},{5,7},{6,4},{7,5},{8,10},{9,11},{10,... | collective-permute-start | bytes 393224 | tf_op jit(solution)/shard_map/ppermute | solution.py:94
  3.6 0.0 collective-permute-start
  4.3 0.0 copy-start.5
  4.3 3.0 %collective-permute-done.1.refs_2_ = bf16[16,4096]{1,0:T(8,128)(2,1)S(1)} collective-permute-done((bf16[16,4096]{1,0:T(8,128)(2,1)}, bf16[16,4096]{1,0:T(8,128)(2,1)S(1)}, u32[]{:S(2)}, u32[]{:S(2)}) %collective-permute-start.1) | collective-permute-done | bytes 131104 | tf_op jit(solution)/shard_map/ppermute | solution.py:94
  7.3 0.0 collective-permute-start.2
  7.4 0.0 collective-permute-done.refs_1_
  7.4 1.3 %collective-permute-done.2.refs_3_ = bf16[16,4096]{1,0:T(8,128)(2,1)S(1)} collective-permute-done((bf16[16,4096]{1,0:T(8,128)(2,1)S(1)}, bf16[16,4096]{1,0:T(8,128)(2,1)S(1)}, u32[]{:S(2)}, u32[]{:S(2)}) %collective-permute-start.2) | collective-permute-done | bytes 131104 | tf_op jit(solution)/shard_map/ppermute | solution.py:94
  8.7 1.1 %copy-done = bf16[1,24,128,128]{3,2,1,0:T(8,128)(2,1)S(1)} copy-done((bf16[1,24,128,128]{3,2,1,0:T(8,128)(2,1)S(1)}, bf16[1,24,128,128]{3,2,1,0:T(8,128)(2,1)}, u32[]{:S(2)}) %copy-start) | copy-done | bytes 786456
  9.8 1.1 %copy-done.1 = bf16[1,24,128,128]{3,2,1,0:T(8,128)(2,1)S(1)} copy-done((bf16[1,24,128,128]{3,2,1,0:T(8,128)(2,1)S(1)}, bf16[1,24,128,128]{3,2,1,0:T(8,128)(2,1)}, u32[]{:S(2)}) %copy-start.1) | copy-done | bytes 786456
  11.0 1.0 %copy-done.2 = bf16[1,64,3584]{2,1,0:T(8,128)(2,1)S(1)} copy-done((bf16[1,64,3584]{2,1,0:T(8,128)(2,1)S(1)}, bf16[1,64,3584]{2,1,0:T(8,128)(2,1)}, u32[]{:S(2)}) %copy-start.2) | copy-done | bytes 458776
  12.0 0.9 %copy-done.3 = bf16[1,16,4096]{2,1,0:T(8,128)(2,1)S(1)} copy-done((bf16[1,16,4096]{2,1,0:T(8,128)(2,1)S(1)}, bf16[1,16,4096]{2,1,0:T(8,128)(2,1)}, u32[]{:S(2)}) %copy-start.3) | copy-done | bytes 131096
  12.9 2.3 %forward_back.1 = (bf16[64,4096]{1,0:T(8,128)(2,1)S(1)}, bf16[29,64,256]{2,1,0:T(8,128)(2,1)S(1)}, f32[16,4096]{1,0:T(8,128)S(1)}, f32[16,4096]{1,0:T(8,128)S(1)}, bf16[2,16,4096]{2,1,0:T(8,128)(2,1)S(1)}) custom-call(s32[2,24]{1,0:T(2,128)S(1)} %pad_add_fusion.table_ref, s32[1]{0:T(128)} %bitcast.1.place_ref, bf16[16,4096]{1,0:T(8,128)(2,1)S(1)} %bitcast.27, ...), custom_call_target="tpu_custom_call" | custom-call | tf_op jit(solution)/shard_map/forward_back/pallas_call | solution.py:132
  15.2 0.2 collective-permute-start.3
  15.4 1.4 %collective-permute-done.3 = bf16[2,16,4096]{2,1,0:T(8,128)(2,1)S(1)} collective-permute-done((bf16[2,16,4096]{2,1,0:T(8,128)(2,1)S(1)}, bf16[2,16,4096]{2,1,0:T(8,128)(2,1)S(1)}, u32[]{:S(2)}, u32[]{:S(2)}) %collective-permute-start.3) | collective-permute-done | bytes 262176 | tf_op jit(solution)/shard_map/ppermute | solution.py:94
  16.8 1.8 %collective-permute-start.4 = (bf16[16,4096]{1,0:T(8,128)(2,1)S(1)}, bf16[16,4096]{1,0:T(8,128)(2,1)S(1)}, u32[]{:S(2)}, u32[]{:S(2)}) collective-permute-start(bf16[16,4096]{1,0:T(8,128)(2,1)S(1)} %fusion.5), channel_id=1, source_target_pairs={{0,2},{1,3},{2,0},{3,1},{4,6},{5,7},{6,4},{7,5},{8,10},{9,11},{10,... | collective-permute-start | bytes 393224 | tf_op jit(solution)/shard_map/ppermute | solution.py:94
  18.6 3.8 %collective-permute-done.4 = bf16[16,4096]{1,0:T(8,128)(2,1)S(1)} collective-permute-done((bf16[16,4096]{1,0:T(8,128)(2,1)S(1)}, bf16[16,4096]{1,0:T(8,128)(2,1)S(1)}, u32[]{:S(2)}, u32[]{:S(2)}) %collective-permute-start.4) | collective-permute-done | bytes 131104 | tf_op jit(solution)/shard_map/ppermute | solution.py:94
  22.5 1.8 %collective-permute-start.5 = (bf16[16,4096]{1,0:T(8,128)(2,1)S(1)}, bf16[16,4096]{1,0:T(8,128)(2,1)S(1)}, u32[]{:S(2)}, u32[]{:S(2)}) collective-permute-start(bf16[16,4096]{1,0:T(8,128)(2,1)S(1)} %get-tuple-element.17), channel_id=1, source_target_pairs={{0,4},{4,0},{8,12},{12,8},{16,20},{20,16},{24,28},{28,24},{1,5},{5... | collective-permute-start | bytes 393224 | tf_op jit(solution)/shard_map/ppermute | solution.py:94
  24.3 3.2 %collective-permute-done.5 = bf16[16,4096]{1,0:T(8,128)(2,1)S(1)} collective-permute-done((bf16[16,4096]{1,0:T(8,128)(2,1)S(1)}, bf16[16,4096]{1,0:T(8,128)(2,1)S(1)}, u32[]{:S(2)}, u32[]{:S(2)}) %collective-permute-start.5) | collective-permute-done | bytes 131104 | tf_op jit(solution)/shard_map/ppermute | solution.py:94
  27.6 1.9 %collective-permute-start.6 = (bf16[16,4096]{1,0:T(8,128)(2,1)S(1)}, bf16[16,4096]{1,0:T(8,128)(2,1)S(1)}, u32[]{:S(2)}, u32[]{:S(2)}) collective-permute-start(bf16[16,4096]{1,0:T(8,128)(2,1)S(1)} %fusion.7), channel_id=1, source_target_pairs={{0,8},{4,12},{8,0},{12,4},{16,24},{20,28},{24,16},{28,20},{1,9},{5... | collective-permute-start | bytes 393224 | tf_op jit(solution)/shard_map/ppermute | solution.py:94
  29.4 3.1 %collective-permute-done.6 = bf16[16,4096]{1,0:T(8,128)(2,1)S(1)} collective-permute-done((bf16[16,4096]{1,0:T(8,128)(2,1)S(1)}, bf16[16,4096]{1,0:T(8,128)(2,1)S(1)}, u32[]{:S(2)}, u32[]{:S(2)}) %collective-permute-start.6) | collective-permute-done | bytes 131104 | tf_op jit(solution)/shard_map/ppermute | solution.py:94
  32.6 3.3 %collective-permute-start.7 = (bf16[16,4096]{1,0:T(8,128)(2,1)S(1)}, bf16[16,4096]{1,0:T(8,128)(2,1)S(1)}, u32[]{:S(2)}, u32[]{:S(2)}) collective-permute-start(bf16[16,4096]{1,0:T(8,128)(2,1)S(1)} %fusion.4), channel_id=1, source_target_pairs={{0,16},{4,20},{8,24},{12,28},{16,0},{20,4},{24,8},{28,12},{1,17},{... | collective-permute-start | bytes 393224 | tf_op jit(solution)/shard_map/ppermute | solution.py:94
  35.9 2.3 %weight_grads.1 = (bf16[24,128,128]{2,1,0:T(8,128)(2,1)}, bf16[24,128,128]{2,1,0:T(8,128)(2,1)}) custom-call(s32[2,24]{1,0:T(2,128)S(1)} %pad_add_fusion.table_ref, bf16[64,4096]{1,0:T(8,128)(2,1)S(1)} %get-tuple-element.13.x_ref, bf16[29,64,256]{2,1,0:T(8,128)(2,1)S(1)} %get-tuple-element.14.cot_ref), custom_call_target="tpu_custom_call" | custom-call | tf_op jit(solution)/shard_map/weight_grads/pallas_call | solution.py:149
  38.2 2.0 %collective-permute-done.7 = bf16[16,4096]{1,0:T(8,128)(2,1)S(1)} collective-permute-done((bf16[16,4096]{1,0:T(8,128)(2,1)S(1)}, bf16[16,4096]{1,0:T(8,128)(2,1)S(1)}, u32[]{:S(2)}, u32[]{:S(2)}) %collective-permute-start.7) | collective-permute-done | bytes 131104 | tf_op jit(solution)/shard_map/ppermute | solution.py:94
  40.3 0.8 %fusion.8 = bf16[1,16,4096]{2,1,0:T(8,128)(2,1)} fusion(bf16[16,4096]{1,0:T(8,128)(2,1)S(1)} %collective-permute-done.7, bf16[16,4096]{1,0:T(8,128)(2,1)S(1)} %collective-permute-done.6, bf16[16,4096]{1,0:T(8,128)(2,1)S(1)} %collective-permute-done.5, f32[16,4096]{1,0:T(8,128)S(1)} %get-tuple-element.18, bf16[16,4096]{1,0:T(8,128)(2,1)S(1)} %copy-done.4, ...), kind=kLoop, calls=%fused_computation.14 | loop fusion | flops 786432 | bytes 917507 | tf_op jit(solution)/shard_map/broadcast_in_dim | solution.py:183
  (13 shorter events, 0.2 us)
Async XLA Ops:
  0.6 6.7 %collective-permute-start.1 = (bf16[16,4096]{1,0:T(8,128)(2,1)}, bf16[16,4096]{1,0:T(8,128)(2,1)S(1)}, u32[]{:S(2)}, u32[]{:S(2)}) collective-permute-start(bf16[16,4096]{1,0:T(8,128)(2,1)} %bitcast.25), channel_id=1, source_target_pairs={{0,2},{1,3},{2,0},{3,1},{4,6},{5,7},{6,4},{7,5},{8,10},{9,11},{10,... | collective-permute-start | bytes 393224 | tf_op jit(solution)/shard_map/ppermute | solution.py:94
  3.6 3.8 %collective-permute-start = (bf16[16,4096]{1,0:T(8,128)(2,1)}, bf16[16,4096]{1,0:T(8,128)(2,1)S(1)}, u32[]{:S(2)}, u32[]{:S(2)}) collective-permute-start(bf16[16,4096]{1,0:T(8,128)(2,1)} %bitcast.26), channel_id=1, source_target_pairs={{0,1},{1,0},{2,3},{3,2},{4,5},{5,4},{6,7},{7,6},{8,9},{9,8},{10,11... | collective-permute-start | bytes 393224 | tf_op jit(solution)/shard_map/ppermute | solution.py:94
  4.3 3.1 %copy-start.5 = (s32[1,24]{1,0:T(1,128)S(1)}, s32[1,24]{1,0:T(1,128)}, u32[]{:S(2)}) copy-start(s32[1,24]{1,0:T(1,128)} %param.12) | copy-start | bytes 292
  7.3 1.3 %collective-permute-start.2 = (bf16[16,4096]{1,0:T(8,128)(2,1)S(1)}, bf16[16,4096]{1,0:T(8,128)(2,1)S(1)}, u32[]{:S(2)}, u32[]{:S(2)}) collective-permute-start(bf16[16,4096]{1,0:T(8,128)(2,1)S(1)} %collective-permute-done.1.refs_2_), channel_id=1, source_target_pairs={{0,1},{1,0},{2,3},{3,2},{4,5},{5,4},{6,7},{7,6},{8,9},{9,8},{10,11... | collective-permute-start | bytes 393224 | tf_op jit(solution)/shard_map/ppermute | solution.py:94
  8.7 1.1 %copy-start = (bf16[1,24,128,128]{3,2,1,0:T(8,128)(2,1)S(1)}, bf16[1,24,128,128]{3,2,1,0:T(8,128)(2,1)}, u32[]{:S(2)}) copy-start(bf16[1,24,128,128]{3,2,1,0:T(8,128)(2,1)} %param.10) | copy-start | bytes 2359300
  9.8 1.1 %copy-start.1 = (bf16[1,24,128,128]{3,2,1,0:T(8,128)(2,1)S(1)}, bf16[1,24,128,128]{3,2,1,0:T(8,128)(2,1)}, u32[]{:S(2)}) copy-start(bf16[1,24,128,128]{3,2,1,0:T(8,128)(2,1)} %param.11) | copy-start | bytes 2359300
  11.0 1.0 %copy-start.2 = (bf16[1,64,3584]{2,1,0:T(8,128)(2,1)S(1)}, bf16[1,64,3584]{2,1,0:T(8,128)(2,1)}, u32[]{:S(2)}) copy-start(bf16[1,64,3584]{2,1,0:T(8,128)(2,1)} %param.8) | copy-start | bytes 1376260
  12.0 0.9 %copy-start.3 = (bf16[1,16,4096]{2,1,0:T(8,128)(2,1)S(1)}, bf16[1,16,4096]{2,1,0:T(8,128)(2,1)}, u32[]{:S(2)}) copy-start(bf16[1,16,4096]{2,1,0:T(8,128)(2,1)} %param.7) | copy-start | bytes 393220
  15.2 1.6 %collective-permute-start.3 = (bf16[2,16,4096]{2,1,0:T(8,128)(2,1)S(1)}, bf16[2,16,4096]{2,1,0:T(8,128)(2,1)S(1)}, u32[]{:S(2)}, u32[]{:S(2)}) collective-permute-start(bf16[2,16,4096]{2,1,0:T(8,128)(2,1)S(1)} %get-tuple-element.11), channel_id=1, source_target_pairs={{0,1},{1,0},{2,3},{3,2},{4,5},{5,4},{6,7},{7,6},{8,9},{9,8},{10,11... | collective-permute-start | bytes 786440 | tf_op jit(solution)/shard_map/ppermute | solution.py:94
  16.8 5.6 %collective-permute-start.4 = (bf16[16,4096]{1,0:T(8,128)(2,1)S(1)}, bf16[16,4096]{1,0:T(8,128)(2,1)S(1)}, u32[]{:S(2)}, u32[]{:S(2)}) collective-permute-start(bf16[16,4096]{1,0:T(8,128)(2,1)S(1)} %fusion.5), channel_id=1, source_target_pairs={{0,2},{1,3},{2,0},{3,1},{4,6},{5,7},{6,4},{7,5},{8,10},{9,11},{10,... | collective-permute-start | bytes 393224 | tf_op jit(solution)/shard_map/ppermute | solution.py:94
  22.5 5.0 %collective-permute-start.5 = (bf16[16,4096]{1,0:T(8,128)(2,1)S(1)}, bf16[16,4096]{1,0:T(8,128)(2,1)S(1)}, u32[]{:S(2)}, u32[]{:S(2)}) collective-permute-start(bf16[16,4096]{1,0:T(8,128)(2,1)S(1)} %get-tuple-element.17), channel_id=1, source_target_pairs={{0,4},{4,0},{8,12},{12,8},{16,20},{20,16},{24,28},{28,24},{1,5},{5... | collective-permute-start | bytes 393224 | tf_op jit(solution)/shard_map/ppermute | solution.py:94
  27.6 5.0 %collective-permute-start.6 = (bf16[16,4096]{1,0:T(8,128)(2,1)S(1)}, bf16[16,4096]{1,0:T(8,128)(2,1)S(1)}, u32[]{:S(2)}, u32[]{:S(2)}) collective-permute-start(bf16[16,4096]{1,0:T(8,128)(2,1)S(1)} %fusion.7), channel_id=1, source_target_pairs={{0,8},{4,12},{8,0},{12,4},{16,24},{20,28},{24,16},{28,20},{1,9},{5... | collective-permute-start | bytes 393224 | tf_op jit(solution)/shard_map/ppermute | solution.py:94
  32.6 7.6 %collective-permute-start.7 = (bf16[16,4096]{1,0:T(8,128)(2,1)S(1)}, bf16[16,4096]{1,0:T(8,128)(2,1)S(1)}, u32[]{:S(2)}, u32[]{:S(2)}) collective-permute-start(bf16[16,4096]{1,0:T(8,128)(2,1)S(1)} %fusion.4), channel_id=1, source_target_pairs={{0,16},{4,20},{8,24},{12,28},{16,0},{20,4},{24,8},{28,12},{1,17},{... | collective-permute-start | bytes 393224 | tf_op jit(solution)/shard_map/ppermute | solution.py:94
  35.9 4.4 %copy-start.4 = (bf16[16,4096]{1,0:T(8,128)(2,1)S(1)}, bf16[16,4096]{1,0:T(8,128)(2,1)}, u32[]{:S(2)}) copy-start(bf16[16,4096]{1,0:T(8,128)(2,1)} %param.9) | copy-start | bytes 393220

commit v2 on v1

--- a/solution.py
+++ b/solution.py
@@ -11,13 +11,25 @@
 BF16 = jnp.bfloat16
 
 
-def _forward_back(
-    masks, blk, table_ref, place_ref, *refs
-):
+def _stage(own_in, grad_in, wg_in, wu_in, own_ref, grad_ref, weight_ref, sems):
+    blk = wg_in.shape[2]
+    copies = [
+        pltpu.make_async_copy(wg_in, weight_ref.at[:, :, :blk], sems.at[0]),
+        pltpu.make_async_copy(wu_in, weight_ref.at[:, :, blk:], sems.at[1]),
+        pltpu.make_async_copy(grad_in, grad_ref, sems.at[2]),
+        pltpu.make_async_copy(own_in, own_ref, sems.at[3]),
+    ]
+    for copy in copies:
+        copy.start()
+    for copy in copies:
+        copy.wait()
+
+
+def _forward_back(masks, blk, table_ref, place_ref, *refs):
     pieces, refs = refs[: len(masks)], refs[len(masks) :]
-    grad_ref, wg_ref, wu_ref, x_ref, cot_ref, *rest = refs
+    grad_ref, weight_ref, x_ref, cot_ref, *rest = refs
     outs, (act_ref, back_ref) = rest[:-2], rest[-2:]
-    slots = wg_ref.shape[0]
+    slots = weight_ref.shape[0]
     rows = x_ref.shape[0]
     row_blocks = x_ref.shape[1] // blk
     col_blocks = cot_ref.shape[0] - 1
@@ -32,12 +44,9 @@
     act_ref[...] = jnp.zeros_like(act_ref)
     back_ref[...] = jnp.zeros_like(back_ref)
 
-    def weights(slot):
-        return jnp.concatenate([wg_ref[slot], wu_ref[slot]], axis=1)
-
     for slot in range(slots):
         start = pl.multiple_of(table_ref[0, slot] * blk, blk)
-        pre = jnp.dot(x_ref[:, pl.ds(start, blk)], weights(slot), preferred_element_type=F32)
+        pre = jnp.dot(x_ref[:, pl.ds(start, blk)], weight_ref[slot], preferred_element_type=F32)
         act_ref[table_ref[1, slot]] += pre
     for col in range(col_blocks):
         gate = act_ref[col, :, :blk]
@@ -51,7 +60,7 @@
     for slot in range(slots):
         back = lax.dot_general(
             cot_ref[table_ref[1, slot]],
-            weights(slot),
+            weight_ref[slot],
             (((1,), (1,)), ((), ())),
             preferred_element_type=F32,
         )
@@ -89,6 +98,9 @@
         up_ref[slot] = grads[:, blk:].astype(BF16)
 
 
+_pinned = pltpu.with_memory_space_constraint
+
+
 def _swap(array, axis, distance):
     count = lax.axis_size(axis)
     return lax.ppermute(array, axis, [(i, i ^ distance) for i in range(count)])
@@ -112,12 +124,28 @@
     )
     place = jnp.reshape(me, (1,)).astype(jnp.int32)
 
+    vmem = pl.BlockSpec(memory_space=pltpu.VMEM)
+    smem = pl.BlockSpec(memory_space=pltpu.SMEM)
+    own_staged, grad_staged, weights = pl.pallas_call(
+        _stage,
+        out_shape=(
+            jax.ShapeDtypeStruct(own_rows.shape, BF16),
+            jax.ShapeDtypeStruct(hidden_grad.shape[1:], BF16),
+            jax.ShapeDtypeStruct((slots, blk, 2 * blk), BF16),
+        ),
+        in_specs=[pl.BlockSpec(memory_space=pltpu.HBM)] * 4,
+        out_specs=[vmem] * 3,
+        scratch_shapes=[pltpu.SemaphoreType.DMA((4,))],
+        compiler_params=pltpu.CompilerParams(vmem_limit_bytes=4 << 20),
+        name="stage",
+    )(*(_pinned(array, pltpu.HBM) for array in (own_rows, hidden_grad[0], w_gate[0], w_up[0])))
+
     paired = tp == 4
     if paired:
         across = _swap(own_rows, "tp", 2)
         beside = _swap(own_rows, "tp", 1)
         beyond = _swap(across, "tp", 1)
-        pieces, masks = (own_rows, beside, across, beyond), (0, 1, 2, 3)
+        pieces, masks = (own_staged, beside, across, beyond), (0, 1, 2, 3)
         terms = (
             jax.ShapeDtypeStruct((count, width), F32),
             jax.ShapeDtypeStruct((count, width), F32),
@@ -127,8 +155,6 @@
         pieces, masks = (lax.all_gather(own_rows, "tp", axis=0, tiled=True),), (0,)
         terms = (jax.ShapeDtypeStruct((rows, width), BF16),)
 
-    vmem = pl.BlockSpec(memory_space=pltpu.VMEM)
-    smem = pl.BlockSpec(memory_space=pltpu.SMEM)
     x_all, cot, *terms = pl.pallas_call(
         functools.partial(_forward_back, masks, blk),
         out_shape=(
@@ -136,22 +162,22 @@
             jax.ShapeDtypeStruct((col_blocks + 1, rows, 2 * blk), BF16),
             *terms,
         ),
-        in_specs=[smem, smem] + [vmem] * (len(pieces) + 3),
+        in_specs=[smem, smem] + [vmem] * (len(pieces) + 2),
         out_specs=[vmem] * (2 + len(terms)),
         scratch_shapes=[
             pltpu.VMEM((col_blocks + 1, rows, 2 * blk), F32),
             pltpu.VMEM((width // blk, rows, blk), F32),
         ],
-        compiler_params=pltpu.CompilerParams(vmem_limit_bytes=48 << 20),
+        compiler_params=pltpu.CompilerParams(vmem_limit_bytes=12 << 20),
         name="forward_back",
-    )(table, place, *pieces, hidden_grad[0], w_gate[0], w_up[0])
+    )(table, place, *(_pinned(array, pltpu.VMEM) for array in (*pieces, grad_staged, weights)))
 
     gate_gradient, up_gradient = pl.pallas_call(
         functools.partial(_weight_grads, blk),
         out_shape=(jax.ShapeDtypeStruct((slots, blk, blk), BF16),) * 2,
         in_specs=[smem, vmem, vmem],
         out_specs=[vmem, vmem],
-        compiler_params=pltpu.CompilerParams(vmem_limit_bytes=48 << 20),
+        compiler_params=pltpu.CompilerParams(vmem_limit_bytes=8 << 20),
         name="weight_grads",
     )(table, x_all, cot)
 
@@ -166,12 +192,17 @@
     total = own_term
     result = top_grad.astype(F32) + own_term
     if sections & (sections - 1) == 0:
-        distance = 1
-        while distance < sections:
-            other = _swap(total.astype(BF16), "section", distance).astype(F32)
-            result = result + jnp.where(section & distance == 0, other, 0.0)
+        block = min(sections, 4)
+        sent = own_term.astype(BF16)
+        for step in range(1, block):
+            other = _swap(sent, "section", step).astype(F32)
+            result = result + jnp.where((section ^ step) > section, other, 0.0)
             total = total + other
-            distance *= 2
+        while block < sections:
+            other = _swap(total.astype(BF16), "section", block ^ (block >> 1)).astype(F32)
+            result = result + jnp.where(section & block == 0, other, 0.0)
+            total = total + other
+            block *= 2
     else:
         distance = 1
         while distance < sections:

time: 41.3 us -> 36.9 us (0.89)
  local copies, waits for them, and re-layouts: 4.2 us -> 0.01 us
  waiting for transfers between devices: 17.9 us -> 15 us
  Pallas kernels: 4.6 us -> 6.12 us
  other arithmetic: 0.93 us -> 1.7 us
  starting transfers between devices: 12 us -> 12.6 us
    unnamed x12 -> x2, local copies, waits for them, and re-layouts: 4.2 us -> 0.01 us
    ppermute x8 -> x9, waiting for transfers between devices: 17.9 us -> 15 us  [_swap(): return lax.ppermute(array, axis, [(i, i ^ distance) for i in range(count)])]
    pallas_call x0 -> x1, Pallas kernels: none -> 1.55 us  [local(): pl.pallas_call(_stage, out_shape=(jax.ShapeDtypeStruct(own_rows.shape, BF...]
    select_n x1, other arithmetic: 0.02 us -> 0.67 us  [local(): position // col_blocks]
    ppermute x8 -> x9, starting transfers between devices: 12 us -> 12.6 us  [_swap(): return lax.ppermute(array, axis, [(i, i ^ distance) for i in range(count)])]
  transfers between devices with their start and end apart: 8 -> 9, of which waited for: 7 -> 7; matrix products, arithmetic and copies ran while one was open for 0% -> 2% of each run, Pallas kernels for 6% -> 11%
where the time goes in v2:
time: 36.9 us; the launch traced here: 36.7 us
  waiting for transfers between devices  15 us (41%)
  starting transfers between devices  12.6 us (34%)
  Pallas kernels  6.12 us (17%)
  other arithmetic  1.7 us (5%)
  between operations  1.34 us (4%)
    ppermute x9, waiting for transfers between devices, _swap(): return lax.ppermute(array, axis, [(i, i ^ distance) for i in range(count)])  15 us
    ppermute x9, starting transfers between devices, _swap(): return lax.ppermute(array, axis, [(i, i ^ distance) for i in range(count)])  12.6 us
    pallas_call x1, Pallas kernels, local(): pl.pallas_call(functools.partial(_weight_grads, blk), out_shape=(jax.Shap...  2.3 us
    pallas_call x1, Pallas kernels, local(): pl.pallas_call(functools.partial(_forward_back, masks, blk), out_shape=(j...  2.26 us
    pallas_call x1, Pallas kernels, local(): pl.pallas_call(_stage, out_shape=(jax.ShapeDtypeStruct(own_rows.shape, BF...  1.55 us
    broadcast_in_dim x1, other arithmetic, local(): return (result.astype(BF16)[None], gate_gradient[None], up_gradient[None])  0.83 us
  transfers between devices with their start and end apart: 9, of which 7 were waited for; matrix products, arithmetic and copies ran while one was open for 2% of the time, Pallas kernels for 11%

profile of v2, /device:TPU:0, one launch (start us, length us, event | category | flops | bytes accessed | tf_op | source)
XLA Modules:
  0.0 36.7 jit_solution(4855897652883953365)
XLA Ops:
  0.6 3.0 %collective-permute-start.1 = (bf16[16,4096]{1,0:T(8,128)(2,1)}, bf16[16,4096]{1,0:T(8,128)(2,1)S(1)}, u32[]{:S(2)}, u32[]{:S(2)}) collective-permute-start(bf16[16,4096]{1,0:T(8,128)(2,1)} %bitcast.30), channel_id=1, source_target_pairs={{0,2},{1,3},{2,0},{3,1},{4,6},{5,7},{6,4},{7,5},{8,10},{9,11},{10,... | collective-permute-start | bytes 393224 | tf_op jit(solution)/shard_map/ppermute | solution.py:106
  3.6 0.0 collective-permute-start
  4.3 3.1 %collective-permute-done.1.refs_2_ = bf16[16,4096]{1,0:T(8,128)(2,1)S(1)} collective-permute-done((bf16[16,4096]{1,0:T(8,128)(2,1)}, bf16[16,4096]{1,0:T(8,128)(2,1)S(1)}, u32[]{:S(2)}, u32[]{:S(2)}) %collective-permute-start.1) | collective-permute-done | bytes 131104 | tf_op jit(solution)/shard_map/ppermute | solution.py:106
  7.3 0.0 collective-permute-start.2
  7.3 0.7 %and_select_fusion.1 = (s32[1,24]{1,0:T(1,128)S(1)}, s32[1,24]{1,0:T(1,128)S(1)}) fusion(s32[1,24]{1,0:T(1,128)} %param.12, s32[]{:T(128)} %bitcast.26), kind=kLoop, calls=%fused_computation.21 | loop fusion | flops 336 | bytes 292 | tf_op jit(solution)/shard_map/jit(floor_divide)/jit(_where)/select_n | solution.py:123
  8.0 1.6 %stage.1 = (bf16[16,4096]{1,0:T(8,128)(2,1)S(1)}, bf16[64,3584]{1,0:T(8,128)(2,1)S(1)}, bf16[24,128,256]{2,1,0:T(8,128)(2,1)S(1)}) custom-call(bf16[16,4096]{1,0:T(8,128)(2,1)} %bitcast.32, bf16[64,3584]{1,0:T(8,128)(2,1)} %bitcast.29, bf16[24,128,128]{2,1,0:T(8,128)(2,1)} %bitcast.27, bf16[24,128,128]{2,1,0:T(8,128)(2,1)} %bitcast.28), custom_call_target="tpu_custom_call" | custom-call | tf_op jit(solution)/shard_map/stage/pallas_call | solution.py:129
  9.6 0.0 collective-permute-done.refs_1_
  9.6 0.0 collective-permute-done.2.refs_3_
  9.6 2.3 %forward_back.1 = (bf16[64,4096]{1,0:T(8,128)(2,1)S(1)}, bf16[29,64,256]{2,1,0:T(8,128)(2,1)S(1)}, f32[16,4096]{1,0:T(8,128)S(1)}, f32[16,4096]{1,0:T(8,128)S(1)}, bf16[2,16,4096]{2,1,0:T(8,128)(2,1)S(1)}) custom-call(s32[2,24]{1,0:T(2,128)S(1)} %pad_add_fusion.table_ref, s32[1]{0:T(128)} %bitcast.1.place_ref, ...), custom_call_target="tpu_custom_call" | custom-call | tf_op jit(solution)/shard_map/forward_back/pallas_call | solution.py:158
  11.9 0.6 %collective-permute-start.3 = (bf16[2,16,4096]{2,1,0:T(8,128)(2,1)S(1)}, bf16[2,16,4096]{2,1,0:T(8,128)(2,1)S(1)}, u32[]{:S(2)}, u32[]{:S(2)}) collective-permute-start(bf16[2,16,4096]{2,1,0:T(8,128)(2,1)S(1)} %get-tuple-element.17), channel_id=1, source_target_pairs={{0,1},{1,0},{2,3},{3,2},{4,5},{5,4},{6,7},{7,6},{8,9},{9,8},{10,11... | collective-permute-start | bytes 786440 | tf_op jit(solution)/shard_map/ppermute | solution.py:106
  12.4 1.2 %collective-permute-done.3 = bf16[2,16,4096]{2,1,0:T(8,128)(2,1)S(1)} collective-permute-done((bf16[2,16,4096]{2,1,0:T(8,128)(2,1)S(1)}, bf16[2,16,4096]{2,1,0:T(8,128)(2,1)S(1)}, u32[]{:S(2)}, u32[]{:S(2)}) %collective-permute-start.3) | collective-permute-done | bytes 262176 | tf_op jit(solution)/shard_map/ppermute | solution.py:106
  13.6 1.8 %collective-permute-start.4 = (bf16[16,4096]{1,0:T(8,128)(2,1)S(1)}, bf16[16,4096]{1,0:T(8,128)(2,1)S(1)}, u32[]{:S(2)}, u32[]{:S(2)}) collective-permute-start(bf16[16,4096]{1,0:T(8,128)(2,1)S(1)} %fusion.6), channel_id=1, source_target_pairs={{0,2},{1,3},{2,0},{3,1},{4,6},{5,7},{6,4},{7,5},{8,10},{9,11},{10,... | collective-permute-start | bytes 393224 | tf_op jit(solution)/shard_map/ppermute | solution.py:106
  15.5 4.0 %collective-permute-done.4 = bf16[16,4096]{1,0:T(8,128)(2,1)S(1)} collective-permute-done((bf16[16,4096]{1,0:T(8,128)(2,1)S(1)}, bf16[16,4096]{1,0:T(8,128)(2,1)S(1)}, u32[]{:S(2)}, u32[]{:S(2)}) %collective-permute-start.4) | collective-permute-done | bytes 131104 | tf_op jit(solution)/shard_map/ppermute | solution.py:106
  19.5 1.8 %collective-permute-start.5 = (bf16[16,4096]{1,0:T(8,128)(2,1)S(1)}, bf16[16,4096]{1,0:T(8,128)(2,1)S(1)}, u32[]{:S(2)}, u32[]{:S(2)}) collective-permute-start(bf16[16,4096]{1,0:T(8,128)(2,1)S(1)} %fusion.9), channel_id=1, source_target_pairs={{0,4},{4,0},{8,12},{12,8},{16,20},{20,16},{24,28},{28,24},{1,5},{5... | collective-permute-start | bytes 393224 | tf_op jit(solution)/shard_map/ppermute | solution.py:106
  21.4 1.6 %collective-permute-start.6 = (bf16[16,4096]{1,0:T(8,128)(2,1)S(1)}, bf16[16,4096]{1,0:T(8,128)(2,1)S(1)}, u32[]{:S(2)}, u32[]{:S(2)}) collective-permute-start(bf16[16,4096]{1,0:T(8,128)(2,1)S(1)} %fusion.9), channel_id=1, source_target_pairs={{0,8},{4,12},{8,0},{12,4},{16,24},{20,28},{24,16},{28,20},{1,9},{5... | collective-permute-start | bytes 393224 | tf_op jit(solution)/shard_map/ppermute | solution.py:106
  22.9 0.1 collective-permute-start.7
  23.1 1.5 %collective-permute-done.5 = bf16[16,4096]{1,0:T(8,128)(2,1)S(1)} collective-permute-done((bf16[16,4096]{1,0:T(8,128)(2,1)S(1)}, bf16[16,4096]{1,0:T(8,128)(2,1)S(1)}, u32[]{:S(2)}, u32[]{:S(2)}) %collective-permute-start.5) | collective-permute-done | bytes 131104 | tf_op jit(solution)/shard_map/ppermute | solution.py:106
  24.6 2.9 %collective-permute-done.6 = bf16[16,4096]{1,0:T(8,128)(2,1)S(1)} collective-permute-done((bf16[16,4096]{1,0:T(8,128)(2,1)S(1)}, bf16[16,4096]{1,0:T(8,128)(2,1)S(1)}, u32[]{:S(2)}, u32[]{:S(2)}) %collective-permute-start.6) | collective-permute-done | bytes 131104 | tf_op jit(solution)/shard_map/ppermute | solution.py:106
  27.5 1.4 %collective-permute-done.7 = bf16[16,4096]{1,0:T(8,128)(2,1)S(1)} collective-permute-done((bf16[16,4096]{1,0:T(8,128)(2,1)S(1)}, bf16[16,4096]{1,0:T(8,128)(2,1)S(1)}, u32[]{:S(2)}, u32[]{:S(2)}) %collective-permute-start.7) | collective-permute-done | bytes 131104 | tf_op jit(solution)/shard_map/ppermute | solution.py:106
  28.8 0.1 fusion.5
  29.0 3.6 %collective-permute-start.8 = (bf16[16,4096]{1,0:T(8,128)(2,1)S(1)}, bf16[16,4096]{1,0:T(8,128)(2,1)S(1)}, u32[]{:S(2)}, u32[]{:S(2)}) collective-permute-start(bf16[16,4096]{1,0:T(8,128)(2,1)S(1)} %fusion.5), channel_id=1, source_target_pairs={{0,24},{4,28},{8,16},{12,20},{16,8},{20,12},{24,0},{28,4},{1,25},{... | collective-permute-start | bytes 393224 | tf_op jit(solution)/shard_map/ppermute | solution.py:106
  32.6 2.3 %weight_grads.1 = (bf16[24,128,128]{2,1,0:T(8,128)(2,1)}, bf16[24,128,128]{2,1,0:T(8,128)(2,1)}) custom-call(s32[2,24]{1,0:T(2,128)S(1)} %pad_add_fusion.table_ref, bf16[64,4096]{1,0:T(8,128)(2,1)S(1)} %get-tuple-element.19.x_ref, bf16[29,64,256]{2,1,0:T(8,128)(2,1)S(1)} %get-tuple-element.20.cot_ref), custom_call_target="tpu_custom_call" | custom-call | tf_op jit(solution)/shard_map/weight_grads/pallas_call | solution.py:175
  34.9 1.0 %collective-permute-done.8 = bf16[16,4096]{1,0:T(8,128)(2,1)S(1)} collective-permute-done((bf16[16,4096]{1,0:T(8,128)(2,1)S(1)}, bf16[16,4096]{1,0:T(8,128)(2,1)S(1)}, u32[]{:S(2)}, u32[]{:S(2)}) %collective-permute-start.8) | collective-permute-done | bytes 131104 | tf_op jit(solution)/shard_map/ppermute | solution.py:106
  35.9 0.8 %fusion.8 = bf16[1,16,4096]{2,1,0:T(8,128)(2,1)} fusion(bf16[16,4096]{1,0:T(8,128)(2,1)S(1)} %collective-permute-done.8, bf16[16,4096]{1,0:T(8,128)(2,1)S(1)} %collective-permute-done.7, bf16[16,4096]{1,0:T(8,128)(2,1)S(1)} %collective-permute-done.6, bf16[16,4096]{1,0:T(8,128)(2,1)S(1)} %collective-permute-done.5, bf16[16,4096]{1,0:T(8,128)(2,1)S(1)} %copy-done, ...), kind=kLoop, calls=%fused_computation.18 | loop fusion | flops 1245184 | bytes 1310724 | tf_op jit(solution)/shard_map/broadcast_in_dim | solution.py:214
  (5 shorter events, 0.1 us)
Async XLA Ops:
  0.6 6.7 %collective-permute-start.1 = (bf16[16,4096]{1,0:T(8,128)(2,1)}, bf16[16,4096]{1,0:T(8,128)(2,1)S(1)}, u32[]{:S(2)}, u32[]{:S(2)}) collective-permute-start(bf16[16,4096]{1,0:T(8,128)(2,1)} %bitcast.30), channel_id=1, source_target_pairs={{0,2},{1,3},{2,0},{3,1},{4,6},{5,7},{6,4},{7,5},{8,10},{9,11},{10,... | collective-permute-start | bytes 393224 | tf_op jit(solution)/shard_map/ppermute | solution.py:106
  3.6 6.0 %collective-permute-start = (bf16[16,4096]{1,0:T(8,128)(2,1)}, bf16[16,4096]{1,0:T(8,128)(2,1)S(1)}, u32[]{:S(2)}, u32[]{:S(2)}) collective-permute-start(bf16[16,4096]{1,0:T(8,128)(2,1)} %bitcast.31), channel_id=1, source_target_pairs={{0,1},{1,0},{2,3},{3,2},{4,5},{5,4},{6,7},{7,6},{8,9},{9,8},{10,11... | collective-permute-start | bytes 393224 | tf_op jit(solution)/shard_map/ppermute | solution.py:106
  7.3 2.3 %collective-permute-start.2 = (bf16[16,4096]{1,0:T(8,128)(2,1)S(1)}, bf16[16,4096]{1,0:T(8,128)(2,1)S(1)}, u32[]{:S(2)}, u32[]{:S(2)}) collective-permute-start(bf16[16,4096]{1,0:T(8,128)(2,1)S(1)} %collective-permute-done.1.refs_2_), channel_id=1, source_target_pairs={{0,1},{1,0},{2,3},{3,2},{4,5},{5,4},{6,7},{7,6},{8,9},{9,8},{10,11... | collective-permute-start | bytes 393224 | tf_op jit(solution)/shard_map/ppermute | solution.py:106
  11.9 1.7 %collective-permute-start.3 = (bf16[2,16,4096]{2,1,0:T(8,128)(2,1)S(1)}, bf16[2,16,4096]{2,1,0:T(8,128)(2,1)S(1)}, u32[]{:S(2)}, u32[]{:S(2)}) collective-permute-start(bf16[2,16,4096]{2,1,0:T(8,128)(2,1)S(1)} %get-tuple-element.17), channel_id=1, source_target_pairs={{0,1},{1,0},{2,3},{3,2},{4,5},{5,4},{6,7},{7,6},{8,9},{9,8},{10,11... | collective-permute-start | bytes 786440 | tf_op jit(solution)/shard_map/ppermute | solution.py:106
  13.6 5.8 %collective-permute-start.4 = (bf16[16,4096]{1,0:T(8,128)(2,1)S(1)}, bf16[16,4096]{1,0:T(8,128)(2,1)S(1)}, u32[]{:S(2)}, u32[]{:S(2)}) collective-permute-start(bf16[16,4096]{1,0:T(8,128)(2,1)S(1)} %fusion.6), channel_id=1, source_target_pairs={{0,2},{1,3},{2,0},{3,1},{4,6},{5,7},{6,4},{7,5},{8,10},{9,11},{10,... | collective-permute-start | bytes 393224 | tf_op jit(solution)/shard_map/ppermute | solution.py:106
  19.5 16.4 %copy-start = (bf16[16,4096]{1,0:T(8,128)(2,1)S(1)}, bf16[16,4096]{1,0:T(8,128)(2,1)}, u32[]{:S(2)}) copy-start(bf16[16,4096]{1,0:T(8,128)(2,1)} %param.9) | copy-start | bytes 393220
  19.5 5.1 %collective-permute-start.5 = (bf16[16,4096]{1,0:T(8,128)(2,1)S(1)}, bf16[16,4096]{1,0:T(8,128)(2,1)S(1)}, u32[]{:S(2)}, u32[]{:S(2)}) collective-permute-start(bf16[16,4096]{1,0:T(8,128)(2,1)S(1)} %fusion.9), channel_id=1, source_target_pairs={{0,4},{4,0},{8,12},{12,8},{16,20},{20,16},{24,28},{28,24},{1,5},{5... | collective-permute-start | bytes 393224 | tf_op jit(solution)/shard_map/ppermute | solution.py:106
  21.4 6.1 %collective-permute-start.6 = (bf16[16,4096]{1,0:T(8,128)(2,1)S(1)}, bf16[16,4096]{1,0:T(8,128)(2,1)S(1)}, u32[]{:S(2)}, u32[]{:S(2)}) collective-permute-start(bf16[16,4096]{1,0:T(8,128)(2,1)S(1)} %fusion.9), channel_id=1, source_target_pairs={{0,8},{4,12},{8,0},{12,4},{16,24},{20,28},{24,16},{28,20},{1,9},{5... | collective-permute-start | bytes 393224 | tf_op jit(solution)/shard_map/ppermute | solution.py:106
  22.9 5.9 %collective-permute-start.7 = (bf16[16,4096]{1,0:T(8,128)(2,1)S(1)}, bf16[16,4096]{1,0:T(8,128)(2,1)S(1)}, u32[]{:S(2)}, u32[]{:S(2)}) collective-permute-start(bf16[16,4096]{1,0:T(8,128)(2,1)S(1)} %fusion.9), channel_id=1, source_target_pairs={{0,12},{4,8},{8,4},{12,0},{16,28},{20,24},{24,20},{28,16},{1,13},{... | collective-permute-start | bytes 393224 | tf_op jit(solution)/shard_map/ppermute | solution.py:106
  29.0 6.9 %collective-permute-start.8 = (bf16[16,4096]{1,0:T(8,128)(2,1)S(1)}, bf16[16,4096]{1,0:T(8,128)(2,1)S(1)}, u32[]{:S(2)}, u32[]{:S(2)}) collective-permute-start(bf16[16,4096]{1,0:T(8,128)(2,1)S(1)} %fusion.5), channel_id=1, source_target_pairs={{0,24},{4,28},{8,16},{12,20},{16,8},{20,12},{24,0},{28,4},{1,25},{... | collective-permute-start | bytes 393224 | tf_op jit(solution)/shard_map/ppermute | solution.py:106

commit v3 on v2

v3 whole, which is shorter than its diff:
```python
import functools

import jax
import jax.numpy as jnp
from jax import lax
from jax.experimental import pallas as pl
from jax.experimental.pallas import tpu as pltpu
from jax.sharding import PartitionSpec as P

F32 = jnp.float32
BF16 = jnp.bfloat16
PARTS = 4


def _shift_and_factor(divisor, limit):
    for shift in range(31):
        factor = -(-(1 << shift) // divisor)
        if factor * limit < 1 << 31 and all(
            (p * factor) >> shift == p // divisor for p in range(limit)
        ):
            return factor, shift
    raise ValueError(divisor)


def _slot(position_ref, live_ref, slot, col_blocks, row_blocks):
    factor, shift = _shift_and_factor(col_blocks, col_blocks * row_blocks)
    position = position_ref[0, slot]
    row = (position * factor) >> shift
    col = position - row * col_blocks
    return row, jnp.where(slot < live_ref[0, 0], col, col_blocks)


def _term(blk, table, grad, weight_ref, ready, x_ref, cot_ref, act_ref, back_ref):
    col_blocks = cot_ref.shape[0] - 1
    slots = len(table)
    for slot, (row, col) in enumerate(table):
        ready(slot)
        start = pl.multiple_of(row * blk, blk)
        act_ref[col] += jnp.dot(
            x_ref[:, pl.ds(start, blk)], weight_ref[slot], preferred_element_type=F32
        )
    for col in range(col_blocks):
        gate = act_ref[col, :, :blk]
        up = act_ref[col, :, blk:]
        upstream = grad(col).astype(F32)
        sig = jax.nn.sigmoid(gate)
        scaled = upstream * sig
        cot_ref[col, :, :blk] = (scaled * up * (1.0 + gate * (1.0 - sig))).astype(BF16)
        cot_ref[col, :, blk:] = (scaled * gate).astype(BF16)
    cot_ref[col_blocks] = jnp.zeros_like(cot_ref[col_blocks])
    for slot in range(slots):
        row, col = table[slot]
        back_ref[row] += lax.dot_general(
            cot_ref[col], weight_ref[slot], (((1,), (1,)), ((), ())), preferred_element_type=F32
        )


def _write_rows(back_ref, start, count, target):
    blk = back_ref.shape[2]
    for row in range(back_ref.shape[0]):
        target[:, row * blk : (row + 1) * blk] = back_ref[row, pl.ds(start, count), :].astype(
            target.dtype
        )


def _near_half(
    blk,
    position_ref,
    live_ref,
    own_in,
    beside_ref,
    grad_in,
    wg_in,
    wu_in,
    x_ref,
    cot_ref,
    keep_ref,
    send_ref,
    weight_ref,
    far_grad_ref,
    grad_ref,
    act_ref,
    back_ref,
    sems,
):
    me = lax.axis_index("tp")
    core, chip = me & 1, me >> 1
    count = own_in.shape[0]
    slots = wg_in.shape[0]
    part = slots // PARTS
    rows = 2 * count
    mine = pl.multiple_of(core * count, count)
    other = pl.multiple_of((core ^ 1) * count, count)
    near = pl.multiple_of(chip * rows, rows)
    far = pl.multiple_of((chip ^ 1) * rows, rows)
    own = pltpu.make_async_copy(own_in, x_ref.at[pl.ds(mine, count), :], sems.at[0])
    near_grad = pltpu.make_async_copy(grad_in.at[pl.ds(near, rows), :], grad_ref, sems.at[1])
    far_grad = pltpu.make_async_copy(grad_in.at[pl.ds(far, rows), :], far_grad_ref, sems.at[2])
    blocks = []
    for index in range(PARTS):
        span = pl.ds(index * part, part)
        blocks.append(
            [
                pltpu.make_async_copy(
                    wg_in.at[span], weight_ref.at[span, :, pl.ds(0, blk)], sems.at[3 + 2 * index]
                ),
                pltpu.make_async_copy(
                    wu_in.at[span], weight_ref.at[span, :, pl.ds(blk, blk)], sems.at[4 + 2 * index]
                ),
            ]
        )
    for copy in (own, *blocks[0], near_grad, *sum(blocks[1:], []), far_grad):
        copy.start()
    x_ref[pl.ds(other, count), :] = beside_ref[...]
    act_ref[...] = jnp.zeros_like(act_ref)
    back_ref[...] = jnp.zeros_like(back_ref)
    own.wait()
    table = [
        _slot(position_ref, live_ref, slot, cot_ref.shape[0] - 1, back_ref.shape[0])
        for slot in range(slots)
    ]

    def ready(slot):
        if slot % part == 0:
            for copy in blocks[slot // part]:
                copy.wait()

    def grad(col):
        if col == 0:
            near_grad.wait()
        return grad_ref[:, col * blk : (col + 1) * blk]

    _term(blk, table, grad, weight_ref, ready, x_ref, cot_ref, act_ref, back_ref)
    _write_rows(back_ref, mine, count, keep_ref)
    _write_rows(back_ref, other, count, send_ref)
    far_grad.wait()


def _far_half(
    blk,
    position_ref,
    live_ref,
    across_ref,
    beyond_ref,
    grad_ref,
    weight_ref,
    x_ref,
    cot_ref,
    far_ref,
    send_ref,
    act_ref,
    back_ref,
):
    me = lax.axis_index("tp")
    core = me & 1
    count = across_ref.shape[0]
    mine = pl.multiple_of(core * count, count)
    other = pl.multiple_of((core ^ 1) * count, count)
    x_ref[pl.ds(mine, count), :] = across_ref[...]
    x_ref[pl.ds(other, count), :] = beyond_ref[...]
    act_ref[...] = jnp.zeros_like(act_ref)
    back_ref[...] = jnp.zeros_like(back_ref)
    table = [
        _slot(position_ref, live_ref, slot, cot_ref.shape[0] - 1, back_ref.shape[0])
        for slot in range(weight_ref.shape[0])
    ]

    def grad(col):
        return grad_ref[:, col * blk : (col + 1) * blk]

    _term(blk, table, grad, weight_ref, lambda slot: None, x_ref, cot_ref, act_ref, back_ref)
    _write_rows(back_ref, other, count, send_ref)
    _write_rows(back_ref, mine, count, far_ref)


def _whole(
    blk,
    position_ref,
    live_ref,
    x_ref,
    grad_ref,
    wg_ref,
    wu_ref,
    cot_ref,
    term_ref,
    weight_ref,
    act_ref,
    back_ref,
):
    weight_ref[:, :, :blk] = wg_ref[...]
    weight_ref[:, :, blk:] = wu_ref[...]
    act_ref[...] = jnp.zeros_like(act_ref)
    back_ref[...] = jnp.zeros_like(back_ref)
    table = [
        _slot(position_ref, live_ref, slot, cot_ref.shape[0] - 1, back_ref.shape[0])
        for slot in range(weight_ref.shape[0])
    ]

    def grad(col):
        return grad_ref[:, col * blk : (col + 1) * blk]

    _term(blk, table, grad, weight_ref, lambda slot: None, x_ref, cot_ref, act_ref, back_ref)
    _write_rows(back_ref, 0, x_ref.shape[0], term_ref)


def _weight_grads(blk, halves, position_ref, live_ref, *refs):
    x_refs, cot_refs, (gate_ref, up_ref) = refs[:halves], refs[halves : 2 * halves], refs[-2:]
    for slot in range(gate_ref.shape[0]):
        row, col = _slot(
            position_ref, live_ref, slot, cot_refs[0].shape[0] - 1, x_refs[0].shape[1] // blk
        )
        start = pl.multiple_of(row * blk, blk)
        grads = lax.dot_general(
            jnp.concatenate([x_ref[:, pl.ds(start, blk)] for x_ref in x_refs], axis=0),
            jnp.concatenate([cot_ref[col] for cot_ref in cot_refs], axis=0),
            (((0,), (0,)), ((), ())),
            preferred_element_type=F32,
        )
        gate_ref[slot] = grads[:, :blk].astype(BF16)
        up_ref[slot] = grads[:, blk:].astype(BF16)


_pinned = pltpu.with_memory_space_constraint


def _swap(array, axis, distance):
    count = lax.axis_size(axis)
    return lax.ppermute(array, axis, [(i, i ^ distance) for i in range(count)])


def _params(mib):
    return pltpu.CompilerParams(vmem_limit_bytes=mib << 20)


def local(inputs, hidden_grad, top_grad, w_gate, w_up, block_pos, live_count):
    own_rows = inputs[0]
    count, width = own_rows.shape
    slots, blk = w_gate.shape[1], w_gate.shape[2]
    hidden = hidden_grad.shape[2]
    col_blocks, row_blocks = hidden // blk, width // blk
    tp = lax.axis_size("tp")
    sections = lax.axis_size("section")
    section = lax.axis_index("section")

    vmem = pl.BlockSpec(memory_space=pltpu.VMEM)
    smem = pl.BlockSpec(memory_space=pltpu.SMEM)
    hbm = pl.BlockSpec(memory_space=pltpu.HBM)
    struct = jax.ShapeDtypeStruct

    def cots(rows):
        return struct((col_blocks + 1, rows, 2 * blk), BF16)

    def sums(rows):
        return [
            pltpu.VMEM((col_blocks + 1, rows, 2 * blk), F32),
            pltpu.VMEM((row_blocks, rows, blk), F32),
        ]

    if tp == 4 and slots % PARTS == 0:
        rows = 2 * count
        across = _swap(own_rows, "tp", 2)
        beside = _swap(own_rows, "tp", 1)
        near_x, near_cot, keep, near_send, weights, far_grad = pl.pallas_call(
            functools.partial(_near_half, blk),
            out_shape=(
                struct((rows, width), BF16),
                cots(rows),
                struct((count, width), F32),
                struct((count, width), BF16),
                struct((slots, blk, 2 * blk), BF16),
                struct((rows, hidden), BF16),
            ),
            in_specs=[smem, smem, hbm, vmem, hbm, hbm, hbm],
            out_specs=[vmem] * 6,
            scratch_shapes=[
                pltpu.VMEM((rows, hidden), BF16),
                *sums(rows),
                pltpu.SemaphoreType.DMA((3 + 2 * PARTS,)),
            ],
            compiler_params=_params(10),
            name="near_half",
        )(
            block_pos,
            live_count,
            _pinned(own_rows, pltpu.HBM),
            beside,
            *(_pinned(array[0], pltpu.HBM) for array in (hidden_grad, w_gate, w_up)),
        )
        across, near_send = lax.optimization_barrier((across, near_send))
        beyond = _swap(across, "tp", 1)
        far_x, far_cot, far, far_send = pl.pallas_call(
            functools.partial(_far_half, blk),
            out_shape=(
                struct((rows, width), BF16),
                cots(rows),
                struct((count, width), F32),
                struct((count, width), BF16),
            ),
            in_specs=[smem, smem] + [vmem] * 4,
            out_specs=[vmem] * 4,
            scratch_shapes=sums(rows),
            compiler_params=_params(10),
            name="far_half",
        )(block_pos, live_count, across, beyond, far_grad, weights)
        near_came = _swap(near_send, "tp", 1)
        far_came = _swap(far_send, "tp", 1)
        crossed = _swap((far + far_came.astype(F32)).astype(BF16), "tp", 2)
        own_term = keep + near_came.astype(F32) + crossed.astype(F32)
        x_parts, cot_parts = (near_x, far_x), (near_cot, far_cot)
    else:
        rows = tp * count
        gathered = lax.all_gather(own_rows, "tp", axis=0, tiled=True)
        cot, term = pl.pallas_call(
            functools.partial(_whole, blk),
            out_shape=(cots(rows), struct((rows, width), BF16)),
            in_specs=[smem, smem] + [vmem] * 4,
            out_specs=[vmem] * 2,
            scratch_shapes=[pltpu.VMEM((slots, blk, 2 * blk), BF16), *sums(rows)],
            compiler_params=_params(24),
            name="whole",
        )(block_pos, live_count, gathered, hidden_grad[0], w_gate[0], w_up[0])
        own_term = lax.psum_scatter(term, "tp", scatter_dimension=0, tiled=True).astype(F32)
        x_parts, cot_parts = (gathered,), (cot,)

    gate_gradient, up_gradient = pl.pallas_call(
        functools.partial(_weight_grads, blk, len(x_parts)),
        out_shape=(struct((slots, blk, blk), BF16),) * 2,
        in_specs=[smem, smem] + [vmem] * (2 * len(x_parts)),
        out_specs=[vmem, vmem],
        compiler_params=_params(8),
        name="weight_grads",
    )(block_pos, live_count, *x_parts, *cot_parts)

    total = own_term
    result = top_grad.astype(F32) + own_term
    if sections & (sections - 1) == 0:
        block = min(sections, 4)
        sent = own_term.astype(BF16)
        for step in range(1, block):
            other = _swap(sent, "section", step).astype(F32)
            result = result + jnp.where((section ^ step) > section, other, 0.0)
            total = total + other
        while block < sections:
            other = _swap(total.astype(BF16), "section", block ^ (block >> 1)).astype(F32)
            result = result + jnp.where(section & block == 0, other, 0.0)
            total = total + other
            block *= 2
    else:
        distance = 1
        while distance < sections:
            moves = [(i, i - distance) for i in range(distance, sections)]
            total = total + lax.ppermute(total.astype(BF16), "section", moves).astype(F32)
            distance *= 2
        result = top_grad.astype(F32) + total
    return (
        result.astype(BF16)[None],
        gate_gradient[None],
        up_gradient[None],
    )


def solution(mesh):
    in_specs = (
        P("section", "tp", None),
        P("section", None, "tp"),
        P("tp", None),
        P("section", "tp", None, None),
        P("section", "tp", None, None),
        P("section", "tp"),
        P("section", "tp"),
    )
    out_specs = (
        P("section", "tp", None),
        P("section", "tp", None, None),
        P("section", "tp", None, None),
    )
    return jax.shard_map(local, mesh=mesh, in_specs=in_specs, out_specs=out_specs, check_vma=False)
```

time: 36.9 us -> 36.2 us (0.981)
  waiting for transfers between devices: 15 us -> 13.5 us
  Pallas kernels: 6.12 us -> 7.5 us
  other arithmetic: 1.7 us -> 1 us
  local copies, waits for them, and re-layouts: 0.01 us -> 0.66 us
  starting transfers between devices: 12.6 us -> 12 us
    ppermute x9 -> x10, waiting for transfers between devices: 15 us -> 13.5 us  [_swap(): return lax.ppermute(array, axis, [(i, i ^ distance) for i in range(count)])]
    pallas_call x3, Pallas kernels: 6.12 us -> 7.5 us  [the longest x1 3.4 us: local(): pl.pallas_call(functools.partial(_near_half, blk), out_shape=(struct((row...]
    select_n x1 -> x0, other arithmetic: 0.67 us -> none  [local(): position // col_blocks]
    unnamed x2 -> x6, local copies, waits for them, and re-layouts: 0.01 us -> 0.66 us
    ppermute x9 -> x10, starting transfers between devices: 12.6 us -> 12 us  [_swap(): return lax.ppermute(array, axis, [(i, i ^ distance) for i in range(count)])]
  transfers between devices with their start and end apart: 9 -> 10, of which waited for: 7 -> 7; matrix products, arithmetic and copies ran while one was open for 2% -> 0% of each run, Pallas kernels for 11% -> 16%
where the time goes in v3:
time: 36.2 us; the launch traced here: 36 us
  waiting for transfers between devices  13.5 us (37%)
  starting transfers between devices  12 us (33%)
  Pallas kernels  7.5 us (21%)
  between operations  1.35 us (4%)
  other arithmetic  1 us (3%)
  local copies, waits for them, and re-layouts  0.66 us (2%)
    ppermute x10, waiting for transfers between devices, _swap(): return lax.ppermute(array, axis, [(i, i ^ distance) for i in range(count)])  13.5 us
    ppermute x10, starting transfers between devices, _swap(): return lax.ppermute(array, axis, [(i, i ^ distance) for i in range(count)])  12 us
    pallas_call x1, Pallas kernels, local(): pl.pallas_call(functools.partial(_near_half, blk), out_shape=(struct((row...  3.4 us
    pallas_call x1, Pallas kernels, local(): pl.pallas_call(functools.partial(_weight_grads, blk, len(x_parts)), out_s...  2.29 us
    pallas_call x1, Pallas kernels, local(): pl.pallas_call(functools.partial(_far_half, blk), out_shape=(struct((rows...  1.8 us
    broadcast_in_dim x1, other arithmetic, local(): return (result.astype(BF16)[None], gate_gradient[None], up_gradient[None])  0.83 us
  transfers between devices with their start and end apart: 10, of which 7 were waited for; matrix products, arithmetic and copies ran while one was open for 0% of the time, Pallas kernels for 16%

profile of v3, /device:TPU:0, one launch (start us, length us, event | category | flops | bytes accessed | tf_op | source)
XLA Modules:
  0.0 36.0 jit_solution(9142440727483432387)
XLA Ops:
  0.6 0.5 %collective-permute-start = (bf16[16,4096]{1,0:T(8,128)(2,1)}, bf16[16,4096]{1,0:T(8,128)(2,1)S(1)}, u32[]{:S(2)}, u32[]{:S(2)}) collective-permute-start(bf16[16,4096]{1,0:T(8,128)(2,1)} %bitcast.11), channel_id=1, source_target_pairs={{0,1},{1,0},{2,3},{3,2},{4,5},{5,4},{6,7},{7,6},{8,9},{9,8},{10,11... | collective-permute-start | bytes 393224 | tf_op jit(solution)/shard_map/ppermute | solution.py:228
  1.2 2.6 %collective-permute-start.1 = (bf16[16,4096]{1,0:T(8,128)(2,1)}, bf16[16,4096]{1,0:T(8,128)(2,1)S(1)}, u32[]{:S(2)}, u32[]{:S(2)}) collective-permute-start(bf16[16,4096]{1,0:T(8,128)(2,1)} %bitcast.12), channel_id=1, source_target_pairs={{0,2},{1,3},{2,0},{3,1},{4,6},{5,7},{6,4},{7,5},{8,10},{9,11},{10,... | collective-permute-start | bytes 393224 | tf_op jit(solution)/shard_map/ppermute | solution.py:228
  4.4 0.6 %copy-done = s32[1,24]{1,0:T(1,128)S(1)} copy-done((s32[1,24]{1,0:T(1,128)S(1)}, s32[1,24]{1,0:T(1,128)}, u32[]{:S(2)}) %copy-start) | copy-done | bytes 120
  5.0 3.4 %near_half.1 = (bf16[32,4096]{1,0:T(8,128)(2,1)S(1)}, bf16[29,32,256]{2,1,0:T(8,128)(2,1)S(1)}, f32[16,4096]{1,0:T(8,128)S(1)}, bf16[16,4096]{1,0:T(8,128)(2,1)S...) custom-call(s32[1,24]{1,0:T(1,128)S(1)} %copy-done, s32[1,1]{1,0:T(1,128)S(6)} %copy.10.live_ref, ...), custom_call_target="tpu_custom_call" | custom-call | tf_op jit(solution)/shard_map/near_half/pallas_call | solution.py:263
  8.5 0.2 collective-permute-start.3
  8.7 1.2 %collective-permute-done.3.beyond_ref = bf16[16,4096]{1,0:T(8,128)(2,1)S(1)} collective-permute-done((bf16[16,4096]{1,0:T(8,128)(2,1)S(1)}, bf16[16,4096]{1,0:T(8,128)(2,1)S(1)}, u32[]{:S(2)}, u32[]{:S(2)}) %collective-permute-start.3) | collective-permute-done | bytes 131104 | tf_op jit(solution)/shard_map/ppermute | solution.py:228
  9.9 1.8 %far_half.1 = (bf16[32,4096]{1,0:T(8,128)(2,1)S(1)}, bf16[29,32,256]{2,1,0:T(8,128)(2,1)S(1)}, f32[16,4096]{1,0:T(8,128)S(1)}, bf16[16,4096]{1,0:T(8,128)(2,1)S(1)}) custom-call(s32[1,24]{1,0:T(1,128)S(1)} %copy-done.1, s32[1,1]{1,0:T(1,128)S(6)} %copy.10.live_ref, bf16[16,4096]{1,0:T(8,128)(2,1)S(1)} %collective-permute-done.1.across_ref, ...), custom_call_target="tpu_custom_call" | custom-call | tf_op jit(solution)/shard_map/far_half/pallas_call | solution.py:291
  11.7 0.2 collective-permute-start.4
  11.9 0.4 collective-permute-start.2
  12.3 0.8 %collective-permute-done.4 = bf16[16,4096]{1,0:T(8,128)(2,1)S(1)} collective-permute-done((bf16[16,4096]{1,0:T(8,128)(2,1)S(1)}, bf16[16,4096]{1,0:T(8,128)(2,1)S(1)}, u32[]{:S(2)}, u32[]{:S(2)}) %collective-permute-start.4) | collective-permute-done | bytes 131104 | tf_op jit(solution)/shard_map/ppermute | solution.py:228
  13.1 1.3 %collective-permute-start.5 = (bf16[16,4096]{1,0:T(8,128)(2,1)S(1)}, bf16[16,4096]{1,0:T(8,128)(2,1)S(1)}, u32[]{:S(2)}, u32[]{:S(2)}) collective-permute-start(bf16[16,4096]{1,0:T(8,128)(2,1)S(1)} %add_convert_fusion), channel_id=1, source_target_pairs={{0,2},{1,3},{2,0},{3,1},{4,6},{5,7},{6,4},{7,5},{8,10},{9,11},{10,... | collective-permute-start | bytes 393224 | tf_op jit(solution)/shard_map/ppermute | solution.py:228
  14.5 4.3 %collective-permute-done.5 = bf16[16,4096]{1,0:T(8,128)(2,1)S(1)} collective-permute-done((bf16[16,4096]{1,0:T(8,128)(2,1)S(1)}, bf16[16,4096]{1,0:T(8,128)(2,1)S(1)}, u32[]{:S(2)}, u32[]{:S(2)}) %collective-permute-start.5) | collective-permute-done | bytes 131104 | tf_op jit(solution)/shard_map/ppermute | solution.py:228
  18.8 0.1 fusion.7
  18.8 1.6 %collective-permute-start.6 = (bf16[16,4096]{1,0:T(8,128)(2,1)S(1)}, bf16[16,4096]{1,0:T(8,128)(2,1)S(1)}, u32[]{:S(2)}, u32[]{:S(2)}) collective-permute-start(bf16[16,4096]{1,0:T(8,128)(2,1)S(1)} %fusion.7), channel_id=1, source_target_pairs={{0,4},{4,0},{8,12},{12,8},{16,20},{20,16},{24,28},{28,24},{1,5},{5... | collective-permute-start | bytes 393224 | tf_op jit(solution)/shard_map/ppermute | solution.py:228
  20.4 1.6 %collective-permute-start.7 = (bf16[16,4096]{1,0:T(8,128)(2,1)S(1)}, bf16[16,4096]{1,0:T(8,128)(2,1)S(1)}, u32[]{:S(2)}, u32[]{:S(2)}) collective-permute-start(bf16[16,4096]{1,0:T(8,128)(2,1)S(1)} %fusion.7), channel_id=1, source_target_pairs={{0,8},{4,12},{8,0},{12,4},{16,24},{20,28},{24,16},{28,20},{1,9},{5... | collective-permute-start | bytes 393224 | tf_op jit(solution)/shard_map/ppermute | solution.py:228
  22.0 0.4 %collective-permute-start.8 = (bf16[16,4096]{1,0:T(8,128)(2,1)S(1)}, bf16[16,4096]{1,0:T(8,128)(2,1)S(1)}, u32[]{:S(2)}, u32[]{:S(2)}) collective-permute-start(bf16[16,4096]{1,0:T(8,128)(2,1)S(1)} %fusion.7), channel_id=1, source_target_pairs={{0,12},{4,8},{8,4},{12,0},{16,28},{20,24},{24,20},{28,16},{1,13},{... | collective-permute-start | bytes 393224 | tf_op jit(solution)/shard_map/ppermute | solution.py:228
  22.4 1.5 %collective-permute-done.6 = bf16[16,4096]{1,0:T(8,128)(2,1)S(1)} collective-permute-done((bf16[16,4096]{1,0:T(8,128)(2,1)S(1)}, bf16[16,4096]{1,0:T(8,128)(2,1)S(1)}, u32[]{:S(2)}, u32[]{:S(2)}) %collective-permute-start.6) | collective-permute-done | bytes 131104 | tf_op jit(solution)/shard_map/ppermute | solution.py:228
  23.8 2.4 %collective-permute-done.7 = bf16[16,4096]{1,0:T(8,128)(2,1)S(1)} collective-permute-done((bf16[16,4096]{1,0:T(8,128)(2,1)S(1)}, bf16[16,4096]{1,0:T(8,128)(2,1)S(1)}, u32[]{:S(2)}, u32[]{:S(2)}) %collective-permute-start.7) | collective-permute-done | bytes 131104 | tf_op jit(solution)/shard_map/ppermute | solution.py:228
  26.3 1.9 %collective-permute-done.8 = bf16[16,4096]{1,0:T(8,128)(2,1)S(1)} collective-permute-done((bf16[16,4096]{1,0:T(8,128)(2,1)S(1)}, bf16[16,4096]{1,0:T(8,128)(2,1)S(1)}, u32[]{:S(2)}, u32[]{:S(2)}) %collective-permute-start.8) | collective-permute-done | bytes 131104 | tf_op jit(solution)/shard_map/ppermute | solution.py:228
  28.1 0.1 fusion.5
  28.2 3.2 %collective-permute-start.9 = (bf16[16,4096]{1,0:T(8,128)(2,1)S(1)}, bf16[16,4096]{1,0:T(8,128)(2,1)S(1)}, u32[]{:S(2)}, u32[]{:S(2)}) collective-permute-start(bf16[16,4096]{1,0:T(8,128)(2,1)S(1)} %fusion.5), channel_id=1, source_target_pairs={{0,24},{4,28},{8,16},{12,20},{16,8},{20,12},{24,0},{28,4},{1,25},{... | collective-permute-start | bytes 393224 | tf_op jit(solution)/shard_map/ppermute | solution.py:228
  31.4 2.3 %weight_grads.1 = (bf16[24,128,128]{2,1,0:T(8,128)(2,1)}, bf16[24,128,128]{2,1,0:T(8,128)(2,1)}) custom-call(s32[1,24]{1,0:T(1,128)S(1)} %copy-done.1, s32[1,1]{1,0:T(1,128)S(6)} %copy.10.live_ref, bf16[32,4096]{1,0:T(8,128)(2,1)S(1)} %get-tuple-element.25.refs_0_, bf16[32,4096]{1,0:T(8,128)(2,1)S(1)} %get-tuple-element.26.refs_1_, ...), custom_call_target="tpu_custom_call" | custom-call | tf_op jit(solution)/shard_map/weight_grads/pallas_call | solution.py:325
  33.7 1.4 %collective-permute-done.9 = bf16[16,4096]{1,0:T(8,128)(2,1)S(1)} collective-permute-done((bf16[16,4096]{1,0:T(8,128)(2,1)S(1)}, bf16[16,4096]{1,0:T(8,128)(2,1)S(1)}, u32[]{:S(2)}, u32[]{:S(2)}) %collective-permute-start.9) | collective-permute-done | bytes 131104 | tf_op jit(solution)/shard_map/ppermute | solution.py:228
  35.2 0.8 %fusion.6 = bf16[1,16,4096]{2,1,0:T(8,128)(2,1)} fusion(bf16[16,4096]{1,0:T(8,128)(2,1)S(1)} %collective-permute-done.9, bf16[16,4096]{1,0:T(8,128)(2,1)S(1)} %collective-permute-done.8, bf16[16,4096]{1,0:T(8,128)(2,1)S(1)} %collective-permute-done.7, bf16[16,4096]{1,0:T(8,128)(2,1)S(1)} %collective-permute-done.6, bf16[16,4096]{1,0:T(8,128)(2,1)S(1)} %copy-done.2, ...), kind=kLoop, calls=%fused_computation.14 | loop fusion | flops 1245184 | bytes 1310724 | tf_op jit(solution)/shard_map/broadcast_in_dim | solution.py:356
  (9 shorter events, 0.0 us)
Async XLA Ops:
  0.6 9.2 %copy-start.1 = (s32[1,24]{1,0:T(1,128)S(1)}, s32[1,24]{1,0:T(1,128)}, u32[]{:S(2)}) copy-start(s32[1,24]{1,0:T(1,128)} %position_ref.5) | copy-start | bytes 292
  0.6 3.7 %collective-permute-start = (bf16[16,4096]{1,0:T(8,128)(2,1)}, bf16[16,4096]{1,0:T(8,128)(2,1)S(1)}, u32[]{:S(2)}, u32[]{:S(2)}) collective-permute-start(bf16[16,4096]{1,0:T(8,128)(2,1)} %bitcast.11), channel_id=1, source_target_pairs={{0,1},{1,0},{2,3},{3,2},{4,5},{5,4},{6,7},{7,6},{8,9},{9,8},{10,11... | collective-permute-start | bytes 393224 | tf_op jit(solution)/shard_map/ppermute | solution.py:228
  1.2 7.3 %collective-permute-start.1 = (bf16[16,4096]{1,0:T(8,128)(2,1)}, bf16[16,4096]{1,0:T(8,128)(2,1)S(1)}, u32[]{:S(2)}, u32[]{:S(2)}) collective-permute-start(bf16[16,4096]{1,0:T(8,128)(2,1)} %bitcast.12), channel_id=1, source_target_pairs={{0,2},{1,3},{2,0},{3,1},{4,6},{5,7},{6,4},{7,5},{8,10},{9,11},{10,... | collective-permute-start | bytes 393224 | tf_op jit(solution)/shard_map/ppermute | solution.py:228
  4.4 0.7 %copy-start = (s32[1,24]{1,0:T(1,128)S(1)}, s32[1,24]{1,0:T(1,128)}, u32[]{:S(2)}) copy-start(s32[1,24]{1,0:T(1,128)} %position_ref.5) | copy-start | bytes 292
  8.5 1.4 %collective-permute-start.3 = (bf16[16,4096]{1,0:T(8,128)(2,1)S(1)}, bf16[16,4096]{1,0:T(8,128)(2,1)S(1)}, u32[]{:S(2)}, u32[]{:S(2)}) collective-permute-start(bf16[16,4096]{1,0:T(8,128)(2,1)S(1)} %collective-permute-done.1.across_ref), channel_id=1, source_target_pairs={{0,1},{1,0},{2,3},{3,2},{4,5},{5,4},{6,7},{7,6},{8,9},{9,8},{10,11... | collective-permute-start | bytes 393224 | tf_op jit(solution)/shard_map/ppermute | solution.py:228
  11.7 1.4 %collective-permute-start.4 = (bf16[16,4096]{1,0:T(8,128)(2,1)S(1)}, bf16[16,4096]{1,0:T(8,128)(2,1)S(1)}, u32[]{:S(2)}, u32[]{:S(2)}) collective-permute-start(bf16[16,4096]{1,0:T(8,128)(2,1)S(1)} %get-tuple-element.24), channel_id=1, source_target_pairs={{0,1},{1,0},{2,3},{3,2},{4,5},{5,4},{6,7},{7,6},{8,9},{9,8},{10,11... | collective-permute-start | bytes 393224 | tf_op jit(solution)/shard_map/ppermute | solution.py:228
  11.9 2.6 %collective-permute-start.2 = (bf16[16,4096]{1,0:T(8,128)(2,1)S(1)}, bf16[16,4096]{1,0:T(8,128)(2,1)S(1)}, u32[]{:S(2)}, u32[]{:S(2)}) collective-permute-start(bf16[16,4096]{1,0:T(8,128)(2,1)S(1)} %get-tuple-element.19), channel_id=1, source_target_pairs={{0,1},{1,0},{2,3},{3,2},{4,5},{5,4},{6,7},{7,6},{8,9},{9,8},{10,11... | collective-permute-start | bytes 393224 | tf_op jit(solution)/shard_map/ppermute | solution.py:228
  13.1 5.6 %collective-permute-start.5 = (bf16[16,4096]{1,0:T(8,128)(2,1)S(1)}, bf16[16,4096]{1,0:T(8,128)(2,1)S(1)}, u32[]{:S(2)}, u32[]{:S(2)}) collective-permute-start(bf16[16,4096]{1,0:T(8,128)(2,1)S(1)} %add_convert_fusion), channel_id=1, source_target_pairs={{0,2},{1,3},{2,0},{3,1},{4,6},{5,7},{6,4},{7,5},{8,10},{9,11},{10,... | collective-permute-start | bytes 393224 | tf_op jit(solution)/shard_map/ppermute | solution.py:228
  18.8 16.4 %copy-start.2 = (bf16[16,4096]{1,0:T(8,128)(2,1)S(1)}, bf16[16,4096]{1,0:T(8,128)(2,1)}, u32[]{:S(2)}) copy-start(bf16[16,4096]{1,0:T(8,128)(2,1)} %param.9) | copy-start | bytes 393220
  18.8 5.0 %collective-permute-start.6 = (bf16[16,4096]{1,0:T(8,128)(2,1)S(1)}, bf16[16,4096]{1,0:T(8,128)(2,1)S(1)}, u32[]{:S(2)}, u32[]{:S(2)}) collective-permute-start(bf16[16,4096]{1,0:T(8,128)(2,1)S(1)} %fusion.7), channel_id=1, source_target_pairs={{0,4},{4,0},{8,12},{12,8},{16,20},{20,16},{24,28},{28,24},{1,5},{5... | collective-permute-start | bytes 393224 | tf_op jit(solution)/shard_map/ppermute | solution.py:228
  20.4 5.9 %collective-permute-start.7 = (bf16[16,4096]{1,0:T(8,128)(2,1)S(1)}, bf16[16,4096]{1,0:T(8,128)(2,1)S(1)}, u32[]{:S(2)}, u32[]{:S(2)}) collective-permute-start(bf16[16,4096]{1,0:T(8,128)(2,1)S(1)} %fusion.7), channel_id=1, source_target_pairs={{0,8},{4,12},{8,0},{12,4},{16,24},{20,28},{24,16},{28,20},{1,9},{5... | collective-permute-start | bytes 393224 | tf_op jit(solution)/shard_map/ppermute | solution.py:228
  22.0 6.1 %collective-permute-start.8 = (bf16[16,4096]{1,0:T(8,128)(2,1)S(1)}, bf16[16,4096]{1,0:T(8,128)(2,1)S(1)}, u32[]{:S(2)}, u32[]{:S(2)}) collective-permute-start(bf16[16,4096]{1,0:T(8,128)(2,1)S(1)} %fusion.7), channel_id=1, source_target_pairs={{0,12},{4,8},{8,4},{12,0},{16,28},{20,24},{24,20},{28,16},{1,13},{... | collective-permute-start | bytes 393224 | tf_op jit(solution)/shard_map/ppermute | solution.py:228
  28.2 6.9 %collective-permute-start.9 = (bf16[16,4096]{1,0:T(8,128)(2,1)S(1)}, bf16[16,4096]{1,0:T(8,128)(2,1)S(1)}, u32[]{:S(2)}, u32[]{:S(2)}) collective-permute-start(bf16[16,4096]{1,0:T(8,128)(2,1)S(1)} %fusion.5), channel_id=1, source_target_pairs={{0,24},{4,28},{8,16},{12,20},{16,8},{20,12},{24,0},{28,4},{1,25},{... | collective-permute-start | bytes 393224 | tf_op jit(solution)/shard_map/ppermute | solution.py:228

commit v4 on v3

--- a/solution.py
+++ b/solution.py
@@ -22,12 +22,17 @@
     raise ValueError(divisor)
 
 
-def _slot(position_ref, live_ref, slot, col_blocks, row_blocks):
+def _make_table(position, live, col_blocks, row_blocks, table_ref):
     factor, shift = _shift_and_factor(col_blocks, col_blocks * row_blocks)
-    position = position_ref[0, slot]
     row = (position * factor) >> shift
-    col = position - row * col_blocks
-    return row, jnp.where(slot < live_ref[0, 0], col, col_blocks)
+    slot = lax.broadcasted_iota(jnp.int32, position.shape, 1)
+    table_ref[0:1, :] = row
+    table_ref[1:2, :] = jnp.where(slot < live, position - row * col_blocks, col_blocks)
+
+
+def _read_table(table_ref):
+    table = table_ref[...]
+    return [(table[0, slot], table[1, slot]) for slot in range(table.shape[1])]
 
 
 def _term(blk, table, grad, weight_ref, ready, x_ref, cot_ref, act_ref, back_ref):
@@ -65,7 +70,7 @@
 
 def _near_half(
     blk,
-    position_ref,
+    position_in,
     live_ref,
     own_in,
     beside_ref,
@@ -78,6 +83,8 @@
     send_ref,
     weight_ref,
     far_grad_ref,
+    table_ref,
+    position_ref,
     grad_ref,
     act_ref,
     back_ref,
@@ -93,6 +100,7 @@
     other = pl.multiple_of((core ^ 1) * count, count)
     near = pl.multiple_of(chip * rows, rows)
     far = pl.multiple_of((chip ^ 1) * rows, rows)
+    position = pltpu.make_async_copy(position_in, position_ref, sems.at[3 + 2 * PARTS])
     own = pltpu.make_async_copy(own_in, x_ref.at[pl.ds(mine, count), :], sems.at[0])
     near_grad = pltpu.make_async_copy(grad_in.at[pl.ds(near, rows), :], grad_ref, sems.at[1])
     far_grad = pltpu.make_async_copy(grad_in.at[pl.ds(far, rows), :], far_grad_ref, sems.at[2])
@@ -109,16 +117,17 @@
                 ),
             ]
         )
-    for copy in (own, *blocks[0], near_grad, *sum(blocks[1:], []), far_grad):
+    for copy in (position, own, *blocks[0], near_grad, *sum(blocks[1:], []), far_grad):
         copy.start()
     x_ref[pl.ds(other, count), :] = beside_ref[...]
     act_ref[...] = jnp.zeros_like(act_ref)
     back_ref[...] = jnp.zeros_like(back_ref)
-    own.wait()
-    table = [
-        _slot(position_ref, live_ref, slot, cot_ref.shape[0] - 1, back_ref.shape[0])
-        for slot in range(slots)
-    ]
+    for copy in (position, own):
+        copy.wait()
+    _make_table(
+        position_ref[...], live_ref[0, 0], cot_ref.shape[0] - 1, back_ref.shape[0], table_ref
+    )
+    table = _read_table(table_ref)
 
     def ready(slot):
         if slot % part == 0:
@@ -138,8 +147,7 @@
 
 def _far_half(
     blk,
-    position_ref,
-    live_ref,
+    table_ref,
     across_ref,
     beyond_ref,
     grad_ref,
@@ -160,10 +168,7 @@
     x_ref[pl.ds(other, count), :] = beyond_ref[...]
     act_ref[...] = jnp.zeros_like(act_ref)
     back_ref[...] = jnp.zeros_like(back_ref)
-    table = [
-        _slot(position_ref, live_ref, slot, cot_ref.shape[0] - 1, back_ref.shape[0])
-        for slot in range(weight_ref.shape[0])
-    ]
+    table = _read_table(table_ref)
 
     def grad(col):
         return grad_ref[:, col * blk : (col + 1) * blk]
@@ -183,6 +188,7 @@
     wu_ref,
     cot_ref,
     term_ref,
+    table_ref,
     weight_ref,
     act_ref,
     back_ref,
@@ -191,10 +197,10 @@
     weight_ref[:, :, blk:] = wu_ref[...]
     act_ref[...] = jnp.zeros_like(act_ref)
     back_ref[...] = jnp.zeros_like(back_ref)
-    table = [
-        _slot(position_ref, live_ref, slot, cot_ref.shape[0] - 1, back_ref.shape[0])
-        for slot in range(weight_ref.shape[0])
-    ]
+    _make_table(
+        position_ref[...], live_ref[0, 0], cot_ref.shape[0] - 1, back_ref.shape[0], table_ref
+    )
+    table = _read_table(table_ref)
 
     def grad(col):
         return grad_ref[:, col * blk : (col + 1) * blk]
@@ -203,12 +209,9 @@
     _write_rows(back_ref, 0, x_ref.shape[0], term_ref)
 
 
-def _weight_grads(blk, halves, position_ref, live_ref, *refs):
+def _weight_grads(blk, halves, table_ref, *refs):
     x_refs, cot_refs, (gate_ref, up_ref) = refs[:halves], refs[halves : 2 * halves], refs[-2:]
-    for slot in range(gate_ref.shape[0]):
-        row, col = _slot(
-            position_ref, live_ref, slot, cot_refs[0].shape[0] - 1, x_refs[0].shape[1] // blk
-        )
+    for slot, (row, col) in enumerate(_read_table(table_ref)):
         start = pl.multiple_of(row * blk, blk)
         grads = lax.dot_general(
             jnp.concatenate([x_ref[:, pl.ds(start, blk)] for x_ref in x_refs], axis=0),
@@ -260,7 +263,7 @@
         rows = 2 * count
         across = _swap(own_rows, "tp", 2)
         beside = _swap(own_rows, "tp", 1)
-        near_x, near_cot, keep, near_send, weights, far_grad = pl.pallas_call(
+        near_x, near_cot, keep, near_send, weights, far_grad, table = pl.pallas_call(
             functools.partial(_near_half, blk),
             out_shape=(
                 struct((rows, width), BF16),
@@ -269,18 +272,20 @@
                 struct((count, width), BF16),
                 struct((slots, blk, 2 * blk), BF16),
                 struct((rows, hidden), BF16),
+                struct((2, slots), jnp.int32),
             ),
-            in_specs=[smem, smem, hbm, vmem, hbm, hbm, hbm],
-            out_specs=[vmem] * 6,
+            in_specs=[hbm, smem, hbm, vmem, hbm, hbm, hbm],
+            out_specs=[vmem] * 7,
             scratch_shapes=[
+                pltpu.VMEM(block_pos.shape, jnp.int32),
                 pltpu.VMEM((rows, hidden), BF16),
                 *sums(rows),
-                pltpu.SemaphoreType.DMA((3 + 2 * PARTS,)),
+                pltpu.SemaphoreType.DMA((4 + 2 * PARTS,)),
             ],
             compiler_params=_params(10),
             name="near_half",
         )(
-            block_pos,
+            _pinned(block_pos, pltpu.HBM),
             live_count,
             _pinned(own_rows, pltpu.HBM),
             beside,
@@ -296,12 +301,12 @@
                 struct((count, width), F32),
                 struct((count, width), BF16),
             ),
-            in_specs=[smem, smem] + [vmem] * 4,
+            in_specs=[vmem] * 5,
             out_specs=[vmem] * 4,
             scratch_shapes=sums(rows),
             compiler_params=_params(10),
             name="far_half",
-        )(block_pos, live_count, across, beyond, far_grad, weights)
+        )(table, across, beyond, far_grad, weights)
         near_came = _swap(near_send, "tp", 1)
         far_came = _swap(far_send, "tp", 1)
         crossed = _swap((far + far_came.astype(F32)).astype(BF16), "tp", 2)
@@ -310,11 +315,11 @@
     else:
         rows = tp * count
         gathered = lax.all_gather(own_rows, "tp", axis=0, tiled=True)
-        cot, term = pl.pallas_call(
+        cot, term, table = pl.pallas_call(
             functools.partial(_whole, blk),
-            out_shape=(cots(rows), struct((rows, width), BF16)),
-            in_specs=[smem, smem] + [vmem] * 4,
-            out_specs=[vmem] * 2,
+            out_shape=(cots(rows), struct((rows, width), BF16), struct((2, slots), jnp.int32)),
+            in_specs=[vmem, smem] + [vmem] * 4,
+            out_specs=[vmem] * 3,
             scratch_shapes=[pltpu.VMEM((slots, blk, 2 * blk), BF16), *sums(rows)],
             compiler_params=_params(24),
             name="whole",
@@ -325,11 +330,11 @@
     gate_gradient, up_gradient = pl.pallas_call(
         functools.partial(_weight_grads, blk, len(x_parts)),
         out_shape=(struct((slots, blk, blk), BF16),) * 2,
-        in_specs=[smem, smem] + [vmem] * (2 * len(x_parts)),
+        in_specs=[vmem] * (1 + 2 * len(x_parts)),
         out_specs=[vmem, vmem],
         compiler_params=_params(8),
         name="weight_grads",
-    )(block_pos, live_count, *x_parts, *cot_parts)
+    )(table, *x_parts, *cot_parts)
 
     total = own_term
     result = top_grad.astype(F32) + own_term

time: 36.2 us -> 35.2 us (0.972)
  Pallas kernels: 7.5 us -> 6.3 us
  local copies, waits for them, and re-layouts: 0.66 us -> 0.01 us
  waiting for transfers between devices: 13.5 us -> 14 us
  starting transfers between devices: 12 us -> 12.4 us
    unnamed x6 -> x2, local copies, waits for them, and re-layouts: 0.66 us -> 0.01 us
    pallas_call x1, Pallas kernels: 3.4 us -> 2.9 us  [local(): pl.pallas_call(functools.partial(_near_half, blk), out_shape=(struct((row...]
    ppermute x10, starting transfers between devices: 12 us -> 12.4 us  [_swap(): return lax.ppermute(array, axis, [(i, i ^ distance) for i in range(count)])]
    ppermute x10, waiting for transfers between devices: 13.5 us -> 14 us  [_swap(): return lax.ppermute(array, axis, [(i, i ^ distance) for i in range(count)])]
    pallas_call x1, Pallas kernels: 1.8 us -> 1.35 us  [local(): pl.pallas_call(functools.partial(_far_half, blk), out_shape=(struct((rows...]
  transfers between devices with their start and end apart: 10 -> 10, of which waited for: 7 -> 8; matrix products, arithmetic and copies ran while one was open for 0% -> 0% of each run, Pallas kernels for 16% -> 14%
where the time goes in v4:
time: 35.2 us; the launch traced here: 35 us
  waiting for transfers between devices  14 us (40%)
  starting transfers between devices  12.4 us (35%)
  Pallas kernels  6.3 us (18%)
  between operations  1.33 us (4%)
  other arithmetic  1 us (3%)
    ppermute x10, waiting for transfers between devices, _swap(): return lax.ppermute(array, axis, [(i, i ^ distance) for i in range(count)])  14 us
    ppermute x10, starting transfers between devices, _swap(): return lax.ppermute(array, axis, [(i, i ^ distance) for i in range(count)])  12.4 us
    pallas_call x1, Pallas kernels, local(): pl.pallas_call(functools.partial(_near_half, blk), out_shape=(struct((row...  2.9 us
    pallas_call x1, Pallas kernels, local(): pl.pallas_call(functools.partial(_weight_grads, blk, len(x_parts)), out_s...  2.05 us
    pallas_call x1, Pallas kernels, local(): pl.pallas_call(functools.partial(_far_half, blk), out_shape=(struct((rows...  1.35 us
    broadcast_in_dim x1, other arithmetic, local(): return (result.astype(BF16)[None], gate_gradient[None], up_gradient[None])  0.83 us
  transfers between devices with their start and end apart: 10, of which 8 were waited for; matrix products, arithmetic and copies ran while one was open for 0% of the time, Pallas kernels for 14%

profile of v4, /device:TPU:0, one launch (start us, length us, event | category | flops | bytes accessed | tf_op | source)
XLA Modules:
  0.0 35.0 jit_solution(12353342869203374532)
XLA Ops:
  0.6 0.5 %collective-permute-start = (bf16[16,4096]{1,0:T(8,128)(2,1)}, bf16[16,4096]{1,0:T(8,128)(2,1)S(1)}, u32[]{:S(2)}, u32[]{:S(2)}) collective-permute-start(bf16[16,4096]{1,0:T(8,128)(2,1)} %bitcast.11), channel_id=1, source_target_pairs={{0,1},{1,0},{2,3},{3,2},{4,5},{5,4},{6,7},{7,6},{8,9},{9,8},{10,11... | collective-permute-start | bytes 393224 | tf_op jit(solution)/shard_map/ppermute | solution.py:231
  1.1 2.6 %collective-permute-start.1 = (bf16[16,4096]{1,0:T(8,128)(2,1)}, bf16[16,4096]{1,0:T(8,128)(2,1)S(1)}, u32[]{:S(2)}, u32[]{:S(2)}) collective-permute-start(bf16[16,4096]{1,0:T(8,128)(2,1)} %bitcast.12), channel_id=1, source_target_pairs={{0,2},{1,3},{2,0},{3,1},{4,6},{5,7},{6,4},{7,5},{8,10},{9,11},{10,... | collective-permute-start | bytes 393224 | tf_op jit(solution)/shard_map/ppermute | solution.py:231
  4.4 2.9 %near_half.1 = (bf16[32,4096]{1,0:T(8,128)(2,1)S(1)}, bf16[29,32,256]{2,1,0:T(8,128)(2,1)S(1)}, f32[16,4096]{1,0:T(8,128)S(1)}, bf16[16,4096]{1,0:T(8,128)(2,1)S...) custom-call(s32[1,24]{1,0:T(1,128)} %position_in.1, ...), custom_call_target="tpu_custom_call" | custom-call | tf_op jit(solution)/shard_map/near_half/pallas_call | solution.py:266
  7.3 0.7 %collective-permute-done.1.across_ref = bf16[16,4096]{1,0:T(8,128)(2,1)S(1)} collective-permute-done((bf16[16,4096]{1,0:T(8,128)(2,1)}, bf16[16,4096]{1,0:T(8,128)(2,1)S(1)}, u32[]{:S(2)}, u32[]{:S(2)}) %collective-permute-start.1) | collective-permute-done | bytes 131104 | tf_op jit(solution)/shard_map/ppermute | solution.py:231
  8.0 0.0 collective-permute-start.3
  8.0 1.3 %collective-permute-done.3.beyond_ref = bf16[16,4096]{1,0:T(8,128)(2,1)S(1)} collective-permute-done((bf16[16,4096]{1,0:T(8,128)(2,1)S(1)}, bf16[16,4096]{1,0:T(8,128)(2,1)S(1)}, u32[]{:S(2)}, u32[]{:S(2)}) %collective-permute-start.3) | collective-permute-done | bytes 131104 | tf_op jit(solution)/shard_map/ppermute | solution.py:231
  9.4 1.4 %far_half.1 = (bf16[32,4096]{1,0:T(8,128)(2,1)S(1)}, bf16[29,32,256]{2,1,0:T(8,128)(2,1)S(1)}, f32[16,4096]{1,0:T(8,128)S(1)}, bf16[16,4096]{1,0:T(8,128)(2,1)S(1)}) custom-call(s32[2,24]{1,0:T(2,128)S(1)} %get-tuple-element.21.table_ref, bf16[16,4096]{1,0:T(8,128)(2,1)S(1)} %collective-permute-done.1.across_ref, ...), custom_call_target="tpu_custom_call" | custom-call | tf_op jit(solution)/shard_map/far_half/pallas_call | solution.py:296
  10.7 0.2 collective-permute-start.4
  10.9 0.4 %collective-permute-start.2 = (bf16[16,4096]{1,0:T(8,128)(2,1)S(1)}, bf16[16,4096]{1,0:T(8,128)(2,1)S(1)}, u32[]{:S(2)}, u32[]{:S(2)}) collective-permute-start(bf16[16,4096]{1,0:T(8,128)(2,1)S(1)} %get-tuple-element.20), channel_id=1, source_target_pairs={{0,1},{1,0},{2,3},{3,2},{4,5},{5,4},{6,7},{7,6},{8,9},{9,8},{10,11... | collective-permute-start | bytes 393224 | tf_op jit(solution)/shard_map/ppermute | solution.py:231
  11.3 0.8 %collective-permute-done.4 = bf16[16,4096]{1,0:T(8,128)(2,1)S(1)} collective-permute-done((bf16[16,4096]{1,0:T(8,128)(2,1)S(1)}, bf16[16,4096]{1,0:T(8,128)(2,1)S(1)}, u32[]{:S(2)}, u32[]{:S(2)}) %collective-permute-start.4) | collective-permute-done | bytes 131104 | tf_op jit(solution)/shard_map/ppermute | solution.py:231
  12.2 1.8 %collective-permute-start.5 = (bf16[16,4096]{1,0:T(8,128)(2,1)S(1)}, bf16[16,4096]{1,0:T(8,128)(2,1)S(1)}, u32[]{:S(2)}, u32[]{:S(2)}) collective-permute-start(bf16[16,4096]{1,0:T(8,128)(2,1)S(1)} %add_convert_fusion), channel_id=1, source_target_pairs={{0,2},{1,3},{2,0},{3,1},{4,6},{5,7},{6,4},{7,5},{8,10},{9,11},{10,... | collective-permute-start | bytes 393224 | tf_op jit(solution)/shard_map/ppermute | solution.py:231
  14.0 3.8 %collective-permute-done.5 = bf16[16,4096]{1,0:T(8,128)(2,1)S(1)} collective-permute-done((bf16[16,4096]{1,0:T(8,128)(2,1)S(1)}, bf16[16,4096]{1,0:T(8,128)(2,1)S(1)}, u32[]{:S(2)}, u32[]{:S(2)}) %collective-permute-start.5) | collective-permute-done | bytes 131104 | tf_op jit(solution)/shard_map/ppermute | solution.py:231
  17.8 0.1 fusion.7
  17.9 1.8 %collective-permute-start.6 = (bf16[16,4096]{1,0:T(8,128)(2,1)S(1)}, bf16[16,4096]{1,0:T(8,128)(2,1)S(1)}, u32[]{:S(2)}, u32[]{:S(2)}) collective-permute-start(bf16[16,4096]{1,0:T(8,128)(2,1)S(1)} %fusion.7), channel_id=1, source_target_pairs={{0,4},{4,0},{8,12},{12,8},{16,20},{20,16},{24,28},{28,24},{1,5},{5... | collective-permute-start | bytes 393224 | tf_op jit(solution)/shard_map/ppermute | solution.py:231
  19.7 1.6 %collective-permute-start.7 = (bf16[16,4096]{1,0:T(8,128)(2,1)S(1)}, bf16[16,4096]{1,0:T(8,128)(2,1)S(1)}, u32[]{:S(2)}, u32[]{:S(2)}) collective-permute-start(bf16[16,4096]{1,0:T(8,128)(2,1)S(1)} %fusion.7), channel_id=1, source_target_pairs={{0,8},{4,12},{8,0},{12,4},{16,24},{20,28},{24,16},{28,20},{1,9},{5... | collective-permute-start | bytes 393224 | tf_op jit(solution)/shard_map/ppermute | solution.py:231
  21.3 0.1 collective-permute-start.8
  21.4 1.7 %collective-permute-done.6 = bf16[16,4096]{1,0:T(8,128)(2,1)S(1)} collective-permute-done((bf16[16,4096]{1,0:T(8,128)(2,1)S(1)}, bf16[16,4096]{1,0:T(8,128)(2,1)S(1)}, u32[]{:S(2)}, u32[]{:S(2)}) %collective-permute-start.6) | collective-permute-done | bytes 131104 | tf_op jit(solution)/shard_map/ppermute | solution.py:231
  23.1 2.4 %collective-permute-done.7 = bf16[16,4096]{1,0:T(8,128)(2,1)S(1)} collective-permute-done((bf16[16,4096]{1,0:T(8,128)(2,1)S(1)}, bf16[16,4096]{1,0:T(8,128)(2,1)S(1)}, u32[]{:S(2)}, u32[]{:S(2)}) %collective-permute-start.7) | collective-permute-done | bytes 131104 | tf_op jit(solution)/shard_map/ppermute | solution.py:231
  25.5 1.6 %collective-permute-done.8 = bf16[16,4096]{1,0:T(8,128)(2,1)S(1)} collective-permute-done((bf16[16,4096]{1,0:T(8,128)(2,1)S(1)}, bf16[16,4096]{1,0:T(8,128)(2,1)S(1)}, u32[]{:S(2)}, u32[]{:S(2)}) %collective-permute-start.8) | collective-permute-done | bytes 131104 | tf_op jit(solution)/shard_map/ppermute | solution.py:231
  27.2 0.1 fusion.5
  27.3 3.4 %collective-permute-start.9 = (bf16[16,4096]{1,0:T(8,128)(2,1)S(1)}, bf16[16,4096]{1,0:T(8,128)(2,1)S(1)}, u32[]{:S(2)}, u32[]{:S(2)}) collective-permute-start(bf16[16,4096]{1,0:T(8,128)(2,1)S(1)} %fusion.5), channel_id=1, source_target_pairs={{0,24},{4,28},{8,16},{12,20},{16,8},{20,12},{24,0},{28,4},{1,25},{... | collective-permute-start | bytes 393224 | tf_op jit(solution)/shard_map/ppermute | solution.py:231
  30.7 2.1 %weight_grads.1 = (bf16[24,128,128]{2,1,0:T(8,128)(2,1)}, bf16[24,128,128]{2,1,0:T(8,128)(2,1)}) custom-call(s32[2,24]{1,0:T(2,128)S(1)} %get-tuple-element.21.table_ref, bf16[32,4096]{1,0:T(8,128)(2,1)S(1)} %get-tuple-element.27.refs_0_, bf16[32,4096]{1,0:T(8,128)(2,1)S(1)} %get-tuple-element.28.refs_1_, ...), custom_call_target="tpu_custom_call" | custom-call | tf_op jit(solution)/shard_map/weight_grads/pallas_call | solution.py:330
  32.7 1.5 %collective-permute-done.9 = bf16[16,4096]{1,0:T(8,128)(2,1)S(1)} collective-permute-done((bf16[16,4096]{1,0:T(8,128)(2,1)S(1)}, bf16[16,4096]{1,0:T(8,128)(2,1)S(1)}, u32[]{:S(2)}, u32[]{:S(2)}) %collective-permute-start.9) | collective-permute-done | bytes 131104 | tf_op jit(solution)/shard_map/ppermute | solution.py:231
  34.2 0.8 %fusion.6 = bf16[1,16,4096]{2,1,0:T(8,128)(2,1)} fusion(bf16[16,4096]{1,0:T(8,128)(2,1)S(1)} %collective-permute-done.9, bf16[16,4096]{1,0:T(8,128)(2,1)S(1)} %collective-permute-done.8, bf16[16,4096]{1,0:T(8,128)(2,1)S(1)} %collective-permute-done.7, bf16[16,4096]{1,0:T(8,128)(2,1)S(1)} %collective-permute-done.6, bf16[16,4096]{1,0:T(8,128)(2,1)S(1)} %copy-done, ...), kind=kLoop, calls=%fused_computation.14 | loop fusion | flops 1245184 | bytes 1310724 | tf_op jit(solution)/shard_map/broadcast_in_dim | solution.py:361
  (5 shorter events, 0.0 us)
Async XLA Ops:
  0.6 3.7 %collective-permute-start = (bf16[16,4096]{1,0:T(8,128)(2,1)}, bf16[16,4096]{1,0:T(8,128)(2,1)S(1)}, u32[]{:S(2)}, u32[]{:S(2)}) collective-permute-start(bf16[16,4096]{1,0:T(8,128)(2,1)} %bitcast.11), channel_id=1, source_target_pairs={{0,1},{1,0},{2,3},{3,2},{4,5},{5,4},{6,7},{7,6},{8,9},{9,8},{10,11... | collective-permute-start | bytes 393224 | tf_op jit(solution)/shard_map/ppermute | solution.py:231
  1.1 6.9 %collective-permute-start.1 = (bf16[16,4096]{1,0:T(8,128)(2,1)}, bf16[16,4096]{1,0:T(8,128)(2,1)S(1)}, u32[]{:S(2)}, u32[]{:S(2)}) collective-permute-start(bf16[16,4096]{1,0:T(8,128)(2,1)} %bitcast.12), channel_id=1, source_target_pairs={{0,2},{1,3},{2,0},{3,1},{4,6},{5,7},{6,4},{7,5},{8,10},{9,11},{10,... | collective-permute-start | bytes 393224 | tf_op jit(solution)/shard_map/ppermute | solution.py:231
  8.0 1.3 %collective-permute-start.3 = (bf16[16,4096]{1,0:T(8,128)(2,1)S(1)}, bf16[16,4096]{1,0:T(8,128)(2,1)S(1)}, u32[]{:S(2)}, u32[]{:S(2)}) collective-permute-start(bf16[16,4096]{1,0:T(8,128)(2,1)S(1)} %collective-permute-done.1.across_ref), channel_id=1, source_target_pairs={{0,1},{1,0},{2,3},{3,2},{4,5},{5,4},{6,7},{7,6},{8,9},{9,8},{10,11... | collective-permute-start | bytes 393224 | tf_op jit(solution)/shard_map/ppermute | solution.py:231
  10.7 1.4 %collective-permute-start.4 = (bf16[16,4096]{1,0:T(8,128)(2,1)S(1)}, bf16[16,4096]{1,0:T(8,128)(2,1)S(1)}, u32[]{:S(2)}, u32[]{:S(2)}) collective-permute-start(bf16[16,4096]{1,0:T(8,128)(2,1)S(1)} %get-tuple-element.26), channel_id=1, source_target_pairs={{0,1},{1,0},{2,3},{3,2},{4,5},{5,4},{6,7},{7,6},{8,9},{9,8},{10,11... | collective-permute-start | bytes 393224 | tf_op jit(solution)/shard_map/ppermute | solution.py:231
  10.9 3.0 %collective-permute-start.2 = (bf16[16,4096]{1,0:T(8,128)(2,1)S(1)}, bf16[16,4096]{1,0:T(8,128)(2,1)S(1)}, u32[]{:S(2)}, u32[]{:S(2)}) collective-permute-start(bf16[16,4096]{1,0:T(8,128)(2,1)S(1)} %get-tuple-element.20), channel_id=1, source_target_pairs={{0,1},{1,0},{2,3},{3,2},{4,5},{5,4},{6,7},{7,6},{8,9},{9,8},{10,11... | collective-permute-start | bytes 393224 | tf_op jit(solution)/shard_map/ppermute | solution.py:231
  12.2 5.6 %collective-permute-start.5 = (bf16[16,4096]{1,0:T(8,128)(2,1)S(1)}, bf16[16,4096]{1,0:T(8,128)(2,1)S(1)}, u32[]{:S(2)}, u32[]{:S(2)}) collective-permute-start(bf16[16,4096]{1,0:T(8,128)(2,1)S(1)} %add_convert_fusion), channel_id=1, source_target_pairs={{0,2},{1,3},{2,0},{3,1},{4,6},{5,7},{6,4},{7,5},{8,10},{9,11},{10,... | collective-permute-start | bytes 393224 | tf_op jit(solution)/shard_map/ppermute | solution.py:231
  17.8 16.4 %copy-start = (bf16[16,4096]{1,0:T(8,128)(2,1)S(1)}, bf16[16,4096]{1,0:T(8,128)(2,1)}, u32[]{:S(2)}) copy-start(bf16[16,4096]{1,0:T(8,128)(2,1)} %param.9) | copy-start | bytes 393220
  17.9 5.2 %collective-permute-start.6 = (bf16[16,4096]{1,0:T(8,128)(2,1)S(1)}, bf16[16,4096]{1,0:T(8,128)(2,1)S(1)}, u32[]{:S(2)}, u32[]{:S(2)}) collective-permute-start(bf16[16,4096]{1,0:T(8,128)(2,1)S(1)} %fusion.7), channel_id=1, source_target_pairs={{0,4},{4,0},{8,12},{12,8},{16,20},{20,16},{24,28},{28,24},{1,5},{5... | collective-permute-start | bytes 393224 | tf_op jit(solution)/shard_map/ppermute | solution.py:231
  19.7 5.8 %collective-permute-start.7 = (bf16[16,4096]{1,0:T(8,128)(2,1)S(1)}, bf16[16,4096]{1,0:T(8,128)(2,1)S(1)}, u32[]{:S(2)}, u32[]{:S(2)}) collective-permute-start(bf16[16,4096]{1,0:T(8,128)(2,1)S(1)} %fusion.7), channel_id=1, source_target_pairs={{0,8},{4,12},{8,0},{12,4},{16,24},{20,28},{24,16},{28,20},{1,9},{5... | collective-permute-start | bytes 393224 | tf_op jit(solution)/shard_map/ppermute | solution.py:231
  21.3 5.9 %collective-permute-start.8 = (bf16[16,4096]{1,0:T(8,128)(2,1)S(1)}, bf16[16,4096]{1,0:T(8,128)(2,1)S(1)}, u32[]{:S(2)}, u32[]{:S(2)}) collective-permute-start(bf16[16,4096]{1,0:T(8,128)(2,1)S(1)} %fusion.7), channel_id=1, source_target_pairs={{0,12},{4,8},{8,4},{12,0},{16,28},{20,24},{24,20},{28,16},{1,13},{... | collective-permute-start | bytes 393224 | tf_op jit(solution)/shard_map/ppermute | solution.py:231
  27.3 6.9 %collective-permute-start.9 = (bf16[16,4096]{1,0:T(8,128)(2,1)S(1)}, bf16[16,4096]{1,0:T(8,128)(2,1)S(1)}, u32[]{:S(2)}, u32[]{:S(2)}) collective-permute-start(bf16[16,4096]{1,0:T(8,128)(2,1)S(1)} %fusion.5), channel_id=1, source_target_pairs={{0,24},{4,28},{8,16},{12,20},{16,8},{20,12},{24,0},{28,4},{1,25},{... | collective-permute-start | bytes 393224 | tf_op jit(solution)/shard_map/ppermute | solution.py:231

commit v5 on v4

--- a/solution.py
+++ b/solution.py
@@ -68,58 +68,45 @@
         )
 
 
-def _near_half(
+def _own_rows(
     blk,
     position_in,
     live_ref,
     own_in,
-    beside_ref,
     grad_in,
     wg_in,
     wu_in,
     x_ref,
     cot_ref,
-    keep_ref,
-    send_ref,
+    term_ref,
     weight_ref,
-    far_grad_ref,
+    grad_ref,
     table_ref,
     position_ref,
-    grad_ref,
     act_ref,
     back_ref,
     sems,
 ):
-    me = lax.axis_index("tp")
-    core, chip = me & 1, me >> 1
-    count = own_in.shape[0]
     slots = wg_in.shape[0]
     part = slots // PARTS
-    rows = 2 * count
-    mine = pl.multiple_of(core * count, count)
-    other = pl.multiple_of((core ^ 1) * count, count)
-    near = pl.multiple_of(chip * rows, rows)
-    far = pl.multiple_of((chip ^ 1) * rows, rows)
-    position = pltpu.make_async_copy(position_in, position_ref, sems.at[3 + 2 * PARTS])
-    own = pltpu.make_async_copy(own_in, x_ref.at[pl.ds(mine, count), :], sems.at[0])
-    near_grad = pltpu.make_async_copy(grad_in.at[pl.ds(near, rows), :], grad_ref, sems.at[1])
-    far_grad = pltpu.make_async_copy(grad_in.at[pl.ds(far, rows), :], far_grad_ref, sems.at[2])
+    position = pltpu.make_async_copy(position_in, position_ref, sems.at[2 * PARTS])
+    own = pltpu.make_async_copy(own_in, x_ref, sems.at[2 * PARTS + 1])
+    grads = pltpu.make_async_copy(grad_in, grad_ref, sems.at[2 * PARTS + 2])
     blocks = []
     for index in range(PARTS):
         span = pl.ds(index * part, part)
         blocks.append(
             [
                 pltpu.make_async_copy(
-                    wg_in.at[span], weight_ref.at[span, :, pl.ds(0, blk)], sems.at[3 + 2 * index]
+                    wg_in.at[span], weight_ref.at[span, :, pl.ds(0, blk)], sems.at[2 * index]
                 ),
                 pltpu.make_async_copy(
-                    wu_in.at[span], weight_ref.at[span, :, pl.ds(blk, blk)], sems.at[4 + 2 * index]
+                    wu_in.at[span], weight_ref.at[span, :, pl.ds(blk, blk)], sems.at[2 * index + 1]
                 ),
             ]
         )
-    for copy in (position, own, *blocks[0], near_grad, *sum(blocks[1:], []), far_grad):
+    for copy in (position, own, *sum(blocks, []), grads):
         copy.start()
-    x_ref[pl.ds(other, count), :] = beside_ref[...]
     act_ref[...] = jnp.zeros_like(act_ref)
     back_ref[...] = jnp.zeros_like(back_ref)
     for copy in (position, own):
@@ -127,55 +114,38 @@
     _make_table(
         position_ref[...], live_ref[0, 0], cot_ref.shape[0] - 1, back_ref.shape[0], table_ref
     )
-    table = _read_table(table_ref)
 
     def ready(slot):
         if slot % part == 0:
             for copy in blocks[slot // part]:
                 copy.wait()
 
+    grad = _grad_rows(grad_ref, 0, x_ref.shape[0], blk, grads.wait)
+    _term(blk, _read_table(table_ref), grad, weight_ref, ready, x_ref, cot_ref, act_ref, back_ref)
+    _write_rows(back_ref, 0, x_ref.shape[0], term_ref)
+
+
+def _grad_rows(grad_ref, mask, count, blk, wait=None):
+    start = pl.multiple_of((lax.axis_index("tp") ^ mask) * count, count)
+
     def grad(col):
-        if col == 0:
-            near_grad.wait()
-        return grad_ref[:, col * blk : (col + 1) * blk]
-
-    _term(blk, table, grad, weight_ref, ready, x_ref, cot_ref, act_ref, back_ref)
-    _write_rows(back_ref, mine, count, keep_ref)
-    _write_rows(back_ref, other, count, send_ref)
-    far_grad.wait()
-
-
-def _far_half(
-    blk,
-    table_ref,
-    across_ref,
-    beyond_ref,
-    grad_ref,
-    weight_ref,
-    x_ref,
-    cot_ref,
-    far_ref,
-    send_ref,
-    act_ref,
-    back_ref,
+        if col == 0 and wait is not None:
+            wait()
+        return grad_ref[pl.ds(start, count), col * blk : (col + 1) * blk]
+
+    return grad
+
+
+def _other_rows(
+    blk, mask, table_ref, x_ref, grad_ref, weight_ref, cot_ref, term_ref, act_ref, back_ref
 ):
-    me = lax.axis_index("tp")
-    core = me & 1
-    count = across_ref.shape[0]
-    mine = pl.multiple_of(core * count, count)
-    other = pl.multiple_of((core ^ 1) * count, count)
-    x_ref[pl.ds(mine, count), :] = across_ref[...]
-    x_ref[pl.ds(other, count), :] = beyond_ref[...]
+    count = x_ref.shape[0]
     act_ref[...] = jnp.zeros_like(act_ref)
     back_ref[...] = jnp.zeros_like(back_ref)
+    grad = _grad_rows(grad_ref, mask, count, blk)
     table = _read_table(table_ref)
-
-    def grad(col):
-        return grad_ref[:, col * blk : (col + 1) * blk]
-
     _term(blk, table, grad, weight_ref, lambda slot: None, x_ref, cot_ref, act_ref, back_ref)
-    _write_rows(back_ref, other, count, send_ref)
-    _write_rows(back_ref, mine, count, far_ref)
+    _write_rows(back_ref, 0, count, term_ref)
 
 
 def _whole(
@@ -260,58 +230,59 @@
         ]
 
     if tp == 4 and slots % PARTS == 0:
-        rows = 2 * count
         across = _swap(own_rows, "tp", 2)
-        beside = _swap(own_rows, "tp", 1)
-        near_x, near_cot, keep, near_send, weights, far_grad, table = pl.pallas_call(
-            functools.partial(_near_half, blk),
+        own_x, own_cot, keep, weights, grads, table = pl.pallas_call(
+            functools.partial(_own_rows, blk),
             out_shape=(
-                struct((rows, width), BF16),
-                cots(rows),
+                struct((count, width), BF16),
+                cots(count),
                 struct((count, width), F32),
-                struct((count, width), BF16),
                 struct((slots, blk, 2 * blk), BF16),
-                struct((rows, hidden), BF16),
+                struct(hidden_grad.shape[1:], BF16),
                 struct((2, slots), jnp.int32),
             ),
-            in_specs=[hbm, smem, hbm, vmem, hbm, hbm, hbm],
-            out_specs=[vmem] * 7,
+            in_specs=[hbm, smem, hbm, hbm, hbm, hbm],
+            out_specs=[vmem] * 6,
             scratch_shapes=[
                 pltpu.VMEM(block_pos.shape, jnp.int32),
-                pltpu.VMEM((rows, hidden), BF16),
-                *sums(rows),
-                pltpu.SemaphoreType.DMA((4 + 2 * PARTS,)),
+                *sums(count),
+                pltpu.SemaphoreType.DMA((2 * PARTS + 3,)),
             ],
             compiler_params=_params(10),
-            name="near_half",
+            name="own_rows",
         )(
             _pinned(block_pos, pltpu.HBM),
             live_count,
             _pinned(own_rows, pltpu.HBM),
-            beside,
             *(_pinned(array[0], pltpu.HBM) for array in (hidden_grad, w_gate, w_up)),
         )
-        across, near_send = lax.optimization_barrier((across, near_send))
+
+        def others(mask, x, dtype, name):
+            return pl.pallas_call(
+                functools.partial(_other_rows, blk, mask),
+                out_shape=(cots(count), struct((count, width), dtype)),
+                in_specs=[vmem] * 4,
+                out_specs=[vmem] * 2,
+                scratch_shapes=sums(count),
+                compiler_params=_params(10),
+                name=name,
+            )(table, x, grads, weights)
+
+        beside = _swap(own_x, "tp", 1)
+        across, keep = lax.optimization_barrier((across, keep))
         beyond = _swap(across, "tp", 1)
-        far_x, far_cot, far, far_send = pl.pallas_call(
-            functools.partial(_far_half, blk),
-            out_shape=(
-                struct((rows, width), BF16),
-                cots(rows),
-                struct((count, width), F32),
-                struct((count, width), BF16),
-            ),
-            in_specs=[vmem] * 5,
-            out_specs=[vmem] * 4,
-            scratch_shapes=sums(rows),
-            compiler_params=_params(10),
-            name="far_half",
-        )(table, across, beyond, far_grad, weights)
+        across_cot, far = others(2, across, F32, "across_rows")
+        beyond, far = lax.optimization_barrier((beyond, far))
+        beyond_cot, far_send = others(3, beyond, BF16, "beyond_rows")
+        far_came = _swap(far_send, "tp", 1)
+        far = (far + far_came.astype(F32)).astype(BF16)
+        far, beside = lax.optimization_barrier((far, beside))
+        crossed = _swap(far, "tp", 2)
+        beside_cot, near_send = others(1, beside, BF16, "beside_rows")
         near_came = _swap(near_send, "tp", 1)
-        far_came = _swap(far_send, "tp", 1)
-        crossed = _swap((far + far_came.astype(F32)).astype(BF16), "tp", 2)
         own_term = keep + near_came.astype(F32) + crossed.astype(F32)
-        x_parts, cot_parts = (near_x, far_x), (near_cot, far_cot)
+        x_parts = own_x, beside, across, beyond
+        cot_parts = own_cot, beside_cot, across_cot, beyond_cot
     else:
         rows = tp * count
         gathered = lax.all_gather(own_rows, "tp", axis=0, tiled=True)

time: 35.2 us -> 34.1 us (0.969)
  waiting for transfers between devices: 14 us -> 11.2 us
  Pallas kernels: 6.3 us -> 7.66 us
    ppermute x10, waiting for transfers between devices: 14 us -> 11.2 us  [_swap(): return lax.ppermute(array, axis, [(i, i ^ distance) for i in range(count)])]
    pallas_call x2 -> x4, Pallas kernels: 4.25 us -> 5.62 us  [the longest x3 3.09 us: others(): pl.pallas_call(functools.partial(_other_rows, blk, mask), out_shape=(cots...]
  transfers between devices with their start and end apart: 10 -> 10, of which waited for: 8 -> 8; matrix products, arithmetic and copies ran while one was open for 0% -> 0% of each run, Pallas kernels for 14% -> 20%
where the time goes in v5:
time: 34.1 us; the launch traced here: 33.9 us
  starting transfers between devices  12.7 us (37%)
  waiting for transfers between devices  11.2 us (33%)
  Pallas kernels  7.66 us (22%)
  between operations  1.35 us (4%)
  other arithmetic  1.01 us (3%)
    ppermute x10, starting transfers between devices, _swap(): return lax.ppermute(array, axis, [(i, i ^ distance) for i in range(count)])  12.7 us
    ppermute x10, waiting for transfers between devices, _swap(): return lax.ppermute(array, axis, [(i, i ^ distance) for i in range(count)])  11.2 us
    pallas_call x3, Pallas kernels, others(): pl.pallas_call(functools.partial(_other_rows, blk, mask), out_shape=(cots...  3.09 us
    pallas_call x1, Pallas kernels, local(): pl.pallas_call(functools.partial(_own_rows, blk), out_shape=(struct((coun...  2.53 us
    pallas_call x1, Pallas kernels, local(): pl.pallas_call(functools.partial(_weight_grads, blk, len(x_parts)), out_s...  2.04 us
    broadcast_in_dim x1, other arithmetic, local(): return (result.astype(BF16)[None], gate_gradient[None], up_gradient[None])  0.83 us
  transfers between devices with their start and end apart: 10, of which 8 were waited for; matrix products, arithmetic and copies ran while one was open for 0% of the time, Pallas kernels for 20%

profile of v5, /device:TPU:0, one launch (start us, length us, event | category | flops | bytes accessed | tf_op | source)
XLA Modules:
  0.0 33.9 jit_solution(12092361958354053795)
XLA Ops:
  0.6 3.0 %collective-permute-start = (bf16[16,4096]{1,0:T(8,128)(2,1)}, bf16[16,4096]{1,0:T(8,128)(2,1)S(1)}, u32[]{:S(2)}, u32[]{:S(2)}) collective-permute-start(bf16[16,4096]{1,0:T(8,128)(2,1)} %bitcast.11), channel_id=1, source_target_pairs={{0,2},{1,3},{2,0},{3,1},{4,6},{5,7},{6,4},{7,5},{8,10},{9,11},{10,... | collective-permute-start | bytes 393224 | tf_op jit(solution)/shard_map/ppermute | solution.py:201
  4.3 2.5 %own_rows.1 = (bf16[16,4096]{1,0:T(8,128)(2,1)S(1)}, bf16[29,16,256]{2,1,0:T(8,128)(2,1)S(1)}, f32[16,4096]{1,0:T(8,128)S(1)}, bf16[24,128,256]{2,1,0:T(8,128)(2...) custom-call(s32[1,24]{1,0:T(1,128)} %position_in.1, s32[1,1]{1,0:T(1,128)S(6)} %copy.10.live_ref, ...), custom_call_target="tpu_custom_call" | custom-call | tf_op jit(solution)/shard_map/own_rows/pallas_call | solution.py:234
  6.8 0.5 %collective-permute-done.x_ref.refs_2_ = bf16[16,4096]{1,0:T(8,128)(2,1)S(1)} collective-permute-done((bf16[16,4096]{1,0:T(8,128)(2,1)}, bf16[16,4096]{1,0:T(8,128)(2,1)S(1)}, u32[]{:S(2)}, u32[]{:S(2)}) %collective-permute-start) | collective-permute-done | bytes 131104 | tf_op jit(solution)/shard_map/ppermute | solution.py:201
  7.3 1.0 %across_rows.1 = (bf16[29,16,256]{2,1,0:T(8,128)(2,1)S(1)}, f32[16,4096]{1,0:T(8,128)S(1)}) custom-call(s32[2,24]{1,0:T(2,128)S(1)} %get-tuple-element.25.table_ref, bf16[16,4096]{1,0:T(8,128)(2,1)S(1)} %collective-permute-done.x_ref.refs_2_, bf16[64,3584]{1,0:T(8,128)(2,1)S(1)} %get-tuple-element.27.grad_ref, ...), custom_call_target="tpu_custom_call" | custom-call | tf_op jit(solution)/shard_map/across_rows/pallas_call | solution.py:261
  8.4 0.3 collective-permute-done.1.x_ref.refs_3_
  8.7 1.0 %beyond_rows.1 = (bf16[29,16,256]{2,1,0:T(8,128)(2,1)S(1)}, bf16[16,4096]{1,0:T(8,128)(2,1)S(1)}) custom-call(s32[2,24]{1,0:T(2,128)S(1)} %get-tuple-element.25.table_ref, bf16[16,4096]{1,0:T(8,128)(2,1)S(1)} %collective-permute-done.1.x_ref.refs_3_, bf16[64,3584]{1,0:T(8,128)(2,1)S(1)} %get-tuple-element.27.grad_ref, ...), custom_call_target="tpu_custom_call" | custom-call | tf_op jit(solution)/shard_map/beyond_rows/pallas_call | solution.py:261
  9.7 0.3 collective-permute-start.2
  10.0 0.3 collective-permute-start.3
  10.3 0.8 %collective-permute-done.2 = bf16[16,4096]{1,0:T(8,128)(2,1)S(1)} collective-permute-done((bf16[16,4096]{1,0:T(8,128)(2,1)S(1)}, bf16[16,4096]{1,0:T(8,128)(2,1)S(1)}, u32[]{:S(2)}, u32[]{:S(2)}) %collective-permute-start.2) | collective-permute-done | bytes 131104 | tf_op jit(solution)/shard_map/ppermute | solution.py:201
  11.2 0.2 collective-permute-done.3.x_ref.refs_1_
  11.4 1.7 %collective-permute-start.5 = (bf16[16,4096]{1,0:T(8,128)(2,1)S(1)}, bf16[16,4096]{1,0:T(8,128)(2,1)S(1)}, u32[]{:S(2)}, u32[]{:S(2)}) collective-permute-start(bf16[16,4096]{1,0:T(8,128)(2,1)S(1)} %add_convert_fusion), channel_id=1, source_target_pairs={{0,2},{1,3},{2,0},{3,1},{4,6},{5,7},{6,4},{7,5},{8,10},{9,11},{10,... | collective-permute-start | bytes 393224 | tf_op jit(solution)/shard_map/ppermute | solution.py:201
  13.1 1.0 %beside_rows.1 = (bf16[29,16,256]{2,1,0:T(8,128)(2,1)S(1)}, bf16[16,4096]{1,0:T(8,128)(2,1)S(1)}) custom-call(s32[2,24]{1,0:T(2,128)S(1)} %get-tuple-element.25.table_ref, bf16[16,4096]{1,0:T(8,128)(2,1)S(1)} %collective-permute-done.3.x_ref.refs_1_, bf16[64,3584]{1,0:T(8,128)(2,1)S(1)} %get-tuple-element.27.grad_ref, ...), custom_call_target="tpu_custom_call" | custom-call | tf_op jit(solution)/shard_map/beside_rows/pallas_call | solution.py:261
  14.1 0.1 collective-permute-start.4
  14.2 2.8 %collective-permute-done.5 = bf16[16,4096]{1,0:T(8,128)(2,1)S(1)} collective-permute-done((bf16[16,4096]{1,0:T(8,128)(2,1)S(1)}, bf16[16,4096]{1,0:T(8,128)(2,1)S(1)}, u32[]{:S(2)}, u32[]{:S(2)}) %collective-permute-start.5) | collective-permute-done | bytes 131104 | tf_op jit(solution)/shard_map/ppermute | solution.py:201
  17.1 2.8 %collective-permute-start.8 = (bf16[16,4096]{1,0:T(8,128)(2,1)S(1)}, bf16[16,4096]{1,0:T(8,128)(2,1)S(1)}, u32[]{:S(2)}, u32[]{:S(2)}) collective-permute-start(bf16[16,4096]{1,0:T(8,128)(2,1)S(1)} %fusion.7), channel_id=1, source_target_pairs={{0,12},{4,8},{8,4},{12,0},{16,28},{20,24},{24,20},{28,16},{1,13},{... | collective-permute-start | bytes 393224 | tf_op jit(solution)/shard_map/ppermute | solution.py:201
  20.0 0.4 %collective-permute-start.7 = (bf16[16,4096]{1,0:T(8,128)(2,1)S(1)}, bf16[16,4096]{1,0:T(8,128)(2,1)S(1)}, u32[]{:S(2)}, u32[]{:S(2)}) collective-permute-start(bf16[16,4096]{1,0:T(8,128)(2,1)S(1)} %fusion.7), channel_id=1, source_target_pairs={{0,8},{4,12},{8,0},{12,4},{16,24},{20,28},{24,16},{28,20},{1,9},{5... | collective-permute-start | bytes 393224 | tf_op jit(solution)/shard_map/ppermute | solution.py:201
  20.4 0.3 collective-permute-start.6
  20.7 3.8 %collective-permute-done.8 = bf16[16,4096]{1,0:T(8,128)(2,1)S(1)} collective-permute-done((bf16[16,4096]{1,0:T(8,128)(2,1)S(1)}, bf16[16,4096]{1,0:T(8,128)(2,1)S(1)}, u32[]{:S(2)}, u32[]{:S(2)}) %collective-permute-start.8) | collective-permute-done | bytes 131104 | tf_op jit(solution)/shard_map/ppermute | solution.py:201
  24.5 1.6 %collective-permute-done.7 = bf16[16,4096]{1,0:T(8,128)(2,1)S(1)} collective-permute-done((bf16[16,4096]{1,0:T(8,128)(2,1)S(1)}, bf16[16,4096]{1,0:T(8,128)(2,1)S(1)}, u32[]{:S(2)}, u32[]{:S(2)}) %collective-permute-start.7) | collective-permute-done | bytes 131104 | tf_op jit(solution)/shard_map/ppermute | solution.py:201
  26.1 0.1 fusion.5
  26.2 3.7 %collective-permute-start.9 = (bf16[16,4096]{1,0:T(8,128)(2,1)S(1)}, bf16[16,4096]{1,0:T(8,128)(2,1)S(1)}, u32[]{:S(2)}, u32[]{:S(2)}) collective-permute-start(bf16[16,4096]{1,0:T(8,128)(2,1)S(1)} %fusion.5), channel_id=1, source_target_pairs={{0,24},{4,28},{8,16},{12,20},{16,8},{20,12},{24,0},{28,4},{1,25},{... | collective-permute-start | bytes 393224 | tf_op jit(solution)/shard_map/ppermute | solution.py:201
  29.9 2.0 %weight_grads.1 = (bf16[24,128,128]{2,1,0:T(8,128)(2,1)}, bf16[24,128,128]{2,1,0:T(8,128)(2,1)}) custom-call(s32[2,24]{1,0:T(2,128)S(1)} %get-tuple-element.25.table_ref, bf16[16,4096]{1,0:T(8,128)(2,1)S(1)} %get-tuple-element.33.refs_0_, bf16[16,4096]{1,0:T(8,128)(2,1)S(1)} %collective-permute-done.3.x_ref.refs_1_, ...), custom_call_target="tpu_custom_call" | custom-call | tf_op jit(solution)/shard_map/weight_grads/pallas_call | solution.py:301
  32.0 1.1 %collective-permute-done.9 = bf16[16,4096]{1,0:T(8,128)(2,1)S(1)} collective-permute-done((bf16[16,4096]{1,0:T(8,128)(2,1)S(1)}, bf16[16,4096]{1,0:T(8,128)(2,1)S(1)}, u32[]{:S(2)}, u32[]{:S(2)}) %collective-permute-start.9) | collective-permute-done | bytes 131104 | tf_op jit(solution)/shard_map/ppermute | solution.py:201
  33.1 0.8 %fusion.6 = bf16[1,16,4096]{2,1,0:T(8,128)(2,1)} fusion(bf16[16,4096]{1,0:T(8,128)(2,1)S(1)} %collective-permute-done.9, bf16[16,4096]{1,0:T(8,128)(2,1)S(1)} %collective-permute-done.8, bf16[16,4096]{1,0:T(8,128)(2,1)S(1)} %collective-permute-done.7, bf16[16,4096]{1,0:T(8,128)(2,1)S(1)} %collective-permute-done.6, bf16[16,4096]{1,0:T(8,128)(2,1)S(1)} %copy-done, ...), kind=kLoop, calls=%fused_computation.14 | loop fusion | flops 1245184 | bytes 1310724 | tf_op jit(solution)/shard_map/broadcast_in_dim | solution.py:332
  (7 shorter events, 0.1 us)
Async XLA Ops:
  0.6 6.7 %collective-permute-start = (bf16[16,4096]{1,0:T(8,128)(2,1)}, bf16[16,4096]{1,0:T(8,128)(2,1)S(1)}, u32[]{:S(2)}, u32[]{:S(2)}) collective-permute-start(bf16[16,4096]{1,0:T(8,128)(2,1)} %bitcast.11), channel_id=1, source_target_pairs={{0,2},{1,3},{2,0},{3,1},{4,6},{5,7},{6,4},{7,5},{8,10},{9,11},{10,... | collective-permute-start | bytes 393224 | tf_op jit(solution)/shard_map/ppermute | solution.py:201
  7.3 1.3 %collective-permute-start.1 = (bf16[16,4096]{1,0:T(8,128)(2,1)S(1)}, bf16[16,4096]{1,0:T(8,128)(2,1)S(1)}, u32[]{:S(2)}, u32[]{:S(2)}) collective-permute-start(bf16[16,4096]{1,0:T(8,128)(2,1)S(1)} %collective-permute-done.x_ref.refs_2_), channel_id=1, source_target_pairs={{0,1},{1,0},{2,3},{3,2},{4,5},{5,4},{6,7},{7,6},{8,9},{9,8},{10,11... | collective-permute-start | bytes 393224 | tf_op jit(solution)/shard_map/ppermute | solution.py:201
  9.7 1.4 %collective-permute-start.2 = (bf16[16,4096]{1,0:T(8,128)(2,1)S(1)}, bf16[16,4096]{1,0:T(8,128)(2,1)S(1)}, u32[]{:S(2)}, u32[]{:S(2)}) collective-permute-start(bf16[16,4096]{1,0:T(8,128)(2,1)S(1)} %get-tuple-element.32), channel_id=1, source_target_pairs={{0,1},{1,0},{2,3},{3,2},{4,5},{5,4},{6,7},{7,6},{8,9},{9,8},{10,11... | collective-permute-start | bytes 393224 | tf_op jit(solution)/shard_map/ppermute | solution.py:201
  10.0 1.3 %collective-permute-start.3 = (bf16[16,4096]{1,0:T(8,128)(2,1)S(1)}, bf16[16,4096]{1,0:T(8,128)(2,1)S(1)}, u32[]{:S(2)}, u32[]{:S(2)}) collective-permute-start(bf16[16,4096]{1,0:T(8,128)(2,1)S(1)} %get-tuple-element.33.refs_0_), channel_id=1, source_target_pairs={{0,1},{1,0},{2,3},{3,2},{4,5},{5,4},{6,7},{7,6},{8,9},{9,8},{10,11... | collective-permute-start | bytes 393224 | tf_op jit(solution)/shard_map/ppermute | solution.py:201
  11.4 5.7 %collective-permute-start.5 = (bf16[16,4096]{1,0:T(8,128)(2,1)S(1)}, bf16[16,4096]{1,0:T(8,128)(2,1)S(1)}, u32[]{:S(2)}, u32[]{:S(2)}) collective-permute-start(bf16[16,4096]{1,0:T(8,128)(2,1)S(1)} %add_convert_fusion), channel_id=1, source_target_pairs={{0,2},{1,3},{2,0},{3,1},{4,6},{5,7},{6,4},{7,5},{8,10},{9,11},{10,... | collective-permute-start | bytes 393224 | tf_op jit(solution)/shard_map/ppermute | solution.py:201
  14.1 18.9 %copy-start = (bf16[16,4096]{1,0:T(8,128)(2,1)S(1)}, bf16[16,4096]{1,0:T(8,128)(2,1)}, u32[]{:S(2)}) copy-start(bf16[16,4096]{1,0:T(8,128)(2,1)} %param.9) | copy-start | bytes 393220
  14.1 2.9 %collective-permute-start.4 = (bf16[16,4096]{1,0:T(8,128)(2,1)S(1)}, bf16[16,4096]{1,0:T(8,128)(2,1)S(1)}, u32[]{:S(2)}, u32[]{:S(2)}) collective-permute-start(bf16[16,4096]{1,0:T(8,128)(2,1)S(1)} %get-tuple-element.35), channel_id=1, source_target_pairs={{0,1},{1,0},{2,3},{3,2},{4,5},{5,4},{6,7},{7,6},{8,9},{9,8},{10,11... | collective-permute-start | bytes 393224 | tf_op jit(solution)/shard_map/ppermute | solution.py:201
  17.1 7.4 %collective-permute-start.8 = (bf16[16,4096]{1,0:T(8,128)(2,1)S(1)}, bf16[16,4096]{1,0:T(8,128)(2,1)S(1)}, u32[]{:S(2)}, u32[]{:S(2)}) collective-permute-start(bf16[16,4096]{1,0:T(8,128)(2,1)S(1)} %fusion.7), channel_id=1, source_target_pairs={{0,12},{4,8},{8,4},{12,0},{16,28},{20,24},{24,20},{28,16},{1,13},{... | collective-permute-start | bytes 393224 | tf_op jit(solution)/shard_map/ppermute | solution.py:201
  20.0 6.1 %collective-permute-start.7 = (bf16[16,4096]{1,0:T(8,128)(2,1)S(1)}, bf16[16,4096]{1,0:T(8,128)(2,1)S(1)}, u32[]{:S(2)}, u32[]{:S(2)}) collective-permute-start(bf16[16,4096]{1,0:T(8,128)(2,1)S(1)} %fusion.7), channel_id=1, source_target_pairs={{0,8},{4,12},{8,0},{12,4},{16,24},{20,28},{24,16},{28,20},{1,9},{5... | collective-permute-start | bytes 393224 | tf_op jit(solution)/shard_map/ppermute | solution.py:201
  20.4 5.7 %collective-permute-start.6 = (bf16[16,4096]{1,0:T(8,128)(2,1)S(1)}, bf16[16,4096]{1,0:T(8,128)(2,1)S(1)}, u32[]{:S(2)}, u32[]{:S(2)}) collective-permute-start(bf16[16,4096]{1,0:T(8,128)(2,1)S(1)} %fusion.7), channel_id=1, source_target_pairs={{0,4},{4,0},{8,12},{12,8},{16,20},{20,16},{24,28},{28,24},{1,5},{5... | collective-permute-start | bytes 393224 | tf_op jit(solution)/shard_map/ppermute | solution.py:201
  26.2 6.9 %collective-permute-start.9 = (bf16[16,4096]{1,0:T(8,128)(2,1)S(1)}, bf16[16,4096]{1,0:T(8,128)(2,1)S(1)}, u32[]{:S(2)}, u32[]{:S(2)}) collective-permute-start(bf16[16,4096]{1,0:T(8,128)(2,1)S(1)} %fusion.5), channel_id=1, source_target_pairs={{0,24},{4,28},{8,16},{12,20},{16,8},{20,12},{24,0},{28,4},{1,25},{... | collective-permute-start | bytes 393224 | tf_op jit(solution)/shard_map/ppermute | solution.py:201

commit v6 on v5

--- a/solution.py
+++ b/solution.py
@@ -272,13 +272,13 @@
         across, keep = lax.optimization_barrier((across, keep))
         beyond = _swap(across, "tp", 1)
         across_cot, far = others(2, across, F32, "across_rows")
-        beyond, far = lax.optimization_barrier((beyond, far))
+        beyond, far, beside = lax.optimization_barrier((beyond, far, beside))
         beyond_cot, far_send = others(3, beyond, BF16, "beyond_rows")
+        beside_cot, near_send = others(1, beside, BF16, "beside_rows")
         far_came = _swap(far_send, "tp", 1)
+        far_came, near_send = lax.optimization_barrier((far_came, near_send))
         far = (far + far_came.astype(F32)).astype(BF16)
-        far, beside = lax.optimization_barrier((far, beside))
         crossed = _swap(far, "tp", 2)
-        beside_cot, near_send = others(1, beside, BF16, "beside_rows")
         near_came = _swap(near_send, "tp", 1)
         own_term = keep + near_came.astype(F32) + crossed.astype(F32)
         x_parts = own_x, beside, across, beyond

time: 34.1 us -> 33.8 us (level)
  transfers between devices with their start and end apart: 10 -> 10, of which waited for: 8 -> 7; matrix products, arithmetic and copies ran while one was open for 0% -> 0% of each run, Pallas kernels for 20% -> 20%
where the time goes in v6:
time: 33.8 us; the launch traced here: 33.6 us
  starting transfers between devices  12.5 us (37%)
  waiting for transfers between devices  11.1 us (33%)
  Pallas kernels  7.67 us (23%)
  between operations  1.36 us (4%)
  other arithmetic  1 us (3%)
    ppermute x10, starting transfers between devices, _swap(): return lax.ppermute(array, axis, [(i, i ^ distance) for i in range(count)])  12.5 us
    ppermute x10, waiting for transfers between devices, _swap(): return lax.ppermute(array, axis, [(i, i ^ distance) for i in range(count)])  11.1 us
    pallas_call x3, Pallas kernels, others(): pl.pallas_call(functools.partial(_other_rows, blk, mask), out_shape=(cots...  3.09 us
    pallas_call x1, Pallas kernels, local(): pl.pallas_call(functools.partial(_own_rows, blk), out_shape=(struct((coun...  2.53 us
    pallas_call x1, Pallas kernels, local(): pl.pallas_call(functools.partial(_weight_grads, blk, len(x_parts)), out_s...  2.04 us
    broadcast_in_dim x1, other arithmetic, local(): return (result.astype(BF16)[None], gate_gradient[None], up_gradient[None])  0.83 us
  transfers between devices with their start and end apart: 10, of which 7 were waited for; matrix products, arithmetic and copies ran while one was open for 0% of the time, Pallas kernels for 20%

profile of v6, /device:TPU:0, one launch (start us, length us, event | category | flops | bytes accessed | tf_op | source)
XLA Modules:
  0.0 33.6 jit_solution(15201172767933388587)
XLA Ops:
  0.6 3.0 %collective-permute-start = (bf16[16,4096]{1,0:T(8,128)(2,1)}, bf16[16,4096]{1,0:T(8,128)(2,1)S(1)}, u32[]{:S(2)}, u32[]{:S(2)}) collective-permute-start(bf16[16,4096]{1,0:T(8,128)(2,1)} %bitcast.11), channel_id=1, source_target_pairs={{0,2},{1,3},{2,0},{3,1},{4,6},{5,7},{6,4},{7,5},{8,10},{9,11},{10,... | collective-permute-start | bytes 393224 | tf_op jit(solution)/shard_map/ppermute | solution.py:201
  4.3 2.5 %own_rows.1 = (bf16[16,4096]{1,0:T(8,128)(2,1)S(1)}, bf16[29,16,256]{2,1,0:T(8,128)(2,1)S(1)}, f32[16,4096]{1,0:T(8,128)S(1)}, bf16[24,128,256]{2,1,0:T(8,128)(2...) custom-call(s32[1,24]{1,0:T(1,128)} %position_in.1, s32[1,1]{1,0:T(1,128)S(6)} %copy.10.live_ref, ...), custom_call_target="tpu_custom_call" | custom-call | tf_op jit(solution)/shard_map/own_rows/pallas_call | solution.py:234
  6.8 0.1 collective-permute-start.2
  6.9 0.4 %collective-permute-done.x_ref.refs_2_ = bf16[16,4096]{1,0:T(8,128)(2,1)S(1)} collective-permute-done((bf16[16,4096]{1,0:T(8,128)(2,1)}, bf16[16,4096]{1,0:T(8,128)(2,1)S(1)}, u32[]{:S(2)}, u32[]{:S(2)}) %collective-permute-start) | collective-permute-done | bytes 131104 | tf_op jit(solution)/shard_map/ppermute | solution.py:201
  7.3 0.1 collective-permute-start.1
  7.4 1.0 %across_rows.1 = (bf16[29,16,256]{2,1,0:T(8,128)(2,1)S(1)}, f32[16,4096]{1,0:T(8,128)S(1)}) custom-call(s32[2,24]{1,0:T(2,128)S(1)} %get-tuple-element.26.table_ref, bf16[16,4096]{1,0:T(8,128)(2,1)S(1)} %collective-permute-done.x_ref.refs_2_, bf16[64,3584]{1,0:T(8,128)(2,1)S(1)} %get-tuple-element.28.grad_ref, ...), custom_call_target="tpu_custom_call" | custom-call | tf_op jit(solution)/shard_map/across_rows/pallas_call | solution.py:261
  8.5 0.2 collective-permute-done.1.x_ref.refs_3_
  8.7 1.0 %beyond_rows.1 = (bf16[29,16,256]{2,1,0:T(8,128)(2,1)S(1)}, bf16[16,4096]{1,0:T(8,128)(2,1)S(1)}) custom-call(s32[2,24]{1,0:T(2,128)S(1)} %get-tuple-element.26.table_ref, bf16[16,4096]{1,0:T(8,128)(2,1)S(1)} %collective-permute-done.1.x_ref.refs_3_, bf16[64,3584]{1,0:T(8,128)(2,1)S(1)} %get-tuple-element.28.grad_ref, ...), custom_call_target="tpu_custom_call" | custom-call | tf_op jit(solution)/shard_map/beyond_rows/pallas_call | solution.py:261
  9.7 0.3 collective-permute-start.3
  10.0 1.0 %beside_rows.1 = (bf16[29,16,256]{2,1,0:T(8,128)(2,1)S(1)}, bf16[16,4096]{1,0:T(8,128)(2,1)S(1)}) custom-call(s32[2,24]{1,0:T(2,128)S(1)} %get-tuple-element.26.table_ref, bf16[16,4096]{1,0:T(8,128)(2,1)S(1)} %collective-permute-done.2.x_ref.refs_1_, bf16[64,3584]{1,0:T(8,128)(2,1)S(1)} %get-tuple-element.28.grad_ref, ...), custom_call_target="tpu_custom_call" | custom-call | tf_op jit(solution)/shard_map/beside_rows/pallas_call | solution.py:261
  11.1 0.1 collective-permute-done.3
  11.2 1.8 %collective-permute-start.5 = (bf16[16,4096]{1,0:T(8,128)(2,1)S(1)}, bf16[16,4096]{1,0:T(8,128)(2,1)S(1)}, u32[]{:S(2)}, u32[]{:S(2)}) collective-permute-start(bf16[16,4096]{1,0:T(8,128)(2,1)S(1)} %add_convert_fusion), channel_id=1, source_target_pairs={{0,2},{1,3},{2,0},{3,1},{4,6},{5,7},{6,4},{7,5},{8,10},{9,11},{10,... | collective-permute-start | bytes 393224 | tf_op jit(solution)/shard_map/ppermute | solution.py:201
  13.0 3.9 %collective-permute-done.5 = bf16[16,4096]{1,0:T(8,128)(2,1)S(1)} collective-permute-done((bf16[16,4096]{1,0:T(8,128)(2,1)S(1)}, bf16[16,4096]{1,0:T(8,128)(2,1)S(1)}, u32[]{:S(2)}, u32[]{:S(2)}) %collective-permute-start.5) | collective-permute-done | bytes 131104 | tf_op jit(solution)/shard_map/ppermute | solution.py:201
  16.9 0.1 fusion.7
  16.9 2.9 %collective-permute-start.8 = (bf16[16,4096]{1,0:T(8,128)(2,1)S(1)}, bf16[16,4096]{1,0:T(8,128)(2,1)S(1)}, u32[]{:S(2)}, u32[]{:S(2)}) collective-permute-start(bf16[16,4096]{1,0:T(8,128)(2,1)S(1)} %fusion.7), channel_id=1, source_target_pairs={{0,12},{4,8},{8,4},{12,0},{16,28},{20,24},{24,20},{28,16},{1,13},{... | collective-permute-start | bytes 393224 | tf_op jit(solution)/shard_map/ppermute | solution.py:201
  19.8 0.4 %collective-permute-start.7 = (bf16[16,4096]{1,0:T(8,128)(2,1)S(1)}, bf16[16,4096]{1,0:T(8,128)(2,1)S(1)}, u32[]{:S(2)}, u32[]{:S(2)}) collective-permute-start(bf16[16,4096]{1,0:T(8,128)(2,1)S(1)} %fusion.7), channel_id=1, source_target_pairs={{0,8},{4,12},{8,0},{12,4},{16,24},{20,28},{24,16},{28,20},{1,9},{5... | collective-permute-start | bytes 393224 | tf_op jit(solution)/shard_map/ppermute | solution.py:201
  20.2 0.3 collective-permute-start.6
  20.5 3.9 %collective-permute-done.8 = bf16[16,4096]{1,0:T(8,128)(2,1)S(1)} collective-permute-done((bf16[16,4096]{1,0:T(8,128)(2,1)S(1)}, bf16[16,4096]{1,0:T(8,128)(2,1)S(1)}, u32[]{:S(2)}, u32[]{:S(2)}) %collective-permute-start.8) | collective-permute-done | bytes 131104 | tf_op jit(solution)/shard_map/ppermute | solution.py:201
  24.4 1.4 %collective-permute-done.7 = bf16[16,4096]{1,0:T(8,128)(2,1)S(1)} collective-permute-done((bf16[16,4096]{1,0:T(8,128)(2,1)S(1)}, bf16[16,4096]{1,0:T(8,128)(2,1)S(1)}, u32[]{:S(2)}, u32[]{:S(2)}) %collective-permute-start.7) | collective-permute-done | bytes 131104 | tf_op jit(solution)/shard_map/ppermute | solution.py:201
  25.8 0.1 fusion.5
  25.9 3.7 %collective-permute-start.9 = (bf16[16,4096]{1,0:T(8,128)(2,1)S(1)}, bf16[16,4096]{1,0:T(8,128)(2,1)S(1)}, u32[]{:S(2)}, u32[]{:S(2)}) collective-permute-start(bf16[16,4096]{1,0:T(8,128)(2,1)S(1)} %fusion.5), channel_id=1, source_target_pairs={{0,24},{4,28},{8,16},{12,20},{16,8},{20,12},{24,0},{28,4},{1,25},{... | collective-permute-start | bytes 393224 | tf_op jit(solution)/shard_map/ppermute | solution.py:201
  29.7 2.0 %weight_grads.1 = (bf16[24,128,128]{2,1,0:T(8,128)(2,1)}, bf16[24,128,128]{2,1,0:T(8,128)(2,1)}) custom-call(s32[2,24]{1,0:T(2,128)S(1)} %get-tuple-element.26.table_ref, bf16[16,4096]{1,0:T(8,128)(2,1)S(1)} %get-tuple-element.31.refs_0_, bf16[16,4096]{1,0:T(8,128)(2,1)S(1)} %collective-permute-done.2.x_ref.refs_1_, ...), custom_call_target="tpu_custom_call" | custom-call | tf_op jit(solution)/shard_map/weight_grads/pallas_call | solution.py:301
  31.7 1.1 %collective-permute-done.9 = bf16[16,4096]{1,0:T(8,128)(2,1)S(1)} collective-permute-done((bf16[16,4096]{1,0:T(8,128)(2,1)S(1)}, bf16[16,4096]{1,0:T(8,128)(2,1)S(1)}, u32[]{:S(2)}, u32[]{:S(2)}) %collective-permute-start.9) | collective-permute-done | bytes 131104 | tf_op jit(solution)/shard_map/ppermute | solution.py:201
  32.8 0.8 %fusion.6 = bf16[1,16,4096]{2,1,0:T(8,128)(2,1)} fusion(bf16[16,4096]{1,0:T(8,128)(2,1)S(1)} %collective-permute-done.9, bf16[16,4096]{1,0:T(8,128)(2,1)S(1)} %collective-permute-done.8, bf16[16,4096]{1,0:T(8,128)(2,1)S(1)} %collective-permute-done.7, bf16[16,4096]{1,0:T(8,128)(2,1)S(1)} %collective-permute-done.6, bf16[16,4096]{1,0:T(8,128)(2,1)S(1)} %copy-done, ...), kind=kLoop, calls=%fused_computation.14 | loop fusion | flops 1245184 | bytes 1310724 | tf_op jit(solution)/shard_map/broadcast_in_dim | solution.py:332
  (7 shorter events, 0.0 us)
Async XLA Ops:
  0.6 6.7 %collective-permute-start = (bf16[16,4096]{1,0:T(8,128)(2,1)}, bf16[16,4096]{1,0:T(8,128)(2,1)S(1)}, u32[]{:S(2)}, u32[]{:S(2)}) collective-permute-start(bf16[16,4096]{1,0:T(8,128)(2,1)} %bitcast.11), channel_id=1, source_target_pairs={{0,2},{1,3},{2,0},{3,1},{4,6},{5,7},{6,4},{7,5},{8,10},{9,11},{10,... | collective-permute-start | bytes 393224 | tf_op jit(solution)/shard_map/ppermute | solution.py:201
  6.8 1.6 %collective-permute-start.2 = (bf16[16,4096]{1,0:T(8,128)(2,1)S(1)}, bf16[16,4096]{1,0:T(8,128)(2,1)S(1)}, u32[]{:S(2)}, u32[]{:S(2)}) collective-permute-start(bf16[16,4096]{1,0:T(8,128)(2,1)S(1)} %get-tuple-element.31.refs_0_), channel_id=1, source_target_pairs={{0,1},{1,0},{2,3},{3,2},{4,5},{5,4},{6,7},{7,6},{8,9},{9,8},{10,11... | collective-permute-start | bytes 393224 | tf_op jit(solution)/shard_map/ppermute | solution.py:201
  7.3 1.3 %collective-permute-start.1 = (bf16[16,4096]{1,0:T(8,128)(2,1)S(1)}, bf16[16,4096]{1,0:T(8,128)(2,1)S(1)}, u32[]{:S(2)}, u32[]{:S(2)}) collective-permute-start(bf16[16,4096]{1,0:T(8,128)(2,1)S(1)} %collective-permute-done.x_ref.refs_2_), channel_id=1, source_target_pairs={{0,1},{1,0},{2,3},{3,2},{4,5},{5,4},{6,7},{7,6},{8,9},{9,8},{10,11... | collective-permute-start | bytes 393224 | tf_op jit(solution)/shard_map/ppermute | solution.py:201
  9.7 1.4 %collective-permute-start.3 = (bf16[16,4096]{1,0:T(8,128)(2,1)S(1)}, bf16[16,4096]{1,0:T(8,128)(2,1)S(1)}, u32[]{:S(2)}, u32[]{:S(2)}) collective-permute-start(bf16[16,4096]{1,0:T(8,128)(2,1)S(1)} %get-tuple-element.33), channel_id=1, source_target_pairs={{0,1},{1,0},{2,3},{3,2},{4,5},{5,4},{6,7},{7,6},{8,9},{9,8},{10,11... | collective-permute-start | bytes 393224 | tf_op jit(solution)/shard_map/ppermute | solution.py:201
  11.2 21.6 %copy-start = (bf16[16,4096]{1,0:T(8,128)(2,1)S(1)}, bf16[16,4096]{1,0:T(8,128)(2,1)}, u32[]{:S(2)}) copy-start(bf16[16,4096]{1,0:T(8,128)(2,1)} %param.9) | copy-start | bytes 393220
  11.2 5.7 %collective-permute-start.5 = (bf16[16,4096]{1,0:T(8,128)(2,1)S(1)}, bf16[16,4096]{1,0:T(8,128)(2,1)S(1)}, u32[]{:S(2)}, u32[]{:S(2)}) collective-permute-start(bf16[16,4096]{1,0:T(8,128)(2,1)S(1)} %add_convert_fusion), channel_id=1, source_target_pairs={{0,2},{1,3},{2,0},{3,1},{4,6},{5,7},{6,4},{7,5},{8,10},{9,11},{10,... | collective-permute-start | bytes 393224 | tf_op jit(solution)/shard_map/ppermute | solution.py:201
  13.0 3.9 %collective-permute-start.4 = (bf16[16,4096]{1,0:T(8,128)(2,1)S(1)}, bf16[16,4096]{1,0:T(8,128)(2,1)S(1)}, u32[]{:S(2)}, u32[]{:S(2)}) collective-permute-start(bf16[16,4096]{1,0:T(8,128)(2,1)S(1)} %get-tuple-element.36), channel_id=1, source_target_pairs={{0,1},{1,0},{2,3},{3,2},{4,5},{5,4},{6,7},{7,6},{8,9},{9,8},{10,11... | collective-permute-start | bytes 393224 | tf_op jit(solution)/shard_map/ppermute | solution.py:201
  16.9 7.4 %collective-permute-start.8 = (bf16[16,4096]{1,0:T(8,128)(2,1)S(1)}, bf16[16,4096]{1,0:T(8,128)(2,1)S(1)}, u32[]{:S(2)}, u32[]{:S(2)}) collective-permute-start(bf16[16,4096]{1,0:T(8,128)(2,1)S(1)} %fusion.7), channel_id=1, source_target_pairs={{0,12},{4,8},{8,4},{12,0},{16,28},{20,24},{24,20},{28,16},{1,13},{... | collective-permute-start | bytes 393224 | tf_op jit(solution)/shard_map/ppermute | solution.py:201
  19.8 6.0 %collective-permute-start.7 = (bf16[16,4096]{1,0:T(8,128)(2,1)S(1)}, bf16[16,4096]{1,0:T(8,128)(2,1)S(1)}, u32[]{:S(2)}, u32[]{:S(2)}) collective-permute-start(bf16[16,4096]{1,0:T(8,128)(2,1)S(1)} %fusion.7), channel_id=1, source_target_pairs={{0,8},{4,12},{8,0},{12,4},{16,24},{20,28},{24,16},{28,20},{1,9},{5... | collective-permute-start | bytes 393224 | tf_op jit(solution)/shard_map/ppermute | solution.py:201
  20.2 5.6 %collective-permute-start.6 = (bf16[16,4096]{1,0:T(8,128)(2,1)S(1)}, bf16[16,4096]{1,0:T(8,128)(2,1)S(1)}, u32[]{:S(2)}, u32[]{:S(2)}) collective-permute-start(bf16[16,4096]{1,0:T(8,128)(2,1)S(1)} %fusion.7), channel_id=1, source_target_pairs={{0,4},{4,0},{8,12},{12,8},{16,20},{20,16},{24,28},{28,24},{1,5},{5... | collective-permute-start | bytes 393224 | tf_op jit(solution)/shard_map/ppermute | solution.py:201
  25.9 6.9 %collective-permute-start.9 = (bf16[16,4096]{1,0:T(8,128)(2,1)S(1)}, bf16[16,4096]{1,0:T(8,128)(2,1)S(1)}, u32[]{:S(2)}, u32[]{:S(2)}) collective-permute-start(bf16[16,4096]{1,0:T(8,128)(2,1)S(1)} %fusion.5), channel_id=1, source_target_pairs={{0,24},{4,28},{8,16},{12,20},{16,8},{20,12},{24,0},{28,4},{1,25},{... | collective-permute-start | bytes 393224 | tf_op jit(solution)/shard_map/ppermute | solution.py:201

commit v7 on v6

v7 whole, which is shorter than its diff:
```python
import functools

import jax
import jax.numpy as jnp
from jax import lax
from jax.experimental import pallas as pl
from jax.experimental.pallas import tpu as pltpu
from jax.sharding import PartitionSpec as P

F32 = jnp.float32
BF16 = jnp.bfloat16


def _shift_and_factor(divisor, limit):
    for shift in range(31):
        factor = -(-(1 << shift) // divisor)
        if factor * limit < 1 << 31 and all(
            (p * factor) >> shift == p // divisor for p in range(limit)
        ):
            return factor, shift
    raise ValueError(divisor)


def _make_table(position, live, col_blocks, row_blocks, table_ref):
    factor, shift = _shift_and_factor(col_blocks, col_blocks * row_blocks)
    row = (position * factor) >> shift
    slot = lax.broadcasted_iota(jnp.int32, position.shape, 1)
    table_ref[0:1, :] = row
    table_ref[1:2, :] = jnp.where(slot < live, position - row * col_blocks, col_blocks)


def _read_table(table_ref):
    table = table_ref[...]
    return [(table[0, slot], table[1, slot]) for slot in range(table.shape[1])]


def _cotangents(blk, table, grad, weight, x_ref, cot_ref, act_ref):
    col_blocks = cot_ref.shape[0] - 1
    act_ref[...] = jnp.zeros_like(act_ref)
    for slot, (row, col) in enumerate(table):
        start = pl.multiple_of(row * blk, blk)
        act_ref[col] += jnp.dot(
            x_ref[:, pl.ds(start, blk)], weight(slot), preferred_element_type=F32
        )
    for col in range(col_blocks):
        gate = act_ref[col, :, :blk]
        up = act_ref[col, :, blk:]
        upstream = grad(col).astype(F32)
        sig = jax.nn.sigmoid(gate)
        scaled = upstream * sig
        cot_ref[col, :, :blk] = (scaled * up * (1.0 + gate * (1.0 - sig))).astype(BF16)
        cot_ref[col, :, blk:] = (scaled * gate).astype(BF16)
    cot_ref[col_blocks] = jnp.zeros_like(cot_ref[col_blocks])


def _add_back(table, weight, cot_ref, back_ref):
    for slot, (row, col) in enumerate(table):
        back_ref[row] += lax.dot_general(
            cot_ref[col], weight(slot), (((1,), (1,)), ((), ())), preferred_element_type=F32
        )


def _beside(gate_ref, up_ref):
    return lambda slot: jnp.concatenate([gate_ref[slot], up_ref[slot]], axis=1)


def _write_rows(back_ref, start, count, target):
    blk = back_ref.shape[2]
    for row in range(back_ref.shape[0]):
        target[:, row * blk : (row + 1) * blk] = back_ref[row, pl.ds(start, count), :].astype(
            target.dtype
        )


def _stage(
    col_blocks,
    row_blocks,
    position_in,
    live_ref,
    own_in,
    grad_in,
    wg_in,
    wu_in,
    x_ref,
    weight_ref,
    grad_ref,
    table_ref,
    position_ref,
    sems,
):
    blk = wg_in.shape[2]
    position = pltpu.make_async_copy(position_in, position_ref, sems.at[0])
    copies = [
        pltpu.make_async_copy(wg_in, weight_ref.at[:, :, pl.ds(0, blk)], sems.at[1]),
        pltpu.make_async_copy(wu_in, weight_ref.at[:, :, pl.ds(blk, blk)], sems.at[2]),
        pltpu.make_async_copy(grad_in, grad_ref, sems.at[3]),
        pltpu.make_async_copy(own_in, x_ref, sems.at[4]),
    ]
    for copy in (position, *copies):
        copy.start()
    position.wait()
    _make_table(position_ref[...], live_ref[0, 0], col_blocks, row_blocks, table_ref)
    for copy in copies:
        copy.wait()


def _grad_rows(grad_ref, mask, count, blk):
    start = pl.multiple_of((lax.axis_index("tp") ^ mask) * count, count)

    def grad(col):
        return grad_ref[pl.ds(start, count), col * blk : (col + 1) * blk]

    return grad


def _across_rows(
    blk, table_ref, x_ref, grad_ref, weight_ref, cot_ref, back_ref, act_ref
):
    back_ref[...] = jnp.zeros_like(back_ref)
    table = _read_table(table_ref)

    def weight(slot):
        return weight_ref[slot]

    grad = _grad_rows(grad_ref, 2, x_ref.shape[0], blk)
    _cotangents(blk, table, grad, weight, x_ref, cot_ref, act_ref)
    _add_back(table, weight, cot_ref, back_ref)


def _across_other(
    blk, table_ref, x_ref, grad_ref, wg_ref, wu_ref, in_ref, term_ref, cot_ref, act_ref, back_ref
):
    back_ref[...] = in_ref[...]
    count = x_ref.shape[0]
    table, weight = _read_table(table_ref), _beside(wg_ref, wu_ref)
    _cotangents(
        blk, table, _grad_rows(grad_ref, 2, count, blk), weight, x_ref, cot_ref, act_ref
    )
    _add_back(table, weight, cot_ref, back_ref)
    _write_rows(back_ref, 0, count, term_ref)


def _own_rows(
    blk,
    table_ref,
    x_ref,
    grad_ref,
    weight_ref,
    other_table_ref,
    other_grad_ref,
    other_wg_ref,
    other_wu_ref,
    cot_ref,
    term_ref,
    other_cot_ref,
    act_ref,
    other_act_ref,
    back_ref,
):
    count = x_ref.shape[0]
    back_ref[...] = jnp.zeros_like(back_ref)
    table, other_table = _read_table(table_ref), _read_table(other_table_ref)
    grad = _grad_rows(grad_ref, 0, count, blk)
    other_grad = _grad_rows(other_grad_ref, 0, count, blk)
    other_weight = _beside(other_wg_ref, other_wu_ref)

    def weight(slot):
        return weight_ref[slot]

    _cotangents(blk, table, grad, weight, x_ref, cot_ref, act_ref)
    _cotangents(blk, other_table, other_grad, other_weight, x_ref, other_cot_ref, other_act_ref)
    _add_back(table, weight, cot_ref, back_ref)
    _add_back(other_table, other_weight, other_cot_ref, back_ref)
    _write_rows(back_ref, 0, count, term_ref)


def _rest_rows(
    blk, table_ref, beside_ref, beyond_ref, grad_ref, weight_ref, cot_ref, far_cot_ref, act_ref
):
    count = beside_ref.shape[0]
    table = _read_table(table_ref)

    def weight(slot):
        return weight_ref[slot]

    for mask, x_ref, out_ref in ((1, beside_ref, cot_ref), (3, beyond_ref, far_cot_ref)):
        grad = _grad_rows(grad_ref, mask, count, blk)
        _cotangents(blk, table, grad, weight, x_ref, out_ref, act_ref)


def _whole(
    blk,
    position_ref,
    live_ref,
    x_ref,
    grad_ref,
    wg_ref,
    wu_ref,
    cot_ref,
    term_ref,
    table_ref,
    weight_ref,
    act_ref,
    back_ref,
):
    weight_ref[:, :, :blk] = wg_ref[...]
    weight_ref[:, :, blk:] = wu_ref[...]
    back_ref[...] = jnp.zeros_like(back_ref)
    _make_table(
        position_ref[...], live_ref[0, 0], cot_ref.shape[0] - 1, back_ref.shape[0], table_ref
    )
    table = _read_table(table_ref)

    def grad(col):
        return grad_ref[:, col * blk : (col + 1) * blk]

    def weight(slot):
        return weight_ref[slot]

    _cotangents(blk, table, grad, weight, x_ref, cot_ref, act_ref)
    _add_back(table, weight, cot_ref, back_ref)
    _write_rows(back_ref, 0, x_ref.shape[0], term_ref)


def _weight_grads(blk, halves, table_ref, *refs):
    x_refs, cot_refs, (gate_ref, up_ref) = refs[:halves], refs[halves : 2 * halves], refs[-2:]
    for slot, (row, col) in enumerate(_read_table(table_ref)):
        start = pl.multiple_of(row * blk, blk)
        grads = lax.dot_general(
            jnp.concatenate([x_ref[:, pl.ds(start, blk)] for x_ref in x_refs], axis=0),
            jnp.concatenate([cot_ref[col] for cot_ref in cot_refs], axis=0),
            (((0,), (0,)), ((), ())),
            preferred_element_type=F32,
        )
        gate_ref[slot] = grads[:, :blk].astype(BF16)
        up_ref[slot] = grads[:, blk:].astype(BF16)


_pinned = pltpu.with_memory_space_constraint


def _swap(array, axis, distance):
    count = lax.axis_size(axis)
    return lax.ppermute(array, axis, [(i, i ^ distance) for i in range(count)])


def _params(mib):
    return pltpu.CompilerParams(vmem_limit_bytes=mib << 20)


def local(inputs, hidden_grad, top_grad, w_gate, w_up, block_pos, live_count):
    own_rows = inputs[0]
    count, width = own_rows.shape
    slots, blk = w_gate.shape[1], w_gate.shape[2]
    hidden = hidden_grad.shape[2]
    col_blocks, row_blocks = hidden // blk, width // blk
    tp = lax.axis_size("tp")
    sections = lax.axis_size("section")
    section = lax.axis_index("section")

    vmem = pl.BlockSpec(memory_space=pltpu.VMEM)
    smem = pl.BlockSpec(memory_space=pltpu.SMEM)
    hbm = pl.BlockSpec(memory_space=pltpu.HBM)
    struct = jax.ShapeDtypeStruct

    def cots(rows):
        return struct((col_blocks + 1, rows, 2 * blk), BF16)

    def sums(rows):
        return [
            pltpu.VMEM((col_blocks + 1, rows, 2 * blk), F32),
            pltpu.VMEM((row_blocks, rows, blk), F32),
        ]

    if tp == 4:
        across = _swap(own_rows, "tp", 2)
        own_x, weights, grads, table = pl.pallas_call(
            functools.partial(_stage, col_blocks, row_blocks),
            out_shape=(
                struct((count, width), BF16),
                struct((slots, blk, 2 * blk), BF16),
                struct(hidden_grad.shape[1:], BF16),
                struct((2, slots), jnp.int32),
            ),
            in_specs=[hbm, smem, hbm, hbm, hbm, hbm],
            out_specs=[vmem] * 4,
            scratch_shapes=[
                pltpu.VMEM(block_pos.shape, jnp.int32),
                pltpu.SemaphoreType.DMA((5,)),
            ],
            compiler_params=_params(4),
            name="stage",
            cost_estimate=pl.CostEstimate(flops=1150000, transcendentals=0, bytes_accessed=0),
        )(
            _pinned(block_pos, pltpu.HBM),
            live_count,
            _pinned(own_rows, pltpu.HBM),
            *(_pinned(array[0], pltpu.HBM) for array in (hidden_grad, w_gate, w_up)),
        )
        other_wg, other_wu, other_grads, other_table = (
            _swap(array, "tp", 1) for array in (w_gate[0], w_up[0], hidden_grad[0], table)
        )
        across, own_x = lax.optimization_barrier((across, own_x))
        act, back = sums(count)
        across_cot, far = pl.pallas_call(
            functools.partial(_across_rows, blk),
            out_shape=(cots(count), struct((row_blocks, count, blk), F32)),
            in_specs=[vmem] * 4,
            out_specs=[vmem] * 2,
            scratch_shapes=[act],
            compiler_params=_params(4),
            name="across_rows",
            cost_estimate=pl.CostEstimate(flops=13800000000, transcendentals=0, bytes_accessed=0),
        )(table, across, grads, weights)
        other_wg, other_wu, other_grads, far = lax.optimization_barrier(
            (other_wg, other_wu, other_grads, far)
        )
        far = pl.pallas_call(
            functools.partial(_across_other, blk),
            out_shape=struct((count, width), BF16),
            in_specs=[vmem] * 6,
            out_specs=vmem,
            scratch_shapes=[pltpu.VMEM(cots(count).shape, BF16), act, back],
            compiler_params=_params(4),
            name="across_other",
        )(other_table, across, other_grads, other_wg, other_wu, far)
        far, own_late, across_late = lax.optimization_barrier((far, own_x, across))
        crossed = _swap(far, "tp", 2)
        own_cot, keep = pl.pallas_call(
            functools.partial(_own_rows, blk),
            out_shape=(cots(count), struct((count, width), F32)),
            in_specs=[vmem] * 8,
            out_specs=[vmem] * 2,
            scratch_shapes=[pltpu.VMEM(cots(count).shape, BF16), act, act, back],
            compiler_params=_params(4),
            name="own_rows",
        )(table, own_late, grads, weights, other_table, other_grads, other_wg, other_wu)
        beside = _swap(own_late, "tp", 1)
        beyond = _swap(across_late, "tp", 1)
        beside_cot, beyond_cot = pl.pallas_call(
            functools.partial(_rest_rows, blk),
            out_shape=(cots(count),) * 2,
            in_specs=[vmem] * 5,
            out_specs=[vmem] * 2,
            scratch_shapes=[act],
            compiler_params=_params(4),
            name="rest_rows",
        )(table, beside, beyond, grads, weights)
        own_term = keep + crossed.astype(F32)
        x_parts = own_late, beside, across_late, beyond
        cot_parts = own_cot, beside_cot, across_cot, beyond_cot
    else:
        rows = tp * count
        gathered = lax.all_gather(own_rows, "tp", axis=0, tiled=True)
        cot, term, table = pl.pallas_call(
            functools.partial(_whole, blk),
            out_shape=(cots(rows), struct((rows, width), BF16), struct((2, slots), jnp.int32)),
            in_specs=[vmem, smem] + [vmem] * 4,
            out_specs=[vmem] * 3,
            scratch_shapes=[pltpu.VMEM((slots, blk, 2 * blk), BF16), *sums(rows)],
            compiler_params=_params(24),
            name="whole",
        )(block_pos, live_count, gathered, hidden_grad[0], w_gate[0], w_up[0])
        own_term = lax.psum_scatter(term, "tp", scatter_dimension=0, tiled=True).astype(F32)
        x_parts, cot_parts = (gathered,), (cot,)

    total = own_term
    result = top_grad.astype(F32) + own_term
    if sections & (sections - 1) == 0:
        block = min(sections, 4)
        sent = own_term.astype(BF16)
        for step in range(1, block):
            other = _swap(sent, "section", step).astype(F32)
            result = result + jnp.where((section ^ step) > section, other, 0.0)
            total = total + other
        if tp == 4:
            total, *cot_parts = lax.optimization_barrier((total, *cot_parts))
        while block < sections:
            other = _swap(total.astype(BF16), "section", block ^ (block >> 1)).astype(F32)
            result = result + jnp.where(section & block == 0, other, 0.0)
            total = total + other
            block *= 2
    else:
        distance = 1
        while distance < sections:
            moves = [(i, i - distance) for i in range(distance, sections)]
            total = total + lax.ppermute(total.astype(BF16), "section", moves).astype(F32)
            distance *= 2
        result = top_grad.astype(F32) + total
    gate_gradient, up_gradient = pl.pallas_call(
        functools.partial(_weight_grads, blk, len(x_parts)),
        out_shape=(struct((slots, blk, blk), BF16),) * 2,
        in_specs=[vmem] * (1 + 2 * len(x_parts)),
        out_specs=[vmem, vmem],
        compiler_params=_params(4),
        name="weight_grads",
    )(table, *x_parts, *cot_parts)

    return (
        result.astype(BF16)[None],
        gate_gradient[None],
        up_gradient[None],
    )


def solution(mesh):
    in_specs = (
        P("section", "tp", None),
        P("section", None, "tp"),
        P("tp", None),
        P("section", "tp", None, None),
        P("section", "tp", None, None),
        P("section", "tp"),
        P("section", "tp"),
    )
    out_specs = (
        P("section", "tp", None),
        P("section", "tp", None, None),
        P("section", "tp", None, None),
    )
    return jax.shard_map(local, mesh=mesh, in_specs=in_specs, out_specs=out_specs, check_vma=False)
```

time: 33.8 us -> 30.8 us (0.911)
  waiting for transfers between devices: 11.1 us -> 6.67 us
  starting transfers between devices: 12.5 us -> 13.6 us
  Pallas kernels: 7.67 us -> 8.03 us
    ppermute x10 -> x12, waiting for transfers between devices: 11.1 us -> 6.67 us  [_swap(): return lax.ppermute(array, axis, [(i, i ^ distance) for i in range(count)])]
    ppermute x10 -> x12, starting transfers between devices: 12.5 us -> 13.6 us  [_swap(): return lax.ppermute(array, axis, [(i, i ^ distance) for i in range(count)])]
    pallas_call x4 -> x5, Pallas kernels: 5.63 us -> 5.98 us  [the longest x1 1.58 us: local(): pl.pallas_call(functools.partial(_stage, col_blocks, row_blocks), out_sha...]
  transfers between devices with their start and end apart: 10 -> 12, of which waited for: 7 -> 6; matrix products, arithmetic and copies ran while one was open for 0% -> 0% of each run, Pallas kernels for 20% -> 23%
where the time goes in v7:
time: 30.8 us; the launch traced here: 30.6 us
  starting transfers between devices  13.6 us (44%)
  Pallas kernels  8.03 us (26%)
  waiting for transfers between devices  6.67 us (22%)
  between operations  1.37 us (4%)
  other arithmetic  0.93 us (3%)
    ppermute x12, starting transfers between devices, _swap(): return lax.ppermute(array, axis, [(i, i ^ distance) for i in range(count)])  13.6 us
    ppermute x12, waiting for transfers between devices, _swap(): return lax.ppermute(array, axis, [(i, i ^ distance) for i in range(count)])  6.67 us
    pallas_call x1, Pallas kernels, local(): pl.pallas_call(functools.partial(_weight_grads, blk, len(x_parts)), out_s...  2.05 us
    pallas_call x1, Pallas kernels, local(): pl.pallas_call(functools.partial(_stage, col_blocks, row_blocks), out_sha...  1.58 us
    pallas_call x1, Pallas kernels, local(): pl.pallas_call(functools.partial(_own_rows, blk), out_shape=(cots(count),...  1.56 us
    pallas_call x1, Pallas kernels, local(): pl.pallas_call(functools.partial(_across_other, blk), out_shape=struct((c...  1.05 us
    pallas_call x1, Pallas kernels, local(): pl.pallas_call(functools.partial(_across_rows, blk), out_shape=(cots(coun...  1 us
    broadcast_in_dim x1, other arithmetic, local(): return (result.astype(BF16)[None], gate_gradient[None], up_gradient[None])  0.81 us
  transfers between devices with their start and end apart: 12, of which 6 were waited for; matrix products, arithmetic and copies ran while one was open for 0% of the time, Pallas kernels for 23%

profile of v7, /device:TPU:0, one launch (start us, length us, event | category | flops | bytes accessed | tf_op | source)
XLA Modules:
  0.0 30.6 jit_solution(8444005013619885531)
XLA Ops:
  0.6 3.0 %collective-permute-start.1 = (bf16[16,4096]{1,0:T(8,128)(2,1)}, bf16[16,4096]{1,0:T(8,128)(2,1)S(1)}, u32[]{:S(2)}, u32[]{:S(2)}) collective-permute-start(bf16[16,4096]{1,0:T(8,128)(2,1)} %bitcast.14), channel_id=1, source_target_pairs={{0,2},{1,3},{2,0},{3,1},{4,6},{5,7},{6,4},{7,5},{8,10},{9,11},{10,... | collective-permute-start | bytes 393224 | tf_op jit(solution)/shard_map/ppermute | solution.py:244
  3.6 0.5 %collective-permute-start.3 = (bf16[24,128,128]{2,1,0:T(8,128)(2,1)}, bf16[24,128,128]{2,1,0:T(8,128)(2,1)S(1)}, u32[]{:S(2)}, u32[]{:S(2)}) collective-permute-start(bf16[24,128,128]{2,1,0:T(8,128)(2,1)} %bitcast.10), channel_id=1, source_target_pairs={{0,1},{1,0},{2,3},{3,2},{4,5},{5,4},{6,7},{7,6},{8,9},{9,8},{10,11... | collective-permute-start | bytes 2359304 | tf_op jit(solution)/shard_map/ppermute | solution.py:244
  4.8 1.6 %stage.1 = (bf16[16,4096]{1,0:T(8,128)(2,1)S(1)}, bf16[24,128,256]{2,1,0:T(8,128)(2,1)S(1)}, bf16[64,3584]{1,0:T(8,128)(2,1)S(1)}, s32[2,24]{1,0:T(2,128)S(1)}) custom-call(s32[1,24]{1,0:T(1,128)} %position_in.1, s32[1,1]{1,0:T(1,128)S(6)} %copy.10.live_ref, bf16[16,4096]{1,0:T(8,128)(2,1)} %bitcast.15, bf16[64,3584]{1,0:T(8,128)(2,1)} %bitcast.13, ...), custom_call_target="tpu_custom_call" | custom-call | flops 1150000 | tf_op jit(solution)/shard_map/stage/pallas_call | solution.py:277
  6.4 0.6 %collective-permute-start = (s32[2,24]{1,0:T(2,128)S(1)}, s32[2,24]{1,0:T(2,128)S(1)}, u32[]{:S(2)}, u32[]{:S(2)}) collective-permute-start(s32[2,24]{1,0:T(2,128)S(1)} %get-tuple-element.29.table_ref), channel_id=1, source_target_pairs={{0,1},{1,0},{2,3},{3,2},{4,5},{5,4},{6,7},{7,6},{8,9},{9,8},{10,11... | collective-permute-start | bytes 584 | tf_op jit(solution)/shard_map/ppermute | solution.py:244
  7.0 0.4 %collective-permute-done.1.x_ref.refs_2_ = bf16[16,4096]{1,0:T(8,128)(2,1)S(1)} collective-permute-done((bf16[16,4096]{1,0:T(8,128)(2,1)}, bf16[16,4096]{1,0:T(8,128)(2,1)S(1)}, u32[]{:S(2)}, u32[]{:S(2)}) %collective-permute-start.1) | collective-permute-done | bytes 131104 | tf_op jit(solution)/shard_map/ppermute | solution.py:244
  7.3 1.0 %across_rows.1 = (bf16[29,16,256]{2,1,0:T(8,128)(2,1)S(1)}, f32[32,16,128]{2,1,0:T(8,128)S(1)}) custom-call(s32[2,24]{1,0:T(2,128)S(1)} %get-tuple-element.29.table_ref, bf16[16,4096]{1,0:T(8,128)(2,1)S(1)} %collective-permute-done.1.x_ref.refs_2_, bf16[64,3584]{1,0:T(8,128)(2,1)S(1)} %get-tuple-element.32.grad_ref, ...), custom_call_target="tpu_custom_call" | custom-call | flops 13799999488 | tf_op jit(solution)/shard_map/across_rows/pallas_call | solution.py:305
  8.3 0.0 collective-permute-done.2.wg_ref.other_wg_ref
  8.4 1.0 %across_other.1 = bf16[16,4096]{1,0:T(8,128)(2,1)S(1)} custom-call(s32[2,24]{1,0:T(2,128)S(1)} %collective-permute-done.table_ref.other_table_ref, bf16[16,4096]{1,0:T(8,128)(2,1)S(1)} %collective-permute-done.1.x_ref.refs_2_, bf16[64,3584]{1,0:T(8,128)(2,1)S(1)} %collective-permute-done.4.grad_ref.other_grad_ref, ...), custom_call_target="tpu_custom_call" | custom-call | tf_op jit(solution)/shard_map/across_other/pallas_call | solution.py:318
  9.4 1.8 %collective-permute-start.5 = (bf16[16,4096]{1,0:T(8,128)(2,1)S(1)}, bf16[16,4096]{1,0:T(8,128)(2,1)S(1)}, u32[]{:S(2)}, u32[]{:S(2)}) collective-permute-start(bf16[16,4096]{1,0:T(8,128)(2,1)S(1)} %across_other.1), channel_id=1, source_target_pairs={{0,2},{1,3},{2,0},{3,1},{4,6},{5,7},{6,4},{7,5},{8,10},{9,11},{10,... | collective-permute-start | bytes 393224 | tf_op jit(solution)/shard_map/ppermute | solution.py:244
  11.3 0.5 %collective-permute-start.10 = (bf16[16,4096]{1,0:T(8,128)(2,1)S(1)}, bf16[16,4096]{1,0:T(8,128)(2,1)S(1)}, u32[]{:S(2)}, u32[]{:S(2)}) collective-permute-start(bf16[16,4096]{1,0:T(8,128)(2,1)S(1)} %collective-permute-done.1.x_ref.refs_2_), channel_id=1, source_target_pairs={{0,1},{1,0},{2,3},{3,2},{4,5},{5,4},{6,7},{7,6},{8,9},{9,8},{10,11... | collective-permute-start | bytes 393224 | tf_op jit(solution)/shard_map/ppermute | solution.py:244
  11.8 1.6 %own_rows.1 = (bf16[29,16,256]{2,1,0:T(8,128)(2,1)S(1)}, f32[16,4096]{1,0:T(8,128)S(1)}) custom-call(s32[2,24]{1,0:T(2,128)S(1)} %get-tuple-element.29.table_ref, bf16[16,4096]{1,0:T(8,128)(2,1)S(1)} %get-tuple-element.40.x_ref.refs_0_, bf16[64,3584]{1,0:T(8,128)(2,1)S(1)} %get-tuple-element.32.grad_ref, ...), custom_call_target="tpu_custom_call" | custom-call | tf_op jit(solution)/shard_map/own_rows/pallas_call | solution.py:329
  13.3 1.3 %collective-permute-done.5 = bf16[16,4096]{1,0:T(8,128)(2,1)S(1)} collective-permute-done((bf16[16,4096]{1,0:T(8,128)(2,1)S(1)}, bf16[16,4096]{1,0:T(8,128)(2,1)S(1)}, u32[]{:S(2)}, u32[]{:S(2)}) %collective-permute-start.5) | collective-permute-done | bytes 131104 | tf_op jit(solution)/shard_map/ppermute | solution.py:244
  14.6 2.7 %collective-permute-start.8 = (bf16[16,4096]{1,0:T(8,128)(2,1)S(1)}, bf16[16,4096]{1,0:T(8,128)(2,1)S(1)}, u32[]{:S(2)}, u32[]{:S(2)}) collective-permute-start(bf16[16,4096]{1,0:T(8,128)(2,1)S(1)} %fusion.6), channel_id=1, source_target_pairs={{0,12},{4,8},{8,4},{12,0},{16,28},{20,24},{24,20},{28,16},{1,13},{... | collective-permute-start | bytes 393224 | tf_op jit(solution)/shard_map/ppermute | solution.py:244
  17.4 0.5 %collective-permute-start.7 = (bf16[16,4096]{1,0:T(8,128)(2,1)S(1)}, bf16[16,4096]{1,0:T(8,128)(2,1)S(1)}, u32[]{:S(2)}, u32[]{:S(2)}) collective-permute-start(bf16[16,4096]{1,0:T(8,128)(2,1)S(1)} %fusion.6), channel_id=1, source_target_pairs={{0,8},{4,12},{8,0},{12,4},{16,24},{20,28},{24,16},{28,20},{1,9},{5... | collective-permute-start | bytes 393224 | tf_op jit(solution)/shard_map/ppermute | solution.py:244
  17.8 0.4 %collective-permute-start.6 = (bf16[16,4096]{1,0:T(8,128)(2,1)S(1)}, bf16[16,4096]{1,0:T(8,128)(2,1)S(1)}, u32[]{:S(2)}, u32[]{:S(2)}) collective-permute-start(bf16[16,4096]{1,0:T(8,128)(2,1)S(1)} %fusion.6), channel_id=1, source_target_pairs={{0,4},{4,0},{8,12},{12,8},{16,20},{20,16},{24,28},{28,24},{1,5},{5... | collective-permute-start | bytes 393224 | tf_op jit(solution)/shard_map/ppermute | solution.py:244
  18.2 0.8 %rest_rows.1 = (bf16[29,16,256]{2,1,0:T(8,128)(2,1)S(1)}, bf16[29,16,256]{2,1,0:T(8,128)(2,1)S(1)}) custom-call(s32[2,24]{1,0:T(2,128)S(1)} %get-tuple-element.29.table_ref, bf16[16,4096]{1,0:T(8,128)(2,1)S(1)} %collective-permute-done.9.beside_ref.refs_1_, bf16[16,4096]{1,0:T(8,128)(2,1)S(1)} %collective-permute-done.10.beyond_ref.refs_3_, ...), custom_call_target="tpu_custom_call" | custom-call | tf_op jit(solution)/shard_map/rest_rows/pallas_call | solution.py:340
  19.0 2.2 %collective-permute-done.8 = bf16[16,4096]{1,0:T(8,128)(2,1)S(1)} collective-permute-done((bf16[16,4096]{1,0:T(8,128)(2,1)S(1)}, bf16[16,4096]{1,0:T(8,128)(2,1)S(1)}, u32[]{:S(2)}, u32[]{:S(2)}) %collective-permute-start.8) | collective-permute-done | bytes 131104 | tf_op jit(solution)/shard_map/ppermute | solution.py:244
  21.3 1.3 %collective-permute-done.7 = bf16[16,4096]{1,0:T(8,128)(2,1)S(1)} collective-permute-done((bf16[16,4096]{1,0:T(8,128)(2,1)S(1)}, bf16[16,4096]{1,0:T(8,128)(2,1)S(1)}, u32[]{:S(2)}, u32[]{:S(2)}) %collective-permute-start.7) | collective-permute-done | bytes 131104 | tf_op jit(solution)/shard_map/ppermute | solution.py:244
  22.6 0.2 collective-permute-done.6
  22.8 0.1 convert_add_fusion
  22.9 3.7 %collective-permute-start.11 = (bf16[16,4096]{1,0:T(8,128)(2,1)S(1)}, bf16[16,4096]{1,0:T(8,128)(2,1)S(1)}, u32[]{:S(2)}, u32[]{:S(2)}) collective-permute-start(bf16[16,4096]{1,0:T(8,128)(2,1)S(1)} %convert_add_fusion), channel_id=1, source_target_pairs={{0,24},{4,28},{8,16},{12,20},{16,8},{20,12},{24,0},{28,4},{1,25},{... | collective-permute-start | bytes 393224 | tf_op jit(solution)/shard_map/ppermute | solution.py:244
  26.5 2.1 %weight_grads.1 = (bf16[24,128,128]{2,1,0:T(8,128)(2,1)}, bf16[24,128,128]{2,1,0:T(8,128)(2,1)}) custom-call(s32[2,24]{1,0:T(2,128)S(1)} %get-tuple-element.29.table_ref, bf16[16,4096]{1,0:T(8,128)(2,1)S(1)} %get-tuple-element.40.x_ref.refs_0_, bf16[16,4096]{1,0:T(8,128)(2,1)S(1)} %collective-permute-done.9.beside_ref.refs_1_, ...), custom_call_target="tpu_custom_call" | custom-call | tf_op jit(solution)/shard_map/weight_grads/pallas_call | solution.py:390
  28.6 1.2 %collective-permute-done.11 = bf16[16,4096]{1,0:T(8,128)(2,1)S(1)} collective-permute-done((bf16[16,4096]{1,0:T(8,128)(2,1)S(1)}, bf16[16,4096]{1,0:T(8,128)(2,1)S(1)}, u32[]{:S(2)}, u32[]{:S(2)}) %collective-permute-start.11) | collective-permute-done | bytes 131104 | tf_op jit(solution)/shard_map/ppermute | solution.py:244
  29.8 0.8 %fusion.5 = bf16[1,16,4096]{2,1,0:T(8,128)(2,1)} fusion(bf16[16,4096]{1,0:T(8,128)(2,1)S(1)} %collective-permute-done.11, bf16[16,4096]{1,0:T(8,128)(2,1)S(1)} %collective-permute-done.8, bf16[16,4096]{1,0:T(8,128)(2,1)S(1)} %collective-permute-done.7, bf16[16,4096]{1,0:T(8,128)(2,1)S(1)} %collective-permute-done.6, bf16[16,4096]{1,0:T(8,128)(2,1)S(1)} %copy-done, ...), kind=kLoop, calls=%fused_computation.12 | loop fusion | flops 1114112 | bytes 1179652 | tf_op jit(solution)/shard_map/broadcast_in_dim | solution.py:400
  (11 shorter events, 0.1 us)
Async XLA Ops:
  0.6 6.7 %collective-permute-start.1 = (bf16[16,4096]{1,0:T(8,128)(2,1)}, bf16[16,4096]{1,0:T(8,128)(2,1)S(1)}, u32[]{:S(2)}, u32[]{:S(2)}) collective-permute-start(bf16[16,4096]{1,0:T(8,128)(2,1)} %bitcast.14), channel_id=1, source_target_pairs={{0,2},{1,3},{2,0},{3,1},{4,6},{5,7},{6,4},{7,5},{8,10},{9,11},{10,... | collective-permute-start | bytes 393224 | tf_op jit(solution)/shard_map/ppermute | solution.py:244
  3.6 4.7 %collective-permute-start.2 = (bf16[24,128,128]{2,1,0:T(8,128)(2,1)}, bf16[24,128,128]{2,1,0:T(8,128)(2,1)S(1)}, u32[]{:S(2)}, u32[]{:S(2)}) collective-permute-start(bf16[24,128,128]{2,1,0:T(8,128)(2,1)} %bitcast.8), channel_id=1, source_target_pairs={{0,1},{1,0},{2,3},{3,2},{4,5},{5,4},{6,7},{7,6},{8,9},{9,8},{10,11... | collective-permute-start | bytes 2359304 | tf_op jit(solution)/shard_map/ppermute | solution.py:244
  3.6 4.7 %collective-permute-start.3 = (bf16[24,128,128]{2,1,0:T(8,128)(2,1)}, bf16[24,128,128]{2,1,0:T(8,128)(2,1)S(1)}, u32[]{:S(2)}, u32[]{:S(2)}) collective-permute-start(bf16[24,128,128]{2,1,0:T(8,128)(2,1)} %bitcast.10), channel_id=1, source_target_pairs={{0,1},{1,0},{2,3},{3,2},{4,5},{5,4},{6,7},{7,6},{8,9},{9,8},{10,11... | collective-permute-start | bytes 2359304 | tf_op jit(solution)/shard_map/ppermute | solution.py:244
  4.1 4.2 %collective-permute-start.4 = (bf16[64,3584]{1,0:T(8,128)(2,1)}, bf16[64,3584]{1,0:T(8,128)(2,1)S(1)}, u32[]{:S(2)}, u32[]{:S(2)}) collective-permute-start(bf16[64,3584]{1,0:T(8,128)(2,1)} %bitcast.12), channel_id=1, source_target_pairs={{0,1},{1,0},{2,3},{3,2},{4,5},{5,4},{6,7},{7,6},{8,9},{9,8},{10,11... | collective-permute-start | bytes 1376264 | tf_op jit(solution)/shard_map/ppermute | solution.py:244
  6.4 2.0 %collective-permute-start = (s32[2,24]{1,0:T(2,128)S(1)}, s32[2,24]{1,0:T(2,128)S(1)}, u32[]{:S(2)}, u32[]{:S(2)}) collective-permute-start(s32[2,24]{1,0:T(2,128)S(1)} %get-tuple-element.29.table_ref), channel_id=1, source_target_pairs={{0,1},{1,0},{2,3},{3,2},{4,5},{5,4},{6,7},{7,6},{8,9},{9,8},{10,11... | collective-permute-start | bytes 584 | tf_op jit(solution)/shard_map/ppermute | solution.py:244
  9.4 5.2 %collective-permute-start.5 = (bf16[16,4096]{1,0:T(8,128)(2,1)S(1)}, bf16[16,4096]{1,0:T(8,128)(2,1)S(1)}, u32[]{:S(2)}, u32[]{:S(2)}) collective-permute-start(bf16[16,4096]{1,0:T(8,128)(2,1)S(1)} %across_other.1), channel_id=1, source_target_pairs={{0,2},{1,3},{2,0},{3,1},{4,6},{5,7},{6,4},{7,5},{8,10},{9,11},{10,... | collective-permute-start | bytes 393224 | tf_op jit(solution)/shard_map/ppermute | solution.py:244
  11.2 7.0 %collective-permute-start.9 = (bf16[16,4096]{1,0:T(8,128)(2,1)S(1)}, bf16[16,4096]{1,0:T(8,128)(2,1)S(1)}, u32[]{:S(2)}, u32[]{:S(2)}) collective-permute-start(bf16[16,4096]{1,0:T(8,128)(2,1)S(1)} %get-tuple-element.40.x_ref.refs_0_), channel_id=1, source_target_pairs={{0,1},{1,0},{2,3},{3,2},{4,5},{5,4},{6,7},{7,6},{8,9},{9,8},{10,11... | collective-permute-start | bytes 393224 | tf_op jit(solution)/shard_map/ppermute | solution.py:244
  11.3 7.0 %collective-permute-start.10 = (bf16[16,4096]{1,0:T(8,128)(2,1)S(1)}, bf16[16,4096]{1,0:T(8,128)(2,1)S(1)}, u32[]{:S(2)}, u32[]{:S(2)}) collective-permute-start(bf16[16,4096]{1,0:T(8,128)(2,1)S(1)} %collective-permute-done.1.x_ref.refs_2_), channel_id=1, source_target_pairs={{0,1},{1,0},{2,3},{3,2},{4,5},{5,4},{6,7},{7,6},{8,9},{9,8},{10,11... | collective-permute-start | bytes 393224 | tf_op jit(solution)/shard_map/ppermute | solution.py:244
  14.6 6.6 %collective-permute-start.8 = (bf16[16,4096]{1,0:T(8,128)(2,1)S(1)}, bf16[16,4096]{1,0:T(8,128)(2,1)S(1)}, u32[]{:S(2)}, u32[]{:S(2)}) collective-permute-start(bf16[16,4096]{1,0:T(8,128)(2,1)S(1)} %fusion.6), channel_id=1, source_target_pairs={{0,12},{4,8},{8,4},{12,0},{16,28},{20,24},{24,20},{28,16},{1,13},{... | collective-permute-start | bytes 393224 | tf_op jit(solution)/shard_map/ppermute | solution.py:244
  17.4 5.3 %collective-permute-start.7 = (bf16[16,4096]{1,0:T(8,128)(2,1)S(1)}, bf16[16,4096]{1,0:T(8,128)(2,1)S(1)}, u32[]{:S(2)}, u32[]{:S(2)}) collective-permute-start(bf16[16,4096]{1,0:T(8,128)(2,1)S(1)} %fusion.6), channel_id=1, source_target_pairs={{0,8},{4,12},{8,0},{12,4},{16,24},{20,28},{24,16},{28,20},{1,9},{5... | collective-permute-start | bytes 393224 | tf_op jit(solution)/shard_map/ppermute | solution.py:244
  17.8 5.0 %collective-permute-start.6 = (bf16[16,4096]{1,0:T(8,128)(2,1)S(1)}, bf16[16,4096]{1,0:T(8,128)(2,1)S(1)}, u32[]{:S(2)}, u32[]{:S(2)}) collective-permute-start(bf16[16,4096]{1,0:T(8,128)(2,1)S(1)} %fusion.6), channel_id=1, source_target_pairs={{0,4},{4,0},{8,12},{12,8},{16,20},{20,16},{24,28},{28,24},{1,5},{5... | collective-permute-start | bytes 393224 | tf_op jit(solution)/shard_map/ppermute | solution.py:244
  19.0 10.8 %copy-start = (bf16[16,4096]{1,0:T(8,128)(2,1)S(1)}, bf16[16,4096]{1,0:T(8,128)(2,1)}, u32[]{:S(2)}) copy-start(bf16[16,4096]{1,0:T(8,128)(2,1)} %param.9) | copy-start | bytes 393220
  22.9 6.9 %collective-permute-start.11 = (bf16[16,4096]{1,0:T(8,128)(2,1)S(1)}, bf16[16,4096]{1,0:T(8,128)(2,1)S(1)}, u32[]{:S(2)}, u32[]{:S(2)}) collective-permute-start(bf16[16,4096]{1,0:T(8,128)(2,1)S(1)} %convert_add_fusion), channel_id=1, source_target_pairs={{0,24},{4,28},{8,16},{12,20},{16,8},{20,12},{24,0},{28,4},{1,25},{... | collective-permute-start | bytes 393224 | tf_op jit(solution)/shard_map/ppermute | solution.py:244
